TPU v7x, 32 devices: a whole 2x2x4 slice. The times are simulated.
32 devices in a mesh: blen: 4 (over z), tm: 8 (over y, x, core).
Axes of the slice: x: 2, y: 2, z: 4, core: 2. Of those that a mesh axis runs over, the one named last changes fastest.
Arguments:
- model_grid: bfloat16 [256, 2, 512, 512], P(('blen', 'tm')), may hold values from -6 to 6
- vis_values: float32 [2, 16384], P(None, ('blen', 'tm')), may hold values from -6 to 6
- weights: float32 [16384], P(('blen', 'tm')), may hold values from 0.3 to 3
- flags: int32 [16384], P(('blen', 'tm')), may hold values 0 or 1
- uv_frac: float32 [2, 16384], P(None, ('blen', 'tm')), may hold values from 0 to 1
- cell_offset: int32 [2, 16384], P(None, ('blen', 'tm')), may hold values from 3 to 507
- tile_index: int32 [16384, 1], P(('blen', 'tm')), may hold values from 0 to 255; in each aligned block of 512 rows (0 to 511, 512 to 1023, ...) at most 4 rows name the same one
Outputs:
- gradient: float32 [8192, 8192], P(('blen', 'tm'))
- weighted_residual: float32 [2, 16384], P(None, ('blen', 'tm'))
Inputs may be any that keep to these rules, and one draw needn't show every extreme that they name: `tile_index`: in the rows of one device no tile is named by more than 4 rows, and some device has a tile named by exactly 4 rows.
All inputs are finite; a program needn't handle non-finite values. No bound on the sum of `flags` on one device may be relied on, other than what follows from the above.
Results may differ from a plain program's by a relative error of at most 0.0095.
Values sent between devices are 32-bit elements; how exact they have to be, the bound alone decides.
No kernel may reach another device: no remote copies, remote signals or barrier semaphores. Data moves between devices by JAX's collectives and lax.ppermute only.
A program may use at most 192 MiB of HBM per device.

v0:
```python
import math

import jax
import jax.numpy as jnp
from jax import lax
from jax.sharding import PartitionSpec as P

NPIX = 8192
KSUP = 8
NT = 16
MOST = 4


kernel_scale = 0.5
highest = lax.Precision.HIGHEST


def taps_full(offsets, fractions, tile_side):
    cell_ids = lax.broadcasted_iota(jnp.int32, offsets.shape + (tile_side,), offsets.ndim)
    shifted = cell_ids - offsets[..., None]
    distance = shifted.astype(jnp.float32) - fractions[..., None]
    inside = (shifted >= 1 - KSUP // 2) & (shifted <= KSUP // 2)
    values = jnp.exp(-kernel_scale * distance * distance)
    return jnp.where(inside, values, 0.0).astype(jnp.bfloat16)


def phase_table(row_count, col_count, period):
    row_ids = lax.broadcasted_iota(jnp.int32, (row_count, col_count), 0)
    col_ids = lax.broadcasted_iota(jnp.int32, (row_count, col_count), 1)
    angles = 2.0 * math.pi / period * (row_ids * col_ids % period).astype(jnp.float32)
    return (jnp.cos(angles), jnp.sin(angles))


def complex_block(cos_part, sin_part):
    return jnp.stack([jnp.stack([cos_part, -sin_part]), jnp.stack([sin_part, cos_part])])


def on_device(model_grid, vis_values, weights, flags, uv_frac, cell_offset, tile_index):
    blen_size = lax.axis_size("blen")
    tm_size = lax.axis_size("tm")
    devices = blen_size * tm_size
    per_dev = model_grid.shape[0]
    tile_side = model_grid.shape[2]
    vis_count = weights.shape[0]
    ntiles = per_dev * devices
    total_slots = ntiles * MOST
    tile_ids = tile_index[:, 0]
    matches = tile_ids[:, None] == lax.broadcasted_iota(jnp.int32, (vis_count, ntiles), 1)
    counts = jnp.sum(matches.astype(jnp.int32), axis=0)
    starts = jnp.cumsum(counts) - counts
    sorting = jnp.argsort(tile_ids, stable=True)
    position = (
        jnp.zeros((vis_count,), jnp.int32).at[sorting].set(jnp.arange(vis_count, dtype=jnp.int32))
    )
    first_slot = jnp.sum(jnp.where(matches, starts[None, :], 0), axis=1)
    rank_in_tile = position - first_slot
    owner_dev = tile_ids // per_dev
    local_tile = tile_ids % per_dev
    slot_of = (local_tile * devices + owner_dev) * MOST + rank_in_tile
    weighted = weights * flags.astype(jnp.float32)
    float_fields = jnp.stack([vis_values[0], vis_values[1], weighted, uv_frac[0], uv_frac[1]])
    send_float = jnp.zeros((5, total_slots), jnp.float32).at[:, slot_of].set(float_fields)
    send_int = jnp.zeros((2, total_slots), jnp.int32).at[:, slot_of].set(cell_offset)
    recv_float, recv_int = (
        lax.all_to_all(
            send_float.reshape(5, per_dev, devices, MOST),
            ("blen", "tm"),
            split_axis=2,
            concat_axis=2,
            tiled=True,
        ),
        lax.all_to_all(
            send_int.reshape(2, per_dev, devices, MOST),
            ("blen", "tm"),
            split_axis=2,
            concat_axis=2,
            tiled=True,
        ),
    )
    owner_rows = devices * MOST
    block_rows = 512 if owner_rows % 512 == 0 else owner_rows
    block_count = owner_rows // block_rows
    float_blocks = recv_float.reshape(5, per_dev, block_count, block_rows).transpose(2, 0, 1, 3)
    int_blocks = recv_int.reshape(2, per_dev, block_count, block_rows).transpose(2, 0, 1, 3)

    def grid_step(adjoint, inputs):
        part_float, part_int = inputs
        taps_u = taps_full(part_int[0], part_float[3], tile_side)
        taps_v = taps_full(part_int[1], part_float[4], tile_side)
        partial_sums = jnp.einsum(
            "qrj,qcji->qrci", taps_v, model_grid, preferred_element_type=jnp.float32
        )
        predicted = jnp.sum(partial_sums * taps_u[:, :, None, :], axis=-1)
        observed = jnp.stack([part_float[0], part_float[1]], axis=-1)
        residual = part_float[2][..., None] * (predicted - observed)
        spread = (residual[..., None] * taps_u[:, :, None, :]).astype(jnp.bfloat16)
        adjoint = adjoint + jnp.einsum(
            "qrj,qrci->qcji", taps_v, spread, preferred_element_type=jnp.float32
        )
        return (adjoint, jnp.moveaxis(residual, -1, 0))

    start_adjoint = jnp.zeros((per_dev, 2, tile_side, tile_side), jnp.float32)
    adjoint, residual_blocks = lax.scan(grid_step, start_adjoint, (float_blocks, int_blocks))
    residual_slots = residual_blocks.transpose(1, 2, 0, 3).reshape(2, per_dev, owner_rows)
    returned = lax.all_to_all(
        residual_slots.reshape(2, per_dev, devices, MOST),
        ("blen", "tm"),
        split_axis=2,
        concat_axis=2,
        tiled=True,
    )
    weighted_residual = returned.reshape(2, total_slots)[:, slot_of]
    relaid = lax.all_to_all(adjoint, "tm", split_axis=2, concat_axis=0, tiled=True)
    tile_cols = NT // blen_size
    col_slice = tile_side // tm_size
    pieces = relaid.reshape(NT, tile_cols, 2, col_slice, tile_side)
    cos_small, sin_small = phase_table(NT, NT, NT)
    small_turn = complex_block(cos_small, sin_small)
    cos_twist, sin_twist = phase_table(NT, tile_side, NPIX)
    cos_tile, sin_tile = phase_table(tile_side, tile_side, tile_side)
    tile_turn = complex_block(cos_tile, sin_tile)
    section_one = jnp.einsum("acnt,tvcji->anvji", small_turn, pieces, precision=highest)
    twist_c = cos_twist[:, None, None, :]
    twist_s = sin_twist[:, None, None, :]
    turned = jnp.stack(
        [
            section_one[0] * twist_c - section_one[1] * twist_s,
            section_one[0] * twist_s + section_one[1] * twist_c,
        ]
    )
    columns = jnp.einsum("acmi,cnvji->amnvj", tile_turn, turned, precision=highest)
    rows_dev = NPIX // devices
    spread_cols = rows_dev * tile_cols * col_slice
    packed = columns.reshape(2, 1, devices, spread_cols)
    landed = lax.all_to_all(packed, ("blen", "tm"), split_axis=2, concat_axis=1, tiled=True)
    landed = landed.reshape(2, blen_size, tm_size, rows_dev, tile_cols, col_slice)
    small_split = small_turn.reshape(2, 2, NT, blen_size, tile_cols)
    section_two = jnp.einsum("acnpv,cptrvj->antrj", small_split, landed, precision=highest)
    twist_cv = cos_twist.reshape(NT, tm_size, 1, col_slice)
    twist_sv = sin_twist.reshape(NT, tm_size, 1, col_slice)
    turned_rows = jnp.stack(
        [
            section_two[0] * twist_cv - section_two[1] * twist_sv,
            section_two[0] * twist_sv + section_two[1] * twist_cv,
        ]
    )
    real_turn = jnp.stack([cos_tile, -sin_tile]).reshape(2, tile_side, tm_size, col_slice)
    image_rows = jnp.einsum("cmtj,cntrj->rmn", real_turn, turned_rows, precision=highest)
    gradient = image_rows.reshape(rows_dev, NPIX) / NPIX
    return (gradient, weighted_residual)


def solution(mesh):
    in_specs = (
        P(("blen", "tm"), None, None, None),
        P(None, ("blen", "tm")),
        P(("blen", "tm")),
        P(("blen", "tm")),
        P(None, ("blen", "tm")),
        P(None, ("blen", "tm")),
        P(("blen", "tm"), None),
    )
    out_specs = (P(("blen", "tm"), None), P(None, ("blen", "tm")))
    return jax.shard_map(
        on_device, mesh=mesh, in_specs=in_specs, out_specs=out_specs, check_vma=False
    )
```

profile of v0, /device:TPU:0, one launch (start us, length us, event | category | flops | bytes accessed | tf_op | source)
XLA Modules:
  0.0 1047.1 jit_solution(14593329809357333968)
XLA Ops:
  0.6 0.8 convert_reduce_fusion
  1.5 0.3 reduce-window.9
  1.8 0.1 slice.64
  1.9 0.1 slice_reduce_fusion
  2.0 0.1 bitcast_subtract_fusion
  2.1 0.9 select_reduce_fusion
  3.0 4.4 sort.17
  7.5 0.8 copy.69
  8.3 2.4 scatter_custom_fusion
  10.7 0.7 compare_select_fusion
  11.4 1.8 scatter_custom_fusion.2
  13.3 1.5 copy.70
  14.8 7.3 all-to-all-start.1
  22.1 0.7 convert_multiply_fusion
  22.8 0.7 maximum_bitcast_fusion.12
  23.5 0.1 copy.66
  23.7 1.8 scatter_custom_fusion.1
  25.5 0.9 copy.67
  26.4 0.9 reshape.495
  27.3 3.0 all-to-all-done.1
  30.3 2.8 all-to-all-start
  33.3 7.1 all-to-all-done
  40.4 0.5 broadcast.622
  40.9 0.7 reduce.2
  41.7 0.2 reshape.496
  42.2 0.1 copy.76
  42.3 0.9 fusion.40
  43.2 5.3 multiply_reduce_fusion
  48.5 7.2 convolution_bitcast_fusion
  55.7 25.1 %copy.78 = f32[8,2,512,512]{3,1,0,2:T(2,128)} copy(f32[8,2,512,512]{2,3,1,0:T(8,128)} %convolution_bitcast_fusion) | data formatting | bytes 33554432 | tf_op jit(solution)/shard_map/while/body/eval_jaxpr/qrj,qrci->qcji/transpose | solution.py:97
  80.8 6.0 all-to-all-start.2
  87.0 0.1 fusion.87
  87.2 3.9 fusion.60
  91.0 4.1 fusion.58
  95.1 1.9 maximum_bitcast_fusion.2
  97.0 0.1 copy.89
  97.2 0.7 copy.90
  97.8 173.0 %all-to-all-done.2 = f32[8,2,512,512]{3,1,0,2:T(2,128)} async-done(((f32[8,2,512,512]{3,1,0,2:T(2,128)}), f32[8,2,512,512]{3,1,0,2:T(2,128)}, u32[]{:S(2)}, u32[]{:S(2)}) %all-to-all-start.2) | async-done | bytes 16777248 | tf_op jit(solution)/shard_map/all_to_all | solution.py:113
  270.8 2.6 all-to-all-start.4
  273.4 11.0 %copy.79 = f32[8,2,512,512]{3,2,1,0:T(8,128)S(1)} copy(f32[8,2,512,512]{3,1,0,2:T(2,128)} %all-to-all-done.2) | data formatting | bytes 33554432 | tf_op jit(solution)/shard_map/all_to_all | solution.py:113
  284.4 6.7 copy.80
  291.1 42.0 %fusion.11 = f32[2,16,4,64,512]{4,1,3,2,0:T(8,128)} fusion(f32[16,4,2,64,512]{4,3,2,1,0:T(8,128)} %bitcast.109, f32[1,2,16,16]{3,2,1,0:T(8,128)S(1)} %get-tuple-element.44, f32[1,2,16,16]{3,2,1,0:T(8,128)S(1)} %get-tuple-element.43), kind=kOutput, calls=%fused_computation.23 | convolution fusion | flops 1610613760 | bytes 33558528 | tf_op jit(solution)/shard_map/acnt,tvcji->anvji/dot_general | solution.py:122
  333.1 7.1 multiply_subtract_fusion.1
  340.2 6.4 pad_maximum_fusion
  346.6 67.2 %fusion.14 = f32[2,512,16,4,64]{1,4,3,2,0:T(8,128)} fusion(f32[2,16,4,64,512]{4,1,3,2,0:T(8,128)} %pad_maximum_fusion, f32[1,2,512,512]{3,2,1,0:T(8,128)S(1)} %copy-done, f32[1,2,512,512]{3,2,1,0:T(8,128)S(1)} %get-tuple-element.34), kind=kOutput, calls=%fused_computation.24 | convolution fusion | flops 51540656128 | bytes 37748736 | tf_op jit(solution)/shard_map/acmi,cnvji->amnvj/dot_general | solution.py:131
  413.8 31.1 %copy.83 = f32[2,512,16,4,64]{4,3,2,1,0:T(4,128)} copy(f32[2,512,16,4,64]{1,4,3,2,0:T(8,128)} %fusion.14) | data formatting | bytes 33554432 | tf_op jit(solution)/shard_map/acmi,cnvji->amnvj/dot_general | solution.py:131
  444.9 27.4 %reshape.436 = f32[2,1,32,65536]{3,2,0,1:T(8,128)} reshape(f32[2,512,16,4,64]{4,3,2,1,0:T(4,128)} %copy.83) | data formatting | bytes 33554432 | tf_op jit(solution)/shard_map/reshape | solution.py:134
  472.2 28.6 %copy.84 = f32[2,1,32,65536]{3,0,1,2:T(2,128)} copy(f32[2,1,32,65536]{3,2,0,1:T(8,128)} %reshape.436) | data formatting | bytes 33554432 | tf_op jit(solution)/shard_map/reshape | solution.py:134
  500.9 6.0 all-to-all-start.3
  506.9 0.2 fusion.110
  507.1 4.2 sine_negate_fusion
  511.2 1.1 fusion.72
  512.3 0.9 copy.91
  513.2 1.6 gather_fusion
  514.9 1.7 copy.93
  516.5 363.0 %all-to-all-done.3 = f32[2,1,32,65536]{3,0,1,2:T(2,128)} async-done(((f32[2,1,32,65536]{3,0,1,2:T(2,128)}), f32[2,1,32,65536]{3,0,1,2:T(2,128)}, u32[]{:S(2)}, u32[]{:S(2)}) %all-to-all-start.3) | async-done | bytes 16777248 | tf_op jit(solution)/shard_map/all_to_all | solution.py:135
  879.5 38.4 %reshape.487 = f32[2,4,8,256,4,64]{5,4,3,0,2,1:T(4,128)} reshape(f32[2,1,32,65536]{3,0,1,2:T(2,128)} %all-to-all-done.3) | data formatting | bytes 33554432 | tf_op jit(solution)/shard_map/reshape | solution.py:136
  918.0 30.9 %copy.86 = f32[2,4,8,256,4,64]{3,4,1,0,5,2:T(4,128)} copy(f32[2,4,8,256,4,64]{5,4,3,0,2,1:T(4,128)} %reshape.487) | data formatting | bytes 33554432 | tf_op jit(solution)/shard_map/reshape | solution.py:136
  948.8 31.8 %fusion.17 = f32[2,16,8,256,64]{3,1,4,2,0:T(8,128)S(1)} fusion(f32[2,4,8,256,4,64]{3,4,1,0,5,2:T(4,128)} %copy.86, f32[2,2,16,4,4,1,1]{2,4,3,1,6,5,0:T(4,128)S(1)} %maximum_bitcast_fusion.17), kind=kOutput, calls=%fused_computation.25 | convolution fusion | flops 1610612736 | bytes 33558528 | tf_op jit(solution)/shard_map/acnpv,cptrvj->antrj/dot_general | solution.py:138
  980.6 2.8 multiply_subtract_fusion
  983.4 1.8 pad_maximum_fusion.1
  985.2 42.3 %fusion.10 = f32[256,512,16]{1,0,2:T(8,128)} fusion(f32[2,16,8,256,64]{3,1,4,2,0:T(8,128)S(1)} %pad_maximum_fusion.1, f32[1,512,8,64]{1,3,2,0:T(8,128)S(1)} %get-tuple-element.56, f32[1,512,8,64]{1,3,2,0:T(8,128)S(1)} %get-tuple-element.57), kind=kOutput, calls=%fused_computation.18 | convolution fusion | flops 25772425216 | bytes 27262976 | tf_op jit(solution)/shard_map/cmtj,cntrj->rmn/dot_general | solution.py:148
  1027.6 10.3 copy.88
  1037.9 8.9 copy.92
  (28 shorter events, 0.7 us)
Async XLA Ops:
  11.4 14.1 %copy-start.1 = (s32[512]{0:T(512)}, s32[512]{0:T(512)S(1)}, u32[]{:S(2)}) copy-start(s32[512]{0:T(512)S(1)} %compare_select_fusion) | copy-start | bytes 6148
  14.8 15.5 %all-to-all-start.1 = ((s32[2,8,32,4]{1,3,0,2:T(4,128)}), s32[2,8,32,4]{1,3,0,2:T(4,128)S(1)}, u32[]{:S(2)}, u32[]{:S(2)}) async-start(s32[2,8,32,4]{1,3,0,2:T(4,128)} %copy.70), calls=%async_computation.1 | async-start | bytes 262144 | tf_op jit(solution)/shard_map/all_to_all | solution.py:72
  30.3 10.1 all-to-all-start
  80.8 190.0 %all-to-all-start.2 = ((f32[8,2,512,512]{3,1,0,2:T(2,128)}), f32[8,2,512,512]{3,1,0,2:T(2,128)}, u32[]{:S(2)}, u32[]{:S(2)}) async-start(f32[8,2,512,512]{3,1,0,2:T(2,128)} %copy.78), calls=%async_computation.2 | async-start | bytes 33554432 | tf_op jit(solution)/shard_map/all_to_all | solution.py:113
  270.8 230.0 %all-to-all-start.4 = ((f32[2,8,32,4]{1,3,0,2:T(4,128)}), f32[2,8,32,4]{1,3,0,2:T(4,128)S(1)}, u32[]{:S(2)}, u32[]{:S(2)}) async-start(f32[2,8,32,4]{1,3,0,2:T(4,128)} %copy.90), calls=%async_computation.4 | async-start | bytes 262144 | tf_op jit(solution)/shard_map/all_to_all | solution.py:105
  340.2 6.4 copy-start
  500.9 6.0 copy-start.2
  500.9 378.7 %all-to-all-start.3 = ((f32[2,1,32,65536]{3,0,1,2:T(2,128)}), f32[2,1,32,65536]{3,0,1,2:T(2,128)}, u32[]{:S(2)}, u32[]{:S(2)}) async-start(f32[2,1,32,65536]{3,0,1,2:T(2,128)} %copy.84), calls=%async_computation.3 | async-start | bytes 33554432 | tf_op jit(solution)/shard_map/all_to_all | solution.py:135
where the time goes:
time: 1060 us; the launch traced here: 1050 us
  waiting for transfers between devices  546 us (52%)
  local copies, waits for them, and re-layouts  235 us (22%)
  matrix products  196 us (18%)
  other arithmetic  44 us (4%)
  starting transfers between devices  24.7 us (2%)
    all_to_all x1, waiting for transfers between devices, on_device(): lax.all_to_all(packed, ('blen', 'tm'), split_axis=2, concat_axis=1, tiled...  363 us
    all_to_all x1, waiting for transfers between devices, on_device(): lax.all_to_all(adjoint, 'tm', split_axis=2, concat_axis=0, tiled=True)  173 us
    reshape x2, local copies, waits for them, and re-layouts, on_device(): landed.reshape(2, blen_size, tm_size, rows_dev, tile_cols, col_slice)  69.3 us
    dot_general x1, matrix products, on_device(): jnp.einsum('acmi,cnvji->amnvj', tile_turn, turned, precision=highest)  67.2 us
    reshape x2, local copies, waits for them, and re-layouts, on_device(): packed = columns.reshape(2, 1, devices, spread_cols)  56 us
    dot_general x1, matrix products, on_device(): jnp.einsum('cmtj,cntrj->rmn', real_turn, turned_rows, precision=highest)  42.3 us
    dot_general x1, matrix products, on_device(): jnp.einsum('acnt,tvcji->anvji', small_turn, pieces, precision=highest)  42 us
    dot_general x1, matrix products, on_device(): jnp.einsum('acnpv,cptrvj->antrj', small_split, landed, precision=highest)  31.8 us
  transfers between devices with their start and end apart: 5, of which 4 were waited for; matrix products, arithmetic and copies ran while one was open for 24% of the time, Pallas kernels for 0%

commit v1 on v0

v1 whole, which is shorter than its diff:
```python
import math

import jax
import jax.numpy as jnp
from jax import lax
from jax.experimental import pallas as pl
from jax.experimental.pallas import tpu as pltpu
from jax.sharding import PartitionSpec as P

NPIX = 8192
KSUP = 8
NT = 16
TVG = 4
MOST = 4
FIELDS = 8
KEPT = 4

AXES = ("blen", "tm")
f32 = jnp.float32
bf16 = jnp.bfloat16
i32 = jnp.int32
NT_DIMS = (((1,), (1,)), ((), ()))
NN_DIMS = (((1,), (0,)), ((), ()))
MIB = 1 << 20


def params(mib):
    return pltpu.CompilerParams(vmem_limit_bytes=mib * MIB)


def split3(x):
    hi = x.astype(bf16)
    rest = x - hi.astype(f32)
    mid = rest.astype(bf16)
    low = (rest - mid.astype(f32)).astype(bf16)
    return hi, mid, low


def tap_block(cells_i, cells_f, offset_row, frac_row):
    first = offset_row.astype(i32) - (KSUP // 2 - 1)
    steps = cells_i - first
    dist = (cells_f - offset_row) - frac_row
    value = jnp.exp(-0.5 * dist * dist)
    inside = (steps >= 0) & (steps < KSUP)
    return jnp.where(inside, value, 0.0).astype(bf16)


def pack_body(tile_col, tile_row, fields, packed, slots, *, devices, per_dev):
    n = tile_row.shape[1]
    t_row = tile_row[...]
    earlier = lax.broadcasted_iota(i32, (n, n), 0) < lax.broadcasted_iota(i32, (n, n), 1)
    same = (tile_col[...] == t_row) & earlier
    rank = jnp.sum(same.astype(f32), axis=0, keepdims=True).astype(i32)
    owner = t_row // per_dev
    local = t_row - owner * per_dev
    slots[...] = rank
    owners = lax.broadcasted_iota(i32, (devices, n), 0) == owner
    places = MOST * per_dev
    hot = (lax.broadcasted_iota(i32, (places, n), 0) == rank * per_dev + local)
    hot = hot.astype(f32).astype(bf16)
    packed[...] = jnp.zeros(packed.shape, f32)
    for f in range(FIELDS - 1):
        spread = jnp.where(owners, fields[f : f + 1, :], 0.0)
        total = jnp.zeros((devices, places), f32)
        for part in split3(spread):
            total = total + lax.dot_general(part, hot, NT_DIMS, preferred_element_type=f32)
        for k in range(MOST):
            at = (k * FIELDS + f) * per_dev
            packed[:, at : at + per_dev] = total[:, k * per_dev : (k + 1) * per_dev]


def unpack_body(recv, pos, rest, *, devices, per_dev):
    turned = recv[...].T
    span = FIELDS * per_dev
    rows = jnp.concatenate([turned[k * span : (k + 1) * span, :] for k in range(MOST)], axis=1)
    for l in range(per_dev):
        for f in range(KEPT):
            pos[l, f : f + 1, :] = rows[f * per_dev + l : f * per_dev + l + 1, :]
            g = f + KEPT
            rest[l, f : f + 1, :] = rows[g * per_dev + l : g * per_dev + l + 1, :]


def predict_body(model, pos, rest, res):
    side = model.shape[2]
    lanes = pos.shape[2]
    cells_i = lax.broadcasted_iota(i32, (side, lanes), 0)
    cells_f = cells_i.astype(f32)
    ku = tap_block(cells_i, cells_f, pos[0, 0:1, :], pos[0, 2:3, :])
    kv = tap_block(cells_i, cells_f, pos[0, 1:2, :], pos[0, 3:4, :]).astype(f32)
    for c in range(2):
        rows = lax.dot_general(model[0, c], ku, NN_DIMS, preferred_element_type=f32)
        predicted = jnp.sum(rows * kv, axis=0, keepdims=True)
        res[0, c : c + 1, :] = rest[0, 2:3, :] * (predicted - rest[0, c : c + 1, :])


def columns_body(pos, res, turn_u, rot, out, kv_all, up_all, *, lanes):
    side = turn_u.shape[1]
    rows2 = turn_u.shape[0]
    rows = rows2 // 2
    short = side // NT
    cells_i = lax.broadcasted_iota(i32, (side, lanes), 0)
    cells_f = cells_i.astype(f32)
    perm_i = (cells_i % short) * NT + cells_i // short
    perm_f = perm_i.astype(f32)

    def step(tu, carry):
        at = pl.multiple_of(tu * lanes, lanes)
        p = pos[0, tu, 0]
        r = res[0, tu, 0]
        ku = tap_block(cells_i, cells_f, p[0:1], p[2:3])
        kv_all[:, pl.ds(at, lanes)] = tap_block(perm_i, perm_f, p[1:2], p[3:4])
        v = lax.dot_general(turn_u[...], ku, NN_DIMS, preferred_element_type=f32)
        r_re = r[0:1] * (1.0 / NPIX)
        r_im = r[1:2] * (1.0 / NPIX)
        cos_t = rot[0, :, pl.ds(at, lanes)]
        sin_t = rot[1, :, pl.ds(at, lanes)]
        c_re = (r_re * cos_t - r_im * sin_t)[None]
        c_im = (r_re * sin_t + r_im * cos_t)[None]
        v_re = v[:rows].reshape(rows // NT, NT, lanes)
        v_im = v[rows:].reshape(rows // NT, NT, lanes)
        u_re = (c_re * v_re - c_im * v_im).reshape(rows, lanes)
        u_im = (c_re * v_im + c_im * v_re).reshape(rows, lanes)
        up_all[0:rows, pl.ds(at, lanes)] = u_re.astype(bf16)
        up_all[rows:rows2, pl.ds(at, lanes)] = u_im.astype(bf16)
        return carry

    lax.fori_loop(0, NT, step, 0)
    ft = lax.dot_general(kv_all[...], up_all[...], NT_DIMS, preferred_element_type=f32)
    out[...] = ft.astype(bf16).reshape(NT, short, rows2)


def fft_pos(z, real_only=False):
    n = len(z)
    if n == 1:
        return z
    even = fft_pos(z[0::2])
    odd = fft_pos(z[1::2])
    low, high = [], []
    for k in range(n // 2):
        o_re, o_im = odd[k]
        if k == 0:
            t_re, t_im = o_re, o_im
        elif 4 * k == n:
            t_re, t_im = -o_im, o_re
        else:
            c, s = math.cos(2 * math.pi * k / n), math.sin(2 * math.pi * k / n)
            t_re = o_re * c - o_im * s
            t_im = None if real_only else o_re * s + o_im * c
        e_re, e_im = even[k]
        if real_only:
            low.append(e_re + t_re)
            high.append(e_re - t_re)
        else:
            low.append((e_re + t_re, e_im + t_im))
            high.append((e_re - t_re, e_im - t_im))
    return low + high


def rows_body(ft, turn_v, twist, out, mid, real, *, block):
    b1 = ft.shape[1]
    rows2 = ft.shape[2]
    rows = rows2 // 2
    at = pl.program_id(0)
    for b0 in range(NT):
        both = lax.dot_general(
            turn_v[...].reshape(2 * block, b1), ft[b0], NN_DIMS, preferred_element_type=f32
        )
        p, q = both[:block], both[block:]
        a_re = p[:, :rows] - q[:, rows:]
        a_im = p[:, rows:] + q[:, :rows]
        if b0 > 0:
            c = twist[0, :, b0 : b0 + 1]
            s = twist[1, :, b0 : b0 + 1]
            a_re, a_im = a_re * c - a_im * s, a_re * s + a_im * c
        mid[0, b0] = a_re
        mid[1, b0] = a_im

    def group(g, carry):
        r0 = pl.multiple_of(g * 8, 8)
        z = [(mid[0, b0, pl.ds(r0, 8), :], mid[1, b0, pl.ds(r0, 8), :]) for b0 in range(NT)]
        x = fft_pos(z, True)
        for n0 in range(NT):
            real[n0, pl.ds(r0, 8), :] = x[n0]
        return carry

    lax.fori_loop(0, block // 8, group, 0)
    for n0 in range(NT):
        off = pl.multiple_of(n0 * b1 + at * block, block)
        out[:, pl.ds(off, block)] = real[n0].T


def own_body(res, tile_row, lane_row, out):
    tiles = res.shape[1]
    lanes = res.shape[2]
    n = tile_row.shape[1]
    hot = lax.broadcasted_iota(i32, (lanes, n), 0) == lane_row[...]
    hot = hot.astype(f32).astype(bf16)
    mine = lax.broadcasted_iota(i32, (tiles, n), 0) == tile_row[...]
    for c in range(2):
        total = jnp.zeros((tiles, n), f32)
        for part in split3(res[c]):
            total = total + lax.dot_general(part, hot, NN_DIMS, preferred_element_type=f32)
        out[c : c + 1, :] = jnp.sum(jnp.where(mine, total, 0.0), axis=0, keepdims=True)


def cos_sin(product, period):
    angle = (2.0 * math.pi / period) * (product % period).astype(f32)
    return jnp.cos(angle), jnp.sin(angle)


def to_all(x, devices):
    sent = jnp.broadcast_to(x[None], (devices,) + x.shape)
    return lax.all_to_all(sent, AXES, split_axis=0, concat_axis=0, tiled=True)


def on_device(model_grid, vis_values, weights, flags, uv_frac, cell_offset, tile_index):
    devices = lax.axis_size("blen") * lax.axis_size("tm")
    me = lax.axis_index("blen") * lax.axis_size("tm") + lax.axis_index("tm")
    per_dev = model_grid.shape[0]
    side = model_grid.shape[2]
    n = weights.shape[0]
    ntiles = per_dev * devices
    lanes = devices * MOST
    rows = NPIX // devices
    short = side // NT
    call = pl.pallas_call
    shape = jax.ShapeDtypeStruct

    tile_row = tile_index.reshape(1, n)
    weighted = weights * flags.astype(f32)
    fields = jnp.concatenate(
        [
            cell_offset.astype(f32),
            uv_frac,
            vis_values,
            weighted[None],
            jnp.zeros((1, n), f32),
        ]
    )
    width = MOST * FIELDS * per_dev
    packed, rank = call(
        lambda *refs: pack_body(*refs, devices=devices, per_dev=per_dev),
        out_shape=(shape((devices, width), f32), shape((1, n), i32)),
        name="pack",
    )(tile_index, tile_row, fields)
    recv = lax.all_to_all(packed, AXES, split_axis=0, concat_axis=0, tiled=True)
    pos, rest = call(
        lambda *refs: unpack_body(*refs, devices=devices, per_dev=per_dev),
        out_shape=(shape((per_dev, KEPT, lanes), f32), shape((per_dev, KEPT, lanes), f32)),
        name="unpack",
    )(recv)
    all_pos = to_all(pos, devices).reshape(NT // TVG, NT, TVG, KEPT, lanes)
    res = call(
        predict_body,
        grid=(per_dev,),
        in_specs=[
            pl.BlockSpec((1, 2, side, side), lambda l: (l, 0, 0, 0)),
            pl.BlockSpec((1, KEPT, lanes), lambda l: (l, 0, 0)),
            pl.BlockSpec((1, KEPT, lanes), lambda l: (l, 0, 0)),
        ],
        out_specs=pl.BlockSpec((1, 2, lanes), lambda l: (l, 0, 0)),
        out_shape=shape((per_dev, 2, lanes), f32),
        compiler_params=params(32),
        name="predict",
    )(model_grid, pos, rest)
    all_res = to_all(res, devices)
    weighted_residual = call(
        own_body,
        out_shape=shape((2, n), f32),
        name="own",
    )(
        all_res.reshape(ntiles, 2, lanes).transpose(1, 0, 2),
        tile_row,
        rank * devices + me,
    )

    image_rows = me * rows + jnp.arange(rows, dtype=i32)
    cells = jnp.arange(side, dtype=i32)
    turn_u = jnp.concatenate(cos_sin(image_rows[:, None] * cells[None, :], NPIX)).astype(bf16)
    lane_tile = jnp.arange(NT * lanes, dtype=i32) // lanes
    rot = jnp.stack(cos_sin(jnp.arange(NT, dtype=i32)[:, None] * lane_tile[None, :], NT))
    columns = call(
        lambda *refs: columns_body(*refs, lanes=lanes),
        grid=(NT,),
        in_specs=[
            pl.BlockSpec((1, NT, 1, KEPT, lanes), lambda t: (t // TVG, 0, t % TVG, 0, 0)),
            pl.BlockSpec((1, NT, 1, 2, lanes), lambda t: (t // TVG, 0, t % TVG, 0, 0)),
            pl.BlockSpec((2 * rows, side), lambda t: (0, 0)),
            pl.BlockSpec((2, NT, NT * lanes), lambda t: (0, 0, 0)),
        ],
        out_specs=pl.BlockSpec((NT, short, 2 * rows), lambda t: (0, t, 0)),
        out_shape=shape((NT, side, 2 * rows), bf16),
        scratch_shapes=[
            pltpu.VMEM((side, NT * lanes), bf16),
            pltpu.VMEM((2 * rows, NT * lanes), bf16),
        ],
        compiler_params=params(48),
        name="columns",
    )(all_pos, all_res.reshape(NT // TVG, NT, TVG, 2, lanes), turn_u, rot)

    block = 128
    turn_v = jnp.stack(cos_sin(cells[:, None] * cells[None, :], side)).astype(bf16)
    twist = jnp.stack(cos_sin(cells[:, None] * jnp.arange(NT, dtype=i32)[None, :], NPIX))
    gradient = call(
        lambda *refs: rows_body(*refs, block=block),
        grid=(side // block,),
        in_specs=[
            pl.BlockSpec((NT, side, 2 * rows), lambda b: (0, 0, 0)),
            pl.BlockSpec((2, block, side), lambda b: (0, b, 0)),
            pl.BlockSpec((2, block, NT), lambda b: (0, b, 0)),
        ],
        out_specs=pl.BlockSpec((rows, NPIX), lambda b: (0, 0)),
        out_shape=shape((rows, NPIX), f32),
        scratch_shapes=[
            pltpu.VMEM((2, NT, block, rows), f32),
            pltpu.VMEM((NT, block, rows), f32),
        ],
        compiler_params=params(56),
        name="rows",
    )(columns, turn_v, twist)
    return (gradient, weighted_residual)


def solution(mesh):
    in_specs = (
        P(AXES, None, None, None),
        P(None, AXES),
        P(AXES),
        P(AXES),
        P(None, AXES),
        P(None, AXES),
        P(AXES, None),
    )
    out_specs = (P(AXES, None), P(None, AXES))
    return jax.shard_map(
        on_device, mesh=mesh, in_specs=in_specs, out_specs=out_specs, check_vma=False
    )
```

time: 1060 us -> 247 us (0.23); the launches traced: 1050 us -> 246 us
  waiting for transfers between devices: 546 us -> 20 us
  local copies, waits for them, and re-layouts: 235 us -> 13.2 us
  matrix products: 196 us -> 0 us
  Pallas kernels: 0 us -> 189 us
  other arithmetic: 44 us -> 10.6 us
  starting transfers between devices: 24.7 us -> 12.5 us
    all_to_all x5 -> x3, waiting for transfers between devices: 546 us -> 20 us  [the longest x2 15.4 us: to_all(): return lax.all_to_all(sent, AXES, split_axis=0, concat_axis=0, tiled=True)]
    dot_general x6 -> x0, matrix products: 196 us -> none  [the longest x1 67.2 us: on_device(): jnp.einsum('acmi,cnvji->amnvj', tile_turn, turned, precision=highest)]
    pallas_call x0 -> x6, Pallas kernels: none -> 189 us  [the longest x1 157 us: on_device(): call(lambda *refs: columns_body(*refs, lanes=lanes), grid=(NT,), in_specs...]
    reshape x6 -> x0, local copies, waits for them, and re-layouts: 128 us -> none  [the longest x2 69.3 us: on_device(): landed.reshape(2, blen_size, tm_size, rows_dev, tile_cols, col_slice)]
    dot_general x1 -> x0, local copies, waits for them, and re-layouts: 31.1 us -> none  [on_device(): jnp.einsum('acmi,cnvji->amnvj', tile_turn, turned, precision=highest)]
    transpose x2 -> x0, local copies, waits for them, and re-layouts: 25.2 us -> none  [the longest x1 25.1 us: grid_step(): jnp.einsum('qrj,qrci->qcji', taps_v, spread, preferred_element_type=jnp.f...]
    all_to_all x4 -> x3, local copies, waits for them, and re-layouts: 19.1 us -> 2.27 us  [the longest x1 1.42 us: on_device(): recv = lax.all_to_all(packed, AXES, split_axis=0, concat_axis=0, tiled=True)]
    all_to_all x5 -> x3, starting transfers between devices: 24.7 us -> 12.5 us  [the longest x1 7.3 us: on_device(): recv = lax.all_to_all(packed, AXES, split_axis=0, concat_axis=0, tiled=True)]
  transfers between devices with their start and end apart: 5 -> 3, of which waited for: 4 -> 3; matrix products, arithmetic and copies ran while one was open for 24% -> 5% of each run, Pallas kernels for 0% -> 1%
where the time goes in v1:
time: 247 us; the launch traced here: 246 us
  Pallas kernels  189 us (77%)
  waiting for transfers between devices  20 us (8%)
  local copies, waits for them, and re-layouts  13.2 us (5%)
  starting transfers between devices  12.5 us (5%)
  other arithmetic  10.6 us (4%)
    pallas_call x1, Pallas kernels, on_device(): call(lambda *refs: columns_body(*refs, lanes=lanes), grid=(NT,), in_specs...  157 us
    pallas_call x1, Pallas kernels, on_device(): call(lambda *refs: rows_body(*refs, block=block), grid=(side // block,),...  23 us
    all_to_all x2, waiting for transfers between devices, to_all(): return lax.all_to_all(sent, AXES, split_axis=0, concat_axis=0, tiled=True)  15.4 us
    all_to_all x1, starting transfers between devices, on_device(): recv = lax.all_to_all(packed, AXES, split_axis=0, concat_axis=0, tiled=True)  7.3 us
    unnamed x12, local copies, waits for them, and re-layouts  6.97 us
    another operation x2, other arithmetic  6.76 us
    all_to_all x2, starting transfers between devices, to_all(): return lax.all_to_all(sent, AXES, split_axis=0, concat_axis=0, tiled=True)  5.19 us
  transfers between devices with their start and end apart: 3, of which 3 were waited for; matrix products, arithmetic and copies ran while one was open for 5% of the time, Pallas kernels for 1%

profile of v1, /device:TPU:0, one launch (start us, length us, event | category | flops | bytes accessed | tf_op | source)
XLA Modules:
  0.0 246.5 jit_solution(1015273869176146554)
XLA Ops:
  0.6 0.7 convert_element_type.59
  1.3 1.5 copy.12.refs_0_
  2.9 0.7 convert_multiply_fusion
  3.6 1.3 concatenate.7.refs_2_
  4.9 2.2 pack.1
  7.0 0.0 copy-start.4
  7.0 1.4 copy.13
  8.5 7.3 %all-to-all-start = ((f32[32,1,256]{2,1,0:T(1,128)}), f32[32,1,256]{2,1,0:T(1,128)S(1)}, u32[]{:S(2)}, u32[]{:S(2)}) async-start(f32[32,1,256]{2,1,0:T(1,128)} %copy.13), calls=%async_computation | async-start | bytes 65536 | tf_op jit(solution)/shard_map/all_to_all | solution.py:246
  15.8 2.5 cosine_convert_fusion.1
  18.3 0.1 fusion.26
  18.4 4.6 %all-to-all-done = f32[32,1,256]{2,1,0:T(1,128)S(1)} async-done(((f32[32,1,256]{2,1,0:T(1,128)}), f32[32,1,256]{2,1,0:T(1,128)S(1)}, u32[]{:S(2)}, u32[]{:S(2)}) %all-to-all-start) | async-done | bytes 32800 | tf_op jit(solution)/shard_map/all_to_all | solution.py:246
  23.0 0.6 copy.22
  23.6 1.5 unpack.1
  25.2 0.0 copy-start
  25.2 3.4 %copy-done = bf16[8,2,512,512]{3,2,1,0:T(8,128)(2,1)S(1)} copy-done((bf16[8,2,512,512]{3,2,1,0:T(8,128)(2,1)S(1)}, bf16[8,2,512,512]{3,2,1,0:T(8,128)(2,1)}, u32[]{:S(2)}) %copy-start) | copy-done | bytes 8388632
  28.6 0.0 copy-start.1
  28.6 0.7 copy-done.1
  29.3 0.0 copy-start.3
  29.3 0.7 copy-done.3
  30.0 0.0 copy-start.2
  30.0 3.9 %predict.1 = f32[8,2,128]{2,1,0:T(2,128)S(1)} custom-call(bf16[8,2,512,512]{3,2,1,0:T(8,128)(2,1)S(1)} %copy-done, f32[8,4,128]{2,1,0:T(4,128)S(1)} %copy-done.1, f32[8,4,128]{2,1,0:T(4,128)S(1)} %copy-done.3), custom_call_target="tpu_custom_call" | custom-call | tf_op jit(solution)/shard_map/predict/pallas_call | solution.py:253
  33.9 0.7 broadcast_in_dim.11
  34.6 2.6 %all-to-all-start.2 = ((f32[32,8,2,128]{3,1,2,0:T(8,128)}), f32[32,8,2,128]{3,1,2,0:T(8,128)S(1)}, u32[]{:S(2)}, u32[]{:S(2)}) async-start(f32[32,8,2,128]{3,1,2,0:T(8,128)} %broadcast_in_dim.11), calls=%async_computation.2 | async-start | bytes 524288 | tf_op jit(solution)/shard_map/all_to_all | solution.py:213
  37.2 1.0 copy.16.refs_2_
  38.3 4.3 %sine_convert_fusion = (bf16[1,512,512]{2,1,0:T(8,128)(2,1)S(1)}, bf16[1,512,512]{2,1,0:T(8,128)(2,1)S(1)}) fusion(), kind=kLoop, calls=%fused_computation.7 | loop fusion | flops 4194304 | bytes 1048576 | tf_op jit(solution)/shard_map/convert.1
  42.6 1.2 pad_maximum_fusion.refs_1_
  43.8 4.1 %all-to-all-done.2 = f32[32,8,2,128]{3,1,2,0:T(8,128)S(1)} async-done(((f32[32,8,2,128]{3,1,2,0:T(8,128)}), f32[32,8,2,128]{3,1,2,0:T(8,128)S(1)}, u32[]{:S(2)}, u32[]{:S(2)}) %all-to-all-start.2) | async-done | bytes 262176 | tf_op jit(solution)/shard_map/all_to_all | solution.py:213
  47.8 0.0 copy-done.2
  47.8 0.9 broadcast_in_dim.10
  48.7 2.6 %all-to-all-start.1 = ((f32[32,8,4,128]{3,2,1,0:T(4,128)}), f32[32,8,4,128]{3,2,1,0:T(4,128)S(1)}, u32[]{:S(2)}, u32[]{:S(2)}) async-start(f32[32,8,4,128]{3,2,1,0:T(4,128)} %broadcast_in_dim.10), calls=%async_computation.1 | async-start | bytes 1048576 | tf_op jit(solution)/shard_map/all_to_all | solution.py:213
  51.4 0.0 copy-done.4
  51.4 0.6 multiply_add_fusion.lane_row
  52.0 0.5 fusion.19
  52.5 0.7 copy.21
  53.2 2.2 own.1
  55.4 0.1 copy.15
  55.6 11.3 %all-to-all-done.1 = f32[32,8,4,128]{3,2,1,0:T(4,128)S(1)} async-done(((f32[32,8,4,128]{3,2,1,0:T(4,128)}), f32[32,8,4,128]{3,2,1,0:T(4,128)S(1)}, u32[]{:S(2)}, u32[]{:S(2)}) %all-to-all-start.1) | async-done | bytes 524320 | tf_op jit(solution)/shard_map/all_to_all | solution.py:213
  66.9 156.6 %columns.1.refs_0_ = bf16[16,512,512]{2,1,0:T(8,128)(2,1)} custom-call(f32[4,16,4,4,128]{4,3,2,1,0:T(4,128)S(1)} %bitcast.13, f32[4,16,4,2,128]{4,3,2,1,0:T(2,128)S(1)} %bitcast.14, bf16[512,512]{1,0:T(8,128)(2,1)S(1)} %pad_maximum_fusion.1.refs_2_, f32[2,16,2048]{2,1,0:T(8,128)S(1)} %pad_maximum_fusion.2.refs_3_), custom_call_target="tpu_custom_call" | custom-call | tf_op jit(solution)/shard_map/columns/pallas_call | solution.py:282
  223.5 23.0 %rows.1 = f32[256,8192]{1,0:T(8,128)} custom-call(bf16[16,512,512]{2,1,0:T(8,128)(2,1)} %columns.1.refs_0_, bf16[2,512,512]{2,1,0:T(8,128)(2,1)} %pad_maximum_fusion.refs_1_, f32[2,512,16]{2,1,0:T(8,128)} %copy.16.refs_2_), custom_call_target="tpu_custom_call" | custom-call | tf_op jit(solution)/shard_map/rows/pallas_call | solution.py:304
  (7 shorter events, 0.1 us)
Async XLA Ops:
  7.0 44.3 %copy-start.4 = (s32[1,512]{1,0:T(1,128)S(1)}, s32[1,512]{1,0:T(1,128)}, u32[]{:S(2)}) copy-start(s32[1,512]{1,0:T(1,128)} %get-tuple-element.9) | copy-start | bytes 6148
  8.5 14.6 %all-to-all-start = ((f32[32,1,256]{2,1,0:T(1,128)}), f32[32,1,256]{2,1,0:T(1,128)S(1)}, u32[]{:S(2)}, u32[]{:S(2)}) async-start(f32[32,1,256]{2,1,0:T(1,128)} %copy.13), calls=%async_computation | async-start | bytes 65536 | tf_op jit(solution)/shard_map/all_to_all | solution.py:246
  25.2 3.4 %copy-start = (bf16[8,2,512,512]{3,2,1,0:T(8,128)(2,1)S(1)}, bf16[8,2,512,512]{3,2,1,0:T(8,128)(2,1)}, u32[]{:S(2)}) copy-start(bf16[8,2,512,512]{3,2,1,0:T(8,128)(2,1)} %model.1) | copy-start | bytes 25165828
  28.6 0.7 copy-start.1
  29.3 0.7 copy-start.3
  30.0 17.8 %copy-start.2 = (f32[8,4,128]{2,1,0:T(4,128)S(1)}, f32[8,4,128]{2,1,0:T(4,128)}, u32[]{:S(2)}) copy-start(f32[8,4,128]{2,1,0:T(4,128)} %get-tuple-element.7.pos) | copy-start | bytes 49156
  34.6 13.2 %all-to-all-start.2 = ((f32[32,8,2,128]{3,1,2,0:T(8,128)}), f32[32,8,2,128]{3,1,2,0:T(8,128)S(1)}, u32[]{:S(2)}, u32[]{:S(2)}) async-start(f32[32,8,2,128]{3,1,2,0:T(8,128)} %broadcast_in_dim.11), calls=%async_computation.2 | async-start | bytes 524288 | tf_op jit(solution)/shard_map/all_to_all | solution.py:213
  48.7 18.2 %all-to-all-start.1 = ((f32[32,8,4,128]{3,2,1,0:T(4,128)}), f32[32,8,4,128]{3,2,1,0:T(4,128)S(1)}, u32[]{:S(2)}, u32[]{:S(2)}) async-start(f32[32,8,4,128]{3,2,1,0:T(4,128)} %broadcast_in_dim.10), calls=%async_computation.1 | async-start | bytes 1048576 | tf_op jit(solution)/shard_map/all_to_all | solution.py:213

commit v2 on v1

--- a/solution.py
+++ b/solution.py
@@ -14,6 +14,7 @@
 MOST = 4
 FIELDS = 8
 KEPT = 4
+CELLS = 16
 
 AXES = ("blen", "tm")
 f32 = jnp.float32
@@ -93,40 +94,48 @@
         res[0, c : c + 1, :] = rest[0, 2:3, :] * (predicted - rest[0, c : c + 1, :])
 
 
+def pattern(first, frac):
+    cells = lax.broadcasted_iota(i32, (CELLS, first.shape[1]), 0)
+    k = (cells - first) & (CELLS - 1)
+    dist = (k - (KSUP // 2 - 1)).astype(f32) - frac
+    value = jnp.where(k < KSUP, jnp.exp(-0.5 * dist * dist), 0.0).astype(bf16)
+    return value, ((first + k) >> 4).astype(f32).astype(bf16)
+
+
+def dense(value, where, side):
+    zero = jnp.zeros_like(value)
+    blocks = [jnp.where(where == jnp.bfloat16(b), value, zero) for b in range(side // CELLS)]
+    return jnp.concatenate(blocks, axis=0)
+
+
 def columns_body(pos, res, turn_u, rot, out, kv_all, up_all, *, lanes):
     side = turn_u.shape[1]
     rows2 = turn_u.shape[0]
     rows = rows2 // 2
-    short = side // NT
-    cells_i = lax.broadcasted_iota(i32, (side, lanes), 0)
-    cells_f = cells_i.astype(f32)
-    perm_i = (cells_i % short) * NT + cells_i // short
-    perm_f = perm_i.astype(f32)
-
-    def step(tu, carry):
-        at = pl.multiple_of(tu * lanes, lanes)
-        p = pos[0, tu, 0]
-        r = res[0, tu, 0]
-        ku = tap_block(cells_i, cells_f, p[0:1], p[2:3])
-        kv_all[:, pl.ds(at, lanes)] = tap_block(perm_i, perm_f, p[1:2], p[3:4])
+    per = max(1, 512 // lanes)
+    span = per * lanes
+    for step in range(NT // per):
+        at = step * span
+        p = jnp.concatenate([pos[0, step * per + i, 0] for i in range(per)], axis=1)
+        r = jnp.concatenate([res[0, step * per + i, 0] for i in range(per)], axis=1)
+        first = p[0:2].astype(i32) - (KSUP // 2 - 1)
+        ku = dense(*pattern(first[0:1], p[2:3]), side)
+        kv_all[:, at : at + span] = dense(*pattern(first[1:2], p[3:4]), side)
         v = lax.dot_general(turn_u[...], ku, NN_DIMS, preferred_element_type=f32)
         r_re = r[0:1] * (1.0 / NPIX)
         r_im = r[1:2] * (1.0 / NPIX)
-        cos_t = rot[0, :, pl.ds(at, lanes)]
-        sin_t = rot[1, :, pl.ds(at, lanes)]
+        cos_t = rot[0, :, at : at + span]
+        sin_t = rot[1, :, at : at + span]
         c_re = (r_re * cos_t - r_im * sin_t)[None]
         c_im = (r_re * sin_t + r_im * cos_t)[None]
-        v_re = v[:rows].reshape(rows // NT, NT, lanes)
-        v_im = v[rows:].reshape(rows // NT, NT, lanes)
-        u_re = (c_re * v_re - c_im * v_im).reshape(rows, lanes)
-        u_im = (c_re * v_im + c_im * v_re).reshape(rows, lanes)
-        up_all[0:rows, pl.ds(at, lanes)] = u_re.astype(bf16)
-        up_all[rows:rows2, pl.ds(at, lanes)] = u_im.astype(bf16)
-        return carry
-
-    lax.fori_loop(0, NT, step, 0)
+        v_re = v[:rows].reshape(rows // NT, NT, span)
+        v_im = v[rows:].reshape(rows // NT, NT, span)
+        u_re = (c_re * v_re - c_im * v_im).reshape(rows, span)
+        u_im = (c_re * v_im + c_im * v_re).reshape(rows, span)
+        up_all[0:rows, at : at + span] = u_re.astype(bf16)
+        up_all[rows:rows2, at : at + span] = u_im.astype(bf16)
     ft = lax.dot_general(kv_all[...], up_all[...], NT_DIMS, preferred_element_type=f32)
-    out[...] = ft.astype(bf16).reshape(NT, short, rows2)
+    out[0] = ft.astype(bf16)
 
 
 def fft_pos(z, real_only=False):
@@ -156,37 +165,52 @@
     return low + high
 
 
-def rows_body(ft, turn_v, twist, out, mid, real, *, block):
-    b1 = ft.shape[1]
-    rows2 = ft.shape[2]
-    rows = rows2 // 2
-    at = pl.program_id(0)
-    for b0 in range(NT):
-        both = lax.dot_general(
-            turn_v[...].reshape(2 * block, b1), ft[b0], NN_DIMS, preferred_element_type=f32
-        )
-        p, q = both[:block], both[block:]
-        a_re = p[:, :rows] - q[:, rows:]
-        a_im = p[:, rows:] + q[:, :rows]
-        if b0 > 0:
-            c = twist[0, :, b0 : b0 + 1]
-            s = twist[1, :, b0 : b0 + 1]
-            a_re, a_im = a_re * c - a_im * s, a_re * s + a_im * c
-        mid[0, b0] = a_re
-        mid[1, b0] = a_im
-
-    def group(g, carry):
-        r0 = pl.multiple_of(g * 8, 8)
-        z = [(mid[0, b0, pl.ds(r0, 8), :], mid[1, b0, pl.ds(r0, 8), :]) for b0 in range(NT)]
-        x = fft_pos(z, True)
+def rows_body(ft, turn_v, twist, out, turned, *flips, steps):
+    side = turn_v.shape[0]
+    rows = ft.shape[2] // 2
+    part = ft.shape[1]
+    width = flips[0].shape[1]
+    g = pl.program_id(0)
+
+    @pl.when(g < steps)
+    def _():
+        for j in range(part // 16):
+            r0 = j * 16
+            tc = twist[0, r0 : r0 + 16, :]
+            ts = twist[1, r0 : r0 + 16, :]
+            at = pl.multiple_of(g * part + r0, 16)
+            for h in range(rows // width):
+                c0 = h * width
+                z = [
+                    (
+                        ft[t, r0 : r0 + 16, c0 : c0 + width].astype(f32),
+                        ft[t, r0 : r0 + 16, rows + c0 : rows + c0 + width].astype(f32),
+                    )
+                    for t in range(NT)
+                ]
+                x = fft_pos(z)
+                for n0 in range(NT):
+                    re, im = x[n0]
+                    if n0 > 0:
+                        c = tc[:, n0 : n0 + 1]
+                        s = ts[:, n0 : n0 + 1]
+                        re, im = re * c - im * s, re * s + im * c
+                    turned[n0, pl.ds(at, 16), c0 : c0 + width] = re.astype(bf16)
+                    turned[n0, pl.ds(at + side, 16), c0 : c0 + width] = im.astype(bf16)
+
+    @pl.when(g == steps)
+    def _():
         for n0 in range(NT):
-            real[n0, pl.ds(r0, 8), :] = x[n0]
-        return carry
-
-    lax.fori_loop(0, block // 8, group, 0)
-    for n0 in range(NT):
-        off = pl.multiple_of(n0 * b1 + at * block, block)
-        out[:, pl.ds(off, block)] = real[n0].T
+            x = lax.dot_general(turn_v[...], turned[n0], NN_DIMS, preferred_element_type=f32)
+            for h in range(rows // width):
+                flips[h][pl.ds(n0, side, stride=NT), :] = x[:, h * width : (h + 1) * width]
+
+    @pl.when(g > steps)
+    def _():
+        cols = out.shape[1]
+        at = pl.multiple_of((g - steps - 1) * cols, cols)
+        for h in range(rows // width):
+            out[h * width : (h + 1) * width, :] = flips[h][pl.ds(at, cols), :].T
 
 
 def own_body(res, tile_row, lane_row, out):
@@ -222,7 +246,6 @@
     ntiles = per_dev * devices
     lanes = devices * MOST
     rows = NPIX // devices
-    short = side // NT
     call = pl.pallas_call
     shape = jax.ShapeDtypeStruct
 
@@ -249,7 +272,7 @@
         out_shape=(shape((per_dev, KEPT, lanes), f32), shape((per_dev, KEPT, lanes), f32)),
         name="unpack",
     )(recv)
-    all_pos = to_all(pos, devices).reshape(NT // TVG, NT, TVG, KEPT, lanes)
+    all_pos = to_all(pos, devices)
     res = call(
         predict_body,
         grid=(per_dev,),
@@ -263,6 +286,8 @@
         compiler_params=params(32),
         name="predict",
     )(model_grid, pos, rest)
+    res, all_pos = lax.optimization_barrier((res, all_pos))
+    all_pos = all_pos.reshape(NT // TVG, NT, TVG, KEPT, lanes)
     all_res = to_all(res, devices)
     weighted_residual = call(
         own_body,
@@ -288,7 +313,7 @@
             pl.BlockSpec((2 * rows, side), lambda t: (0, 0)),
             pl.BlockSpec((2, NT, NT * lanes), lambda t: (0, 0, 0)),
         ],
-        out_specs=pl.BlockSpec((NT, short, 2 * rows), lambda t: (0, t, 0)),
+        out_specs=pl.BlockSpec((1, side, 2 * rows), lambda t: (t, 0, 0)),
         out_shape=shape((NT, side, 2 * rows), bf16),
         scratch_shapes=[
             pltpu.VMEM((side, NT * lanes), bf16),
@@ -298,24 +323,27 @@
         name="columns",
     )(all_pos, all_res.reshape(NT // TVG, NT, TVG, 2, lanes), turn_u, rot)
 
-    block = 128
-    turn_v = jnp.stack(cos_sin(cells[:, None] * cells[None, :], side)).astype(bf16)
+    steps = 8
+    part = side // steps
+    width = min(128, rows)
+    wide = 512
+    cos_v, sin_v = cos_sin(cells[:, None] * cells[None, :], side)
+    turn_v = jnp.concatenate([cos_v, -sin_v], axis=1).astype(bf16)
     twist = jnp.stack(cos_sin(cells[:, None] * jnp.arange(NT, dtype=i32)[None, :], NPIX))
+    last = steps - 1
     gradient = call(
-        lambda *refs: rows_body(*refs, block=block),
-        grid=(side // block,),
+        lambda *refs: rows_body(*refs, steps=steps),
+        grid=(steps + 1 + NPIX // wide,),
         in_specs=[
-            pl.BlockSpec((NT, side, 2 * rows), lambda b: (0, 0, 0)),
-            pl.BlockSpec((2, block, side), lambda b: (0, b, 0)),
-            pl.BlockSpec((2, block, NT), lambda b: (0, b, 0)),
+            pl.BlockSpec((NT, part, 2 * rows), lambda g: (0, jnp.minimum(g, last), 0)),
+            pl.BlockSpec((side, 2 * side), lambda g: (0, 0)),
+            pl.BlockSpec((2, part, NT), lambda g: (0, jnp.minimum(g, last), 0)),
         ],
-        out_specs=pl.BlockSpec((rows, NPIX), lambda b: (0, 0)),
+        out_specs=pl.BlockSpec((rows, wide), lambda g: (0, jnp.maximum(g - steps - 1, 0))),
         out_shape=shape((rows, NPIX), f32),
-        scratch_shapes=[
-            pltpu.VMEM((2, NT, block, rows), f32),
-            pltpu.VMEM((NT, block, rows), f32),
-        ],
-        compiler_params=params(56),
+        scratch_shapes=[pltpu.VMEM((NT, 2 * side, rows), bf16)]
+        + [pltpu.VMEM((NPIX, width), f32)] * (rows // width),
+        compiler_params=params(48),
         name="rows",
     )(columns, turn_v, twist)
     return (gradient, weighted_residual)

time: 247 us -> 131 us (0.53)
  Pallas kernels: 189 us -> 76.1 us
  waiting for transfers between devices: 20 us -> 16 us
    pallas_call x1, Pallas kernels: 157 us -> 41.8 us  [on_device(): call(lambda *refs: columns_body(*refs, lanes=lanes), grid=(NT,), in_specs...]
    all_to_all x2, waiting for transfers between devices: 15.4 us -> 11.2 us  [to_all(): return lax.all_to_all(sent, AXES, split_axis=0, concat_axis=0, tiled=True)]
    another operation x3 -> x2, other arithmetic: 7.92 us -> 6.81 us
    unnamed x12 -> x10, local copies, waits for them, and re-layouts: 6.97 us -> 6.97 us
  transfers between devices with their start and end apart: 3 -> 3, of which waited for: 3 -> 3; matrix products, arithmetic and copies ran while one was open for 5% -> 6% of each run, Pallas kernels for 1% -> 3%
where the time goes in v2:
time: 131 us; the launch traced here: 130 us
  Pallas kernels  76.1 us (58%)
  waiting for transfers between devices  16 us (12%)
  starting transfers between devices  14.3 us (11%)
  local copies, waits for them, and re-layouts  13.1 us (10%)
  other arithmetic  9.63 us (7%)
    pallas_call x1, Pallas kernels, on_device(): call(lambda *refs: columns_body(*refs, lanes=lanes), grid=(NT,), in_specs...  41.8 us
    pallas_call x1, Pallas kernels, on_device(): call(lambda *refs: rows_body(*refs, steps=steps), grid=(steps + 1 + NPIX...  24.6 us
    all_to_all x2, waiting for transfers between devices, to_all(): return lax.all_to_all(sent, AXES, split_axis=0, concat_axis=0, tiled=True)  11.2 us
    all_to_all x1, starting transfers between devices, on_device(): recv = lax.all_to_all(packed, AXES, split_axis=0, concat_axis=0, tiled=True)  7.3 us
    all_to_all x2, starting transfers between devices, to_all(): return lax.all_to_all(sent, AXES, split_axis=0, concat_axis=0, tiled=True)  7.02 us
    unnamed x10, local copies, waits for them, and re-layouts  6.97 us
    another operation x2, other arithmetic  6.81 us
    all_to_all x1, waiting for transfers between devices, on_device(): recv = lax.all_to_all(packed, AXES, split_axis=0, concat_axis=0, tiled=True)  4.76 us
  transfers between devices with their start and end apart: 3, of which 3 were waited for; matrix products, arithmetic and copies ran while one was open for 6% of the time, Pallas kernels for 3%

profile of v2, /device:TPU:0, one launch (start us, length us, event | category | flops | bytes accessed | tf_op | source)
XLA Modules:
  0.0 129.9 jit_solution(16032731136048318571)
XLA Ops:
  0.6 0.7 convert_element_type.48
  1.3 1.5 %copy.12.refs_0_ = s32[512,1]{1,0:T(8,128)} copy(s32[512,1]{0,1:T(1,128)} %param.13) | data formatting | bytes 4096 | tf_op args[6]
  2.9 0.7 convert_multiply_fusion
  3.6 1.3 %concatenate.11.refs_2_ = f32[8,512]{1,0:T(8,128)} concatenate(f32[2,512]{1,0:T(2,128)S(1)} %convert_element_type.48, f32[2,512]{1,0:T(2,128)} %param.11, f32[2,512]{1,0:T(2,128)} %param.8, f32[1,512]{1,0:T(1,128)S(1)} %bitcast.20, f32[1,512]{1,0:T(1,128)S(1)} %broadcast_in_dim.9), dimensions={0} | concatenate | bytes 32768 | tf_op jit(solution)/shard_map/concatenate | solution.py:254
  4.9 2.2 %pack.1 = (f32[32,256]{1,0:T(8,128)}, s32[1,512]{1,0:T(1,128)}) custom-call(s32[512,1]{1,0:T(8,128)} %copy.12.refs_0_, s32[1,512]{1,0:T(1,128)} %bitcast.18, f32[8,512]{1,0:T(8,128)} %concatenate.11.refs_2_), custom_call_target="tpu_custom_call" | custom-call | tf_op jit(solution)/shard_map/pack/pallas_call | solution.py:264
  7.0 1.4 %copy.13 = f32[32,1,256]{2,1,0:T(1,128)} copy(f32[32,1,256]{2,0,1:T(8,128)} %bitcast.17) | data formatting | bytes 65536 | tf_op jit(solution)/shard_map/all_to_all | solution.py:269
  8.4 7.3 %all-to-all-start = ((f32[32,1,256]{2,1,0:T(1,128)}), f32[32,1,256]{2,1,0:T(1,128)S(1)}, u32[]{:S(2)}, u32[]{:S(2)}) async-start(f32[32,1,256]{2,1,0:T(1,128)} %copy.13), calls=%async_computation | async-start | bytes 65536 | tf_op jit(solution)/shard_map/all_to_all | solution.py:269
  15.8 0.0 copy-start.3
  15.8 2.5 %cosine_convert_fusion.1 = (bf16[256,512]{1,0:T(8,128)(2,1)S(1)}, bf16[256,512]{1,0:T(8,128)(2,1)S(1)}) fusion(s32[256]{0:T(256)S(1)} %iota_add_fusion), kind=kLoop, calls=%fused_computation.20 | loop fusion | flops 2097152 | bytes 525312 | tf_op jit(solution)/shard_map/convert.2
  18.2 4.8 %all-to-all-done = f32[32,1,256]{2,1,0:T(1,128)S(1)} async-done(((f32[32,1,256]{2,1,0:T(1,128)}), f32[32,1,256]{2,1,0:T(1,128)S(1)}, u32[]{:S(2)}, u32[]{:S(2)}) %all-to-all-start) | async-done | bytes 32800 | tf_op jit(solution)/shard_map/all_to_all | solution.py:269
  23.0 0.6 copy.22
  23.6 1.5 %unpack.1 = (f32[8,4,128]{2,1,0:T(4,128)}, f32[8,4,128]{2,1,0:T(4,128)}) custom-call(f32[32,256]{1,0:T(8,128)} %bitcast.16), custom_call_target="tpu_custom_call" | custom-call | tf_op jit(solution)/shard_map/unpack/pallas_call | solution.py:270
  25.1 1.6 %broadcast_in_dim.10 = f32[32,8,4,128]{3,2,1,0:T(4,128)} broadcast(f32[8,4,128]{2,1,0:T(4,128)} %get-tuple-element.9.pos), dimensions={1,2,3} | broadcast | bytes 540672 | tf_op jit(solution)/shard_map/broadcast_in_dim | solution.py:236
  26.8 2.6 %all-to-all-start.1 = ((f32[32,8,4,128]{3,2,1,0:T(4,128)}), f32[32,8,4,128]{3,2,1,0:T(4,128)S(1)}, u32[]{:S(2)}, u32[]{:S(2)}) async-start(f32[32,8,4,128]{3,2,1,0:T(4,128)} %broadcast_in_dim.10), calls=%async_computation.1 | async-start | bytes 1048576 | tf_op jit(solution)/shard_map/all_to_all | solution.py:237
  29.4 0.1 fusion.26
  29.6 4.3 %negate_convert_fusion = (bf16[512,512]{1,0:T(8,128)(2,1)S(1)}, bf16[512,512]{1,0:T(8,128)(2,1)S(1)}) fusion(), kind=kLoop, calls=%fused_computation.7 | loop fusion | flops 4456448 | bytes 1048576 | tf_op jit(solution)/shard_map/convert.1
  34.0 0.1 pad_maximum_fusion.refs_1_
  34.1 0.5 fusion.19
  34.6 0.0 copy-start
  34.6 3.4 %copy-done = bf16[8,2,512,512]{3,2,1,0:T(8,128)(2,1)S(1)} copy-done((bf16[8,2,512,512]{3,2,1,0:T(8,128)(2,1)S(1)}, bf16[8,2,512,512]{3,2,1,0:T(8,128)(2,1)}, u32[]{:S(2)}) %copy-start) | copy-done | bytes 8388632
  38.0 0.0 copy-start.1
  38.0 0.7 copy-done.1
  38.7 0.0 copy-start.2
  38.7 0.7 copy-done.2
  39.4 3.9 %predict.1 = f32[8,2,128]{2,1,0:T(2,128)S(1)} custom-call(bf16[8,2,512,512]{3,2,1,0:T(8,128)(2,1)S(1)} %copy-done, f32[8,4,128]{2,1,0:T(4,128)S(1)} %copy-done.1, f32[8,4,128]{2,1,0:T(4,128)S(1)} %copy-done.2), custom_call_target="tpu_custom_call" | custom-call | tf_op jit(solution)/shard_map/predict/pallas_call | solution.py:276
  43.3 1.6 %all-to-all-done.1 = f32[32,8,4,128]{3,2,1,0:T(4,128)S(1)} async-done(((f32[32,8,4,128]{3,2,1,0:T(4,128)}), f32[32,8,4,128]{3,2,1,0:T(4,128)S(1)}, u32[]{:S(2)}, u32[]{:S(2)}) %all-to-all-start.1) | async-done | bytes 524320 | tf_op jit(solution)/shard_map/all_to_all | solution.py:237
  44.9 0.7 broadcast_in_dim.11
  45.7 4.4 %all-to-all-start.2 = ((f32[32,8,2,128]{3,1,2,0:T(8,128)}), f32[32,8,2,128]{3,1,2,0:T(8,128)S(1)}, u32[]{:S(2)}, u32[]{:S(2)}) async-start(f32[32,8,2,128]{3,1,2,0:T(8,128)} %broadcast_in_dim.11), calls=%async_computation.2 | async-start | bytes 524288 | tf_op jit(solution)/shard_map/all_to_all | solution.py:237
  50.1 0.2 copy.16.refs_2_
  50.3 0.0 copy-done.3
  50.3 0.6 multiply_add_fusion.lane_row
  50.9 9.6 %all-to-all-done.2 = f32[32,8,2,128]{3,1,2,0:T(8,128)S(1)} async-done(((f32[32,8,2,128]{3,1,2,0:T(8,128)}), f32[32,8,2,128]{3,1,2,0:T(8,128)S(1)}, u32[]{:S(2)}, u32[]{:S(2)}) %all-to-all-start.2) | async-done | bytes 262176 | tf_op jit(solution)/shard_map/all_to_all | solution.py:237
  60.5 0.7 copy.21
  61.2 2.2 %own.1 = f32[2,512]{1,0:T(2,128)} custom-call(f32[2,256,128]{2,1,0:T(8,128)} %bitcast.15, s32[1,512]{1,0:T(1,128)} %bitcast.19, s32[1,512]{1,0:T(1,128)} %multiply_add_fusion.lane_row), custom_call_target="tpu_custom_call" | custom-call | tf_op jit(solution)/shard_map/own/pallas_call | solution.py:292
  63.4 0.1 copy.15
  63.6 41.8 %columns.1.refs_0_ = bf16[16,512,512]{2,1,0:T(8,128)(2,1)} custom-call(f32[4,16,4,4,128]{4,3,2,1,0:T(4,128)S(1)} %bitcast.13, f32[4,16,4,2,128]{4,3,2,1,0:T(2,128)S(1)} %bitcast.14, bf16[512,512]{1,0:T(8,128)(2,1)S(1)} %pad_maximum_fusion.1.refs_2_, f32[2,16,2048]{2,1,0:T(8,128)S(1)} %pad_maximum_fusion.2.refs_3_), custom_call_target="tpu_custom_call" | custom-call | tf_op jit(solution)/shard_map/columns/pallas_call | solution.py:307
  105.3 24.6 %rows.1 = f32[256,8192]{1,0:T(8,128)} custom-call(bf16[16,512,512]{2,1,0:T(8,128)(2,1)} %columns.1.refs_0_, bf16[512,1024]{1,0:T(8,128)(2,1)S(1)} %pad_maximum_fusion.refs_1_, f32[2,512,16]{2,1,0:T(8,128)S(1)} %copy.16.refs_2_), custom_call_target="tpu_custom_call" | custom-call | tf_op jit(solution)/shard_map/rows/pallas_call | solution.py:334
  (7 shorter events, 0.1 us)
Async XLA Ops:
  8.4 14.6 %all-to-all-start = ((f32[32,1,256]{2,1,0:T(1,128)}), f32[32,1,256]{2,1,0:T(1,128)S(1)}, u32[]{:S(2)}, u32[]{:S(2)}) async-start(f32[32,1,256]{2,1,0:T(1,128)} %copy.13), calls=%async_computation | async-start | bytes 65536 | tf_op jit(solution)/shard_map/all_to_all | solution.py:269
  15.8 34.6 %copy-start.3 = (s32[1,512]{1,0:T(1,128)S(1)}, s32[1,512]{1,0:T(1,128)}, u32[]{:S(2)}) copy-start(s32[1,512]{1,0:T(1,128)} %get-tuple-element.13) | copy-start | bytes 6148
  26.8 18.2 %all-to-all-start.1 = ((f32[32,8,4,128]{3,2,1,0:T(4,128)}), f32[32,8,4,128]{3,2,1,0:T(4,128)S(1)}, u32[]{:S(2)}, u32[]{:S(2)}) async-start(f32[32,8,4,128]{3,2,1,0:T(4,128)} %broadcast_in_dim.10), calls=%async_computation.1 | async-start | bytes 1048576 | tf_op jit(solution)/shard_map/all_to_all | solution.py:237
  34.6 3.4 %copy-start = (bf16[8,2,512,512]{3,2,1,0:T(8,128)(2,1)S(1)}, bf16[8,2,512,512]{3,2,1,0:T(8,128)(2,1)}, u32[]{:S(2)}) copy-start(bf16[8,2,512,512]{3,2,1,0:T(8,128)(2,1)} %model.1) | copy-start | bytes 25165828
  38.0 0.7 copy-start.1
  38.7 0.7 copy-start.2
  45.7 14.8 %all-to-all-start.2 = ((f32[32,8,2,128]{3,1,2,0:T(8,128)}), f32[32,8,2,128]{3,1,2,0:T(8,128)S(1)}, u32[]{:S(2)}, u32[]{:S(2)}) async-start(f32[32,8,2,128]{3,1,2,0:T(8,128)} %broadcast_in_dim.11), calls=%async_computation.2 | async-start | bytes 524288 | tf_op jit(solution)/shard_map/all_to_all | solution.py:237

commit v3 on v1

v3 whole, which is shorter than its diff:
```python
import math

import jax
import jax.numpy as jnp
from jax import lax
from jax.experimental import pallas as pl
from jax.experimental.pallas import tpu as pltpu
from jax.sharding import PartitionSpec as P

NPIX = 8192
KSUP = 8
NT = 16
TVG = 4
MOST = 4
FIELDS = 8
USED = 7
SENT = 6
CELLS = 16
CHUNK = 256

AXES = ("blen", "tm")
f32 = jnp.float32
bf16 = jnp.bfloat16
i32 = jnp.int32
NT_DIMS = (((1,), (1,)), ((), ()))
NN_DIMS = (((1,), (0,)), ((), ()))
MIB = 1 << 20


def params(mib):
    return pltpu.CompilerParams(vmem_limit_bytes=mib * MIB)


def split3(x):
    hi = x.astype(bf16)
    rest = x - hi.astype(f32)
    mid = rest.astype(bf16)
    low = (rest - mid.astype(f32)).astype(bf16)
    return hi, mid, low


def pattern(first, frac):
    cells = lax.broadcasted_iota(i32, (CELLS, first.shape[1]), 0)
    k = (cells - first) & (CELLS - 1)
    dist = (k - (KSUP // 2 - 1)).astype(f32) - frac
    value = jnp.where(k < KSUP, jnp.exp(-0.5 * dist * dist), 0.0).astype(bf16)
    return value, ((first + k) >> 4).astype(f32).astype(bf16)


def dense(value, where, side):
    zero = jnp.zeros_like(value)
    blocks = [jnp.where(where == jnp.bfloat16(b), value, zero) for b in range(side // CELLS)]
    return jnp.concatenate(blocks, axis=0)


def pack_body(tile_row, offset, frac, vis, weight, flag, packed, rank_out, *, devices, per_dev):
    n = tile_row.shape[1]
    t_row = tile_row[...]
    across = jnp.broadcast_to(t_row.astype(f32), (128, n)).T
    parts = []
    for c in range(n // 128):
        part = t_row[:, c * 128 : (c + 1) * 128].astype(f32)
        before = lax.broadcasted_iota(i32, (n, 128), 0)
        before = before < lax.broadcasted_iota(i32, (n, 128), 1) + c * 128
        same = jnp.where((across == part) & before, 1.0, 0.0)
        parts.append(jnp.sum(same, axis=0, keepdims=True))
    rank = jnp.concatenate(parts, axis=1).astype(i32)
    rank_out[...] = rank
    owner = t_row // per_dev
    local = t_row - owner * per_dev
    owners = lax.broadcasted_iota(i32, (devices, n), 0) == owner
    places = MOST * per_dev
    hot = lax.broadcasted_iota(i32, (places, n), 0) == rank * per_dev + local
    hot = hot.astype(f32).astype(bf16)
    rows = [
        offset[0:1, :].astype(f32),
        offset[1:2, :].astype(f32),
        frac[0:1, :],
        frac[1:2, :],
        vis[0:1, :],
        vis[1:2, :],
        weight[...] * flag[...].astype(f32),
    ]
    packed[...] = jnp.zeros(packed.shape, f32)
    for f in range(USED):
        spread = jnp.where(owners, rows[f], 0.0)
        total = jnp.zeros((devices, places), f32)
        for part in split3(spread):
            total = total + lax.dot_general(part, hot, NT_DIMS, preferred_element_type=f32)
        for k in range(MOST):
            at = (k * FIELDS + f) * per_dev
            packed[:, at : at + per_dev] = total[:, k * per_dev : (k + 1) * per_dev]


def predict_body(recv, model, sent, back, fields, *, per_dev):
    side = model.shape[2]
    lanes = back.shape[2]
    l = pl.program_id(0)

    @pl.when(l == 0)
    def _():
        turned = recv[...].T
        span = FIELDS * per_dev
        for k in range(MOST):
            some = turned[k * span : (k + 1) * span, :]
            width = some.shape[1]
            for t in range(per_dev):
                for f in range(FIELDS):
                    at = f * per_dev + t
                    fields[t, f : f + 1, k * width : (k + 1) * width] = some[at : at + 1, :]

    rows = fields[l]
    first = rows[0:2].astype(i32) - (KSUP // 2 - 1)
    ku = dense(*pattern(first[0:1], rows[2:3]), side)
    kv = dense(*pattern(first[1:2], rows[3:4]), side).astype(f32)
    residual = []
    for c in range(2):
        product = lax.dot_general(model[0, c], ku, NN_DIMS, preferred_element_type=f32)
        predicted = jnp.sum(product * kv, axis=0, keepdims=True)
        residual.append(rows[6:7] * (predicted - rows[4 + c : 5 + c]))
    back[0] = jnp.concatenate(residual, axis=0)
    there = rows[0:1] > 0.5
    above = lax.broadcasted_iota(i32, (lanes, lanes), 0) < lax.broadcasted_iota(i32, (lanes, lanes), 1)
    above = above.astype(f32).astype(bf16)
    ones = jnp.broadcast_to(there.astype(f32), (8, lanes)).astype(bf16)
    place = lax.dot_general(ones, above, NN_DIMS, preferred_element_type=f32)[0:1]
    place = jnp.where(there, place, -1.0).astype(i32)
    move = lax.broadcasted_iota(i32, (lanes, lanes), 0) == place
    move = move.astype(f32).astype(bf16)
    all_rows = jnp.concatenate([rows[0:4]] + residual + [jnp.zeros((2, lanes), f32)], axis=0)
    total = jnp.zeros((8, lanes), f32)
    for part in split3(all_rows):
        total = total + lax.dot_general(part, move, NT_DIMS, preferred_element_type=f32)
    sent[0] = total[0:SENT]


def fft_pos(z):
    n = len(z)
    if n == 1:
        return z
    even = fft_pos(z[0::2])
    odd = fft_pos(z[1::2])
    low, high = [], []
    for k in range(n // 2):
        o_re, o_im = odd[k]
        if k == 0:
            t_re, t_im = o_re, o_im
        elif 4 * k == n:
            t_re, t_im = -o_im, o_re
        else:
            c, s = math.cos(2 * math.pi * k / n), math.sin(2 * math.pi * k / n)
            t_re = o_re * c - o_im * s
            t_im = o_re * s + o_im * c
        e_re, e_im = even[k]
        low.append((e_re + t_re, e_im + t_im))
        high.append((e_re - t_re, e_im - t_im))
    return low + high


def image_body(
    counts, tiles, turn_u, rot, turn_v, twist, out,
    merged, kv_all, up_all, grid, turned, stage, sems, *flips,
):
    side = turn_u.shape[1]
    rows2 = turn_u.shape[0]
    rows = rows2 // 2
    lanes = tiles.shape[2]
    width = flips[0].shape[1]
    most = NT * lanes

    def tile_column(tv, carry):
        group = tv // TVG * (NT * TVG) + tv % TVG
        merged[...] = jnp.zeros(merged.shape, f32)
        used = jnp.int32(0)
        for tu in range(NT):
            tile = group + tu * TVG
            base = pl.multiple_of(used // 128 * 128, 128)
            cell = tiles[tile]
            tail = jnp.zeros((SENT, 128), f32)
            moved = pltpu.roll(jnp.concatenate([cell, tail], axis=1), used % 128, axis=1)
            at = (slice(0, SENT), pl.ds(base, lanes + 128))
            merged[at] = merged[at] + moved
            at = (slice(SENT, SENT + 1), pl.ds(base, lanes + 128))
            mark = jnp.full((1, lanes + 128), float(tu), f32)
            here = lax.broadcasted_iota(i32, mark.shape, 1) >= used % 128
            merged[at] = jnp.where(here, mark, merged[at])
            used = used + counts[tile]
        chunks = jnp.maximum(1, (used + CHUNK - 1) // CHUNK)

        def chunk(i, c):
            at = pl.multiple_of(i * CHUNK, CHUNK)
            m = merged[:, pl.ds(at, CHUNK)]
            first = m[0:2].astype(i32) - (KSUP // 2 - 1)
            ku = dense(*pattern(first[0:1], m[2:3]), side)
            kv_all[:, pl.ds(at, CHUNK)] = dense(*pattern(first[1:2], m[3:4]), side)
            v = lax.dot_general(turn_u[...], ku, NN_DIMS, preferred_element_type=f32)
            r_re = m[4:5] * (1.0 / NPIX)
            r_im = m[5:6] * (1.0 / NPIX)
            which = lax.broadcasted_iota(i32, (NT, CHUNK), 0).astype(f32) == m[6:7]
            which = which.astype(f32).astype(bf16)
            turn = jnp.zeros((2 * NT, CHUNK), f32)
            for j in range(3):
                turn = turn + lax.dot_general(rot[j], which, NN_DIMS, preferred_element_type=f32)
            cos_t, sin_t = turn[:NT], turn[NT:]
            c_re = (r_re * cos_t - r_im * sin_t)[None]
            c_im = (r_re * sin_t + r_im * cos_t)[None]
            v_re = v[:rows].reshape(rows // NT, NT, CHUNK)
            v_im = v[rows:].reshape(rows // NT, NT, CHUNK)
            u_re = (c_re * v_re - c_im * v_im).reshape(rows, CHUNK)
            u_im = (c_re * v_im + c_im * v_re).reshape(rows, CHUNK)
            up_all[0:rows, pl.ds(at, CHUNK)] = u_re.astype(bf16)
            up_all[rows:rows2, pl.ds(at, CHUNK)] = u_im.astype(bf16)
            return c

        lax.fori_loop(0, chunks, chunk, 0)

        if most // CHUNK <= 8:
            for n in range(1, most // CHUNK + 1):

                @pl.when(chunks == n)
                def _():
                    ft = lax.dot_general(
                        kv_all[:, 0 : n * CHUNK],
                        up_all[:, 0 : n * CHUNK],
                        NT_DIMS,
                        preferred_element_type=f32,
                    )
                    grid[tv] = ft.astype(bf16)

        else:

            def add(i, ft):
                at = pl.multiple_of(i * CHUNK, CHUNK)
                return ft + lax.dot_general(
                    kv_all[:, pl.ds(at, CHUNK)],
                    up_all[:, pl.ds(at, CHUNK)],
                    NT_DIMS,
                    preferred_element_type=f32,
                )

            ft = lax.fori_loop(0, chunks, add, jnp.zeros((side, rows2), f32))
            grid[tv] = ft.astype(bf16)
        return carry

    lax.fori_loop(0, NT, tile_column, 0)

    def stripe(j, carry):
        r0 = pl.multiple_of(j * 16, 16)
        tc = twist[0, pl.ds(r0, 16), :]
        ts = twist[1, pl.ds(r0, 16), :]
        for h in range(rows // width):
            c0 = h * width
            z = [
                (
                    grid[t, pl.ds(r0, 16), c0 : c0 + width].astype(f32),
                    grid[t, pl.ds(r0, 16), rows + c0 : rows + c0 + width].astype(f32),
                )
                for t in range(NT)
            ]
            x = fft_pos(z)
            for n0 in range(NT):
                re, im = x[n0]
                if n0 > 0:
                    c = tc[:, n0 : n0 + 1]
                    s = ts[:, n0 : n0 + 1]
                    re, im = re * c - im * s, re * s + im * c
                turned[n0, pl.ds(r0, 16), c0 : c0 + width] = re.astype(bf16)
                turned[n0, pl.ds(r0 + side, 16), c0 : c0 + width] = im.astype(bf16)
        return carry

    lax.fori_loop(0, side // 16, stripe, 0)

    for n0 in range(NT):
        x = lax.dot_general(turn_v[...], turned[n0], NN_DIMS, preferred_element_type=f32)
        for h in range(rows // width):
            flips[h][pl.ds(n0, side, stride=NT), :] = x[:, h * width : (h + 1) * width]

    pieces = sems.shape[0]
    wide = NPIX // pieces
    copies = []
    for i in range(pieces):
        for h in range(rows // width):
            stage[h * width : (h + 1) * width, i * wide : (i + 1) * wide] = (
                flips[h][i * wide : (i + 1) * wide, :].T
            )
        copy = pltpu.make_async_copy(
            stage.at[:, pl.ds(i * wide, wide)], out.at[:, pl.ds(i * wide, wide)], sems.at[i]
        )
        copy.start()
        copies.append(copy)
    for copy in copies:
        copy.wait()


def own_body(res, tile_row, rank, out, *, per_dev):
    devices = res.shape[0]
    n = tile_row.shape[1]
    t_row = tile_row[...]
    owner = t_row // per_dev
    local = t_row - owner * per_dev
    hot = lax.broadcasted_iota(i32, (devices, n), 0) == owner
    hot = hot.astype(f32).astype(bf16)
    places = MOST * per_dev
    mine = lax.broadcasted_iota(i32, (places, n), 0) == rank[...] * per_dev + local
    turned = res[...].T
    total = jnp.zeros((2 * places, n), f32)
    for part in split3(turned):
        total = total + lax.dot_general(part, hot, NN_DIMS, preferred_element_type=f32)
    for c in range(2):
        some = total[c * places : (c + 1) * places]
        out[c : c + 1, :] = jnp.sum(jnp.where(mine, some, 0.0), axis=0, keepdims=True)


def cos_sin(product, period):
    angle = (2.0 * math.pi / period) * (product % period).astype(f32)
    return jnp.cos(angle), jnp.sin(angle)


def exchange(x):
    return lax.all_to_all(x, AXES, split_axis=0, concat_axis=0, tiled=True)


def on_device(model_grid, vis_values, weights, flags, uv_frac, cell_offset, tile_index):
    devices = lax.axis_size("blen") * lax.axis_size("tm")
    me = lax.axis_index("blen") * lax.axis_size("tm") + lax.axis_index("tm")
    per_dev = model_grid.shape[0]
    side = model_grid.shape[2]
    n = weights.shape[0]
    ntiles = per_dev * devices
    lanes = devices * MOST
    rows = NPIX // devices
    call = pl.pallas_call
    shape = jax.ShapeDtypeStruct

    tile_row = tile_index.reshape(1, n)
    width = MOST * FIELDS * per_dev
    packed, rank = call(
        lambda *refs: pack_body(*refs, devices=devices, per_dev=per_dev),
        out_shape=(shape((devices, width), f32), shape((1, n), i32)),
        name="pack",
    )(tile_row, cell_offset, uv_frac, vis_values, weights.reshape(1, n), flags.reshape(1, n))
    recv = exchange(packed)
    sent, back = call(
        lambda *refs: predict_body(*refs, per_dev=per_dev),
        grid=(per_dev,),
        in_specs=[
            pl.BlockSpec((devices, width), lambda l: (0, 0)),
            pl.BlockSpec((1, 2, side, side), lambda l: (l, 0, 0, 0)),
        ],
        out_specs=(
            pl.BlockSpec((1, SENT, lanes), lambda l: (l, 0, 0)),
            pl.BlockSpec((1, 2, lanes), lambda l: (l, 0, 0)),
        ),
        out_shape=(shape((per_dev, SENT, lanes), f32), shape((per_dev, 2, lanes), f32)),
        scratch_shapes=[pltpu.VMEM((per_dev, FIELDS, lanes), f32)],
        compiler_params=params(32),
        name="predict",
    )(recv, model_grid)
    tiles = exchange(jnp.broadcast_to(sent[None], (devices,) + sent.shape))
    tiles = tiles.reshape(ntiles, SENT, lanes)
    counts = jnp.sum((tiles[:, 0, :] > 0.5).astype(i32), axis=1)
    back, counts = lax.optimization_barrier((back, counts))
    returned = back.reshape(per_dev, 2, MOST, devices).transpose(3, 1, 2, 0)
    returned = exchange(returned.reshape(devices, 2 * MOST * per_dev))

    image_rows = me * rows + jnp.arange(rows, dtype=i32)
    cells = jnp.arange(side, dtype=i32)
    small = jnp.arange(NT, dtype=i32)
    turn_u = jnp.concatenate(cos_sin(image_rows[:, None] * cells[None, :], NPIX)).astype(bf16)
    rot = jnp.stack(split3(jnp.concatenate(cos_sin(small[:, None] * small[None, :], NT))))
    cos_v, sin_v = cos_sin(cells[:, None] * cells[None, :], side)
    turn_v = jnp.concatenate([cos_v, -sin_v], axis=1).astype(bf16)
    twist = jnp.stack(cos_sin(cells[:, None] * small[None, :], NPIX))
    thin = min(128, rows)
    vmem = pl.BlockSpec(memory_space=pltpu.VMEM)
    gradient = call(
        image_body,
        in_specs=[pl.BlockSpec(memory_space=pltpu.SMEM)] + [vmem] * 5,
        out_specs=pl.BlockSpec(memory_space=pl.ANY),
        out_shape=shape((rows, NPIX), f32),
        scratch_shapes=[
            pltpu.VMEM((8, NT * lanes + 128), f32),
            pltpu.VMEM((side, NT * lanes), bf16),
            pltpu.VMEM((2 * rows, NT * lanes), bf16),
            pltpu.VMEM((NT, side, 2 * rows), bf16),
            pltpu.VMEM((NT, 2 * side, rows), bf16),
            pltpu.VMEM((rows, NPIX), f32),
            pltpu.SemaphoreType.DMA((8,)),
        ]
        + [pltpu.VMEM((NPIX, thin), f32)] * (rows // thin),
        compiler_params=params(56),
        name="image",
    )(counts, tiles, turn_u, rot, turn_v, twist)
    weighted_residual = call(
        lambda *refs: own_body(*refs, per_dev=per_dev),
        out_shape=shape((2, n), f32),
        name="own",
    )(returned, tile_row, rank)
    return (gradient, weighted_residual)


def solution(mesh):
    in_specs = (
        P(AXES, None, None, None),
        P(None, AXES),
        P(AXES),
        P(AXES),
        P(None, AXES),
        P(None, AXES),
        P(AXES, None),
    )
    out_specs = (P(AXES, None), P(None, AXES))
    return jax.shard_map(
        on_device, mesh=mesh, in_specs=in_specs, out_specs=out_specs, check_vma=False
    )
```

time: 247 us -> 136 us (0.55)
  Pallas kernels: 189 us -> 79.3 us
  blocking collectives: 0 us -> 14.4 us
  waiting for transfers between devices: 20 us -> 11.5 us
  starting transfers between devices: 12.5 us -> 6.35 us
  local copies, waits for them, and re-layouts: 13.2 us -> 7.74 us
  other arithmetic: 10.6 us -> 14.9 us
    pallas_call x5 -> x3, Pallas kernels: 187 us -> 77.4 us  [the longest x1 69.6 us: on_device(): call(image_body, in_specs=[pl.BlockSpec(memory_space=pltpu.SMEM)] + [vmem...]
    all_to_all x0 -> x1, blocking collectives: none -> 14.4 us  [exchange(): return lax.all_to_all(x, AXES, split_axis=0, concat_axis=0, tiled=True)]
    all_to_all x3 -> x2, waiting for transfers between devices: 20 us -> 11.5 us  [exchange(): return lax.all_to_all(x, AXES, split_axis=0, concat_axis=0, tiled=True)]
    all_to_all x3 -> x2, starting transfers between devices: 12.5 us -> 6.35 us  [exchange(): return lax.all_to_all(x, AXES, split_axis=0, concat_axis=0, tiled=True)]
    reduce_sum x0 -> x1, other arithmetic: none -> 5.24 us  [on_device(): counts = jnp.sum((tiles[:, 0, :] > 0.5).astype(i32), axis=1)]
    unnamed x12 -> x7, local copies, waits for them, and re-layouts: 6.97 us -> 3.98 us
    another operation x5 -> x4, other arithmetic: 7.94 us -> 7.42 us
  transfers between devices with their start and end apart: 3 -> 2, of which waited for: 3 -> 1; matrix products, arithmetic and copies ran while one was open for 5% -> 8% of each run, Pallas kernels for 1% -> 52%
where the time goes in v3:
time: 136 us; the launch traced here: 135 us
  Pallas kernels  79.3 us (58%)
  other arithmetic  14.9 us (11%)
  blocking collectives  14.4 us (11%)
  waiting for transfers between devices  11.5 us (8%)
  local copies, waits for them, and re-layouts  7.74 us (6%)
  starting transfers between devices  6.35 us (5%)
    pallas_call x1, Pallas kernels, on_device(): call(image_body, in_specs=[pl.BlockSpec(memory_space=pltpu.SMEM)] + [vmem...  69.6 us
    all_to_all x1, blocking collectives, exchange(): return lax.all_to_all(x, AXES, split_axis=0, concat_axis=0, tiled=True)  14.4 us
    all_to_all x2, waiting for transfers between devices, exchange(): return lax.all_to_all(x, AXES, split_axis=0, concat_axis=0, tiled=True)  11.5 us
    another operation x2, other arithmetic  6.8 us
    all_to_all x2, starting transfers between devices, exchange(): return lax.all_to_all(x, AXES, split_axis=0, concat_axis=0, tiled=True)  6.35 us
    pallas_call x1, Pallas kernels, on_device(): call(lambda *refs: predict_body(*refs, per_dev=per_dev), grid=(per_dev,),...  6.18 us
    reduce_sum x1, other arithmetic, on_device(): counts = jnp.sum((tiles[:, 0, :] > 0.5).astype(i32), axis=1)  5.24 us
    unnamed x7, local copies, waits for them, and re-layouts  3.98 us
  transfers between devices with their start and end apart: 2, of which 1 were waited for; matrix products, arithmetic and copies ran while one was open for 8% of the time, Pallas kernels for 52%

profile of v3, /device:TPU:0, one launch (start us, length us, event | category | flops | bytes accessed | tf_op | source)
XLA Modules:
  0.0 134.9 jit_solution(16377553536025248193)
XLA Ops:
  0.6 2.0 %pack.1 = (f32[32,256]{1,0:T(8,128)}, s32[1,512]{1,0:T(1,128)}) custom-call(s32[1,512]{1,0:T(1,128)} %bitcast.22, s32[2,512]{1,0:T(2,128)} %refs_1_.2, f32[2,512]{1,0:T(2,128)} %refs_2_.1, f32[2,512]{1,0:T(2,128)} %refs_3_.1, f32[1,512]{1,0:T(1,128)} %bitcast.24, s32[1,512]{1,0:T(1,128)} %bitcast.25), custom_call_target="tpu_custom_call" | custom-call | tf_op jit(solution)/shard_map/pack/pallas_call | solution.py:337
  2.6 0.8 copy.18
  3.4 14.4 %all_to_all.27 = f32[32,1,256]{2,1,0:T(1,128)S(1)} all-to-all(f32[32,1,256]{2,1,0:T(1,128)S(1)} %copy.18), channel_id=1, replica_groups=mesh['blen'=4,'tm'=8] {'blen','tm'}, dimensions={0} | all-to-all | bytes 65536 | tf_op jit(solution)/shard_map/all_to_all | solution.py:320
  17.8 0.0 copy-start
  17.8 3.4 %copy-done = bf16[8,2,512,512]{3,2,1,0:T(8,128)(2,1)S(1)} copy-done((bf16[8,2,512,512]{3,2,1,0:T(8,128)(2,1)S(1)}, bf16[8,2,512,512]{3,2,1,0:T(8,128)(2,1)}, u32[]{:S(2)}) %copy-start) | copy-done | bytes 8388632
  21.1 6.2 %predict.1 = (f32[8,6,128]{2,1,0:T(8,128)S(1)}, f32[8,2,128]{2,1,0:T(2,128)S(1)}) custom-call(f32[32,256]{1,0:T(8,128)S(1)} %bitcast.16, bf16[8,2,512,512]{3,2,1,0:T(8,128)(2,1)S(1)} %copy-done), custom_call_target="tpu_custom_call" | custom-call | tf_op jit(solution)/shard_map/predict/pallas_call | solution.py:343
  27.3 1.0 broadcast_in_dim.2
  28.3 2.6 %all-to-all-start.1 = ((f32[32,8,6,128]{3,1,2,0:T(8,128)}), f32[32,8,6,128]{3,1,2,0:T(8,128)S(1)}, u32[]{:S(2)}, u32[]{:S(2)}) async-start(f32[32,8,6,128]{3,1,2,0:T(8,128)} %broadcast_in_dim.2), calls=%async_computation.1 | async-start | bytes 1572864 | tf_op jit(solution)/shard_map/all_to_all | solution.py:320
  30.9 0.1 sine_bitcast_fusion
  31.0 0.1 fusion.19
  31.2 2.5 %cosine_convert_fusion.1 = (bf16[256,512]{1,0:T(8,128)(2,1)S(1)}, bf16[256,512]{1,0:T(8,128)(2,1)S(1)}) fusion(s32[256]{0:T(256)S(1)} %iota_add_fusion), kind=kLoop, calls=%fused_computation.20 | loop fusion | flops 2097152 | bytes 525312 | tf_op jit(solution)/shard_map/convert.2
  33.7 0.8 pad_maximum_fusion.1.turn_u
  34.5 4.3 %negate_convert_fusion = (bf16[512,512]{1,0:T(8,128)(2,1)S(1)}, bf16[512,512]{1,0:T(8,128)(2,1)S(1)}) fusion(), kind=kLoop, calls=%fused_computation.7 | loop fusion | flops 4456448 | bytes 1048576 | tf_op jit(solution)/shard_map/convert.1
  38.8 1.2 pad_maximum_fusion.turn_v
  40.0 11.5 %all-to-all-done.1 = f32[32,8,6,128]{3,1,2,0:T(8,128)S(1)} async-done(((f32[32,8,6,128]{3,1,2,0:T(8,128)}), f32[32,8,6,128]{3,1,2,0:T(8,128)S(1)}, u32[]{:S(2)}, u32[]{:S(2)}) %all-to-all-start.1) | async-done | bytes 786464 | tf_op jit(solution)/shard_map/all_to_all | solution.py:320
  51.5 0.2 copy.20
  51.7 0.0 copy-start.1
  51.7 5.2 %fusion.12.counts = s32[256]{0:T(256)} fusion(f32[256,6,128]{2,1,0:T(8,128)S(1)} %bitcast.17), kind=kLoop, calls=%fused_computation.25 | loop fusion | flops 98048 | bytes 132096 | tf_op jit(solution)/shard_map/reduce_sum | solution.py:361
  57.0 0.1 reshape.186
  57.1 0.7 copy.23
  57.8 3.7 %all-to-all-start.2 = ((f32[32,1,64]{2,1,0:T(1,128)}), f32[32,1,64]{2,1,0:T(1,128)S(1)}, u32[]{:S(2)}, u32[]{:S(2)}) async-start(f32[32,1,64]{2,1,0:T(1,128)} %copy.23), calls=%async_computation.2 | async-start | bytes 32768 | tf_op jit(solution)/shard_map/all_to_all | solution.py:320
  61.5 0.6 pad_maximum_fusion.3.rot
  62.1 1.0 copy.21.twist
  63.1 0.0 copy-done.1
  63.1 69.6 %image.1 = f32[256,8192]{1,0:T(8,128)} custom-call(s32[256]{0:T(256)} %fusion.12.counts, f32[256,6,128]{2,1,0:T(8,128)} %bitcast.18, bf16[512,512]{1,0:T(8,128)(2,1)} %pad_maximum_fusion.1.turn_u, bf16[3,32,16]{2,1,0:T(8,128)(2,1)} %pad_maximum_fusion.3.rot, bf16[512,1024]{1,0:T(8,128)(2,1)} %pad_maximum_fusion.turn_v, f32[2,512,16]{2,1,0:T(8,128)} %copy.21.twist), custom_call_target="tpu_custom_call" | custom-call | tf_op jit(solution)/shard_map/image/pallas_call | solution.py:376
  132.7 0.0 all-to-all-done.2
  132.8 0.0 copy-start.2
  132.8 0.6 copy-done.2
  133.4 1.6 %own.1 = f32[2,512]{1,0:T(2,128)} custom-call(f32[32,64]{1,0:T(8,128)} %bitcast.20, s32[1,512]{1,0:T(1,128)} %bitcast.23, s32[1,512]{1,0:T(1,128)} %get-tuple-element.13.refs_2_), custom_call_target="tpu_custom_call" | custom-call | tf_op jit(solution)/shard_map/own/pallas_call | solution.py:394
  (7 shorter events, 0.0 us)
Async XLA Ops:
  17.8 3.4 %copy-start = (bf16[8,2,512,512]{3,2,1,0:T(8,128)(2,1)S(1)}, bf16[8,2,512,512]{3,2,1,0:T(8,128)(2,1)}, u32[]{:S(2)}) copy-start(bf16[8,2,512,512]{3,2,1,0:T(8,128)(2,1)} %refs_1_.3) | copy-start | bytes 25165828
  28.3 23.2 %all-to-all-start.1 = ((f32[32,8,6,128]{3,1,2,0:T(8,128)}), f32[32,8,6,128]{3,1,2,0:T(8,128)S(1)}, u32[]{:S(2)}, u32[]{:S(2)}) async-start(f32[32,8,6,128]{3,1,2,0:T(8,128)} %broadcast_in_dim.2), calls=%async_computation.1 | async-start | bytes 1572864 | tf_op jit(solution)/shard_map/all_to_all | solution.py:320
  51.7 11.4 %copy-start.1 = (f32[32,8,6,128]{3,2,1,0:T(8,128)}, f32[32,8,6,128]{3,2,1,0:T(8,128)S(1)}, u32[]{:S(2)}) copy-start(f32[32,8,6,128]{3,2,1,0:T(8,128)S(1)} %copy.20) | copy-start | bytes 2359300
  57.8 75.0 %all-to-all-start.2 = ((f32[32,1,64]{2,1,0:T(1,128)}), f32[32,1,64]{2,1,0:T(1,128)S(1)}, u32[]{:S(2)}, u32[]{:S(2)}) async-start(f32[32,1,64]{2,1,0:T(1,128)} %copy.23), calls=%async_computation.2 | async-start | bytes 32768 | tf_op jit(solution)/shard_map/all_to_all | solution.py:320
  132.8 0.6 copy-start.2

commit v4 on v3

--- a/solution.py
+++ b/solution.py
@@ -113,25 +113,30 @@
     first = rows[0:2].astype(i32) - (KSUP // 2 - 1)
     ku = dense(*pattern(first[0:1], rows[2:3]), side)
     kv = dense(*pattern(first[1:2], rows[3:4]), side).astype(f32)
-    residual = []
     for c in range(2):
         product = lax.dot_general(model[0, c], ku, NN_DIMS, preferred_element_type=f32)
         predicted = jnp.sum(product * kv, axis=0, keepdims=True)
-        residual.append(rows[6:7] * (predicted - rows[4 + c : 5 + c]))
-    back[0] = jnp.concatenate(residual, axis=0)
-    there = rows[0:1] > 0.5
-    above = lax.broadcasted_iota(i32, (lanes, lanes), 0) < lax.broadcasted_iota(i32, (lanes, lanes), 1)
-    above = above.astype(f32).astype(bf16)
-    ones = jnp.broadcast_to(there.astype(f32), (8, lanes)).astype(bf16)
-    place = lax.dot_general(ones, above, NN_DIMS, preferred_element_type=f32)[0:1]
-    place = jnp.where(there, place, -1.0).astype(i32)
-    move = lax.broadcasted_iota(i32, (lanes, lanes), 0) == place
-    move = move.astype(f32).astype(bf16)
-    all_rows = jnp.concatenate([rows[0:4]] + residual + [jnp.zeros((2, lanes), f32)], axis=0)
-    total = jnp.zeros((8, lanes), f32)
-    for part in split3(all_rows):
-        total = total + lax.dot_general(part, move, NT_DIMS, preferred_element_type=f32)
-    sent[0] = total[0:SENT]
+        residual = rows[6:7] * (predicted - rows[4 + c : 5 + c])
+        fields[l, 4 + c : 5 + c, :] = residual
+        back[l, c : c + 1, :] = residual
+
+    @pl.when(l == per_dev - 1)
+    def _():
+        above = lax.broadcasted_iota(i32, (lanes, lanes), 0)
+        above = above < lax.broadcasted_iota(i32, (lanes, lanes), 1)
+        above = above.astype(f32).astype(bf16)
+        there = jnp.concatenate([fields[t, 0:1, :] for t in range(per_dev)], axis=0) > 0.5
+        place = lax.dot_general(
+            there.astype(f32).astype(bf16), above, NN_DIMS, preferred_element_type=f32
+        )
+        place = jnp.where(there, place, -1.0).astype(i32)
+        for t in range(per_dev):
+            move = lax.broadcasted_iota(i32, (lanes, lanes), 0) == place[t : t + 1]
+            move = move.astype(f32).astype(bf16)
+            parts = jnp.concatenate(split3(fields[t]), axis=0)
+            total = lax.dot_general(parts, move, NT_DIMS, preferred_element_type=f32)
+            total = total[0:8] + total[8:16] + total[16:24]
+            sent[t] = total[0:SENT]
 
 
 def fft_pos(z):
@@ -158,15 +163,54 @@
 
 
 def image_body(
-    counts, tiles, turn_u, rot, turn_v, twist, out,
-    merged, kv_all, up_all, grid, turned, stage, sems, *flips,
+    tiles, turn_u, rot, turn_v, twist, out,
+    merged, kv_all, up_all, grid, turned, stage, sems, tally, counts, *flips,
 ):
     side = turn_u.shape[1]
     rows2 = turn_u.shape[0]
     rows = rows2 // 2
     lanes = tiles.shape[2]
     width = flips[0].shape[1]
-    most = NT * lanes
+    most = NT * lanes // CHUNK
+
+    there = jnp.where(tiles[:, 0, :] > 0.5, 1.0, 0.0).astype(bf16)
+    total = lax.dot_general(
+        jnp.ones((8, lanes), bf16), there, NT_DIMS, preferred_element_type=f32
+    )
+    tally[...] = total.astype(i32)
+    count_copy = pltpu.make_async_copy(tally, counts, sems.at[0])
+    count_copy.start()
+    count_copy.wait()
+
+    def chunk(at):
+        m = merged[:, pl.ds(at, CHUNK)]
+        first = m[0:2].astype(i32) - (KSUP // 2 - 1)
+        ku = dense(*pattern(first[0:1], m[2:3]), side)
+        kv_all[:, pl.ds(at, CHUNK)] = dense(*pattern(first[1:2], m[3:4]), side)
+        v = lax.dot_general(turn_u[...], ku, NN_DIMS, preferred_element_type=f32)
+        r_re = m[4:5] * (1.0 / NPIX)
+        r_im = m[5:6] * (1.0 / NPIX)
+        which = lax.broadcasted_iota(i32, (NT, CHUNK), 0).astype(f32) == m[6:7]
+        which = which.astype(f32).astype(bf16)
+        which = jnp.concatenate([which] * 3, axis=0)
+        turn = lax.dot_general(rot[...], which, NN_DIMS, preferred_element_type=f32)
+        cos_t, sin_t = turn[:NT], turn[NT:]
+        c_re = (r_re * cos_t - r_im * sin_t)[None]
+        c_im = (r_re * sin_t + r_im * cos_t)[None]
+        v_re = v[:rows].reshape(rows // NT, NT, CHUNK)
+        v_im = v[rows:].reshape(rows // NT, NT, CHUNK)
+        u_re = (c_re * v_re - c_im * v_im).reshape(rows, CHUNK)
+        u_im = (c_re * v_im + c_im * v_re).reshape(rows, CHUNK)
+        up_all[0:rows, pl.ds(at, CHUNK)] = u_re.astype(bf16)
+        up_all[rows:rows2, pl.ds(at, CHUNK)] = u_im.astype(bf16)
+
+    def product(at, size):
+        return lax.dot_general(
+            kv_all[:, pl.ds(at, size)],
+            up_all[:, pl.ds(at, size)],
+            NT_DIMS,
+            preferred_element_type=f32,
+        )
 
     def tile_column(tv, carry):
         group = tv // TVG * (NT * TVG) + tv % TVG
@@ -174,70 +218,36 @@
         used = jnp.int32(0)
         for tu in range(NT):
             tile = group + tu * TVG
-            base = pl.multiple_of(used // 128 * 128, 128)
             cell = tiles[tile]
-            tail = jnp.zeros((SENT, 128), f32)
-            moved = pltpu.roll(jnp.concatenate([cell, tail], axis=1), used % 128, axis=1)
-            at = (slice(0, SENT), pl.ds(base, lanes + 128))
-            merged[at] = merged[at] + moved
-            at = (slice(SENT, SENT + 1), pl.ds(base, lanes + 128))
-            mark = jnp.full((1, lanes + 128), float(tu), f32)
-            here = lax.broadcasted_iota(i32, mark.shape, 1) >= used % 128
-            merged[at] = jnp.where(here, mark, merged[at])
-            used = used + counts[tile]
-        chunks = jnp.maximum(1, (used + CHUNK - 1) // CHUNK)
-
-        def chunk(i, c):
-            at = pl.multiple_of(i * CHUNK, CHUNK)
-            m = merged[:, pl.ds(at, CHUNK)]
-            first = m[0:2].astype(i32) - (KSUP // 2 - 1)
-            ku = dense(*pattern(first[0:1], m[2:3]), side)
-            kv_all[:, pl.ds(at, CHUNK)] = dense(*pattern(first[1:2], m[3:4]), side)
-            v = lax.dot_general(turn_u[...], ku, NN_DIMS, preferred_element_type=f32)
-            r_re = m[4:5] * (1.0 / NPIX)
-            r_im = m[5:6] * (1.0 / NPIX)
-            which = lax.broadcasted_iota(i32, (NT, CHUNK), 0).astype(f32) == m[6:7]
-            which = which.astype(f32).astype(bf16)
-            turn = jnp.zeros((2 * NT, CHUNK), f32)
-            for j in range(3):
-                turn = turn + lax.dot_general(rot[j], which, NN_DIMS, preferred_element_type=f32)
-            cos_t, sin_t = turn[:NT], turn[NT:]
-            c_re = (r_re * cos_t - r_im * sin_t)[None]
-            c_im = (r_re * sin_t + r_im * cos_t)[None]
-            v_re = v[:rows].reshape(rows // NT, NT, CHUNK)
-            v_im = v[rows:].reshape(rows // NT, NT, CHUNK)
-            u_re = (c_re * v_re - c_im * v_im).reshape(rows, CHUNK)
-            u_im = (c_re * v_im + c_im * v_re).reshape(rows, CHUNK)
-            up_all[0:rows, pl.ds(at, CHUNK)] = u_re.astype(bf16)
-            up_all[rows:rows2, pl.ds(at, CHUNK)] = u_im.astype(bf16)
-            return c
-
-        lax.fori_loop(0, chunks, chunk, 0)
-
-        if most // CHUNK <= 8:
-            for n in range(1, most // CHUNK + 1):
-
-                @pl.when(chunks == n)
+            mark = jnp.where(cell[0:1] > 0.5, float(tu), 0.0)
+            cell = jnp.concatenate([cell, mark, jnp.zeros((1, lanes), f32)], axis=0)
+            cell = jnp.concatenate([cell, jnp.zeros((8, 128), f32)], axis=1)
+            at = pl.ds(pl.multiple_of(used // 128 * 128, 128), lanes + 128)
+            merged[:, at] = merged[:, at] + pltpu.roll(cell, used % 128, axis=1)
+            used = used + counts[0, tile]
+        chunks = (used + CHUNK - 1) // CHUNK
+
+        if most == 8:
+            low = -1
+            for n in (2, 4, 5, 6, 8):
+
+                @pl.when((chunks > low) & (chunks <= n))
                 def _():
-                    ft = lax.dot_general(
-                        kv_all[:, 0 : n * CHUNK],
-                        up_all[:, 0 : n * CHUNK],
-                        NT_DIMS,
-                        preferred_element_type=f32,
-                    )
-                    grid[tv] = ft.astype(bf16)
-
+                    for i in range(n):
+                        chunk(i * CHUNK)
+                    grid[tv] = product(0, n * CHUNK).astype(bf16)
+
+                low = n
         else:
 
+            def make(i, c):
+                chunk(pl.multiple_of(i * CHUNK, CHUNK))
+                return c
+
             def add(i, ft):
-                at = pl.multiple_of(i * CHUNK, CHUNK)
-                return ft + lax.dot_general(
-                    kv_all[:, pl.ds(at, CHUNK)],
-                    up_all[:, pl.ds(at, CHUNK)],
-                    NT_DIMS,
-                    preferred_element_type=f32,
-                )
-
+                return ft + product(pl.multiple_of(i * CHUNK, CHUNK), CHUNK)
+
+            lax.fori_loop(0, chunks, make, 0)
             ft = lax.fori_loop(0, chunks, add, jnp.zeros((side, rows2), f32))
             grid[tv] = ft.astype(bf16)
         return carry
@@ -348,18 +358,17 @@
             pl.BlockSpec((1, 2, side, side), lambda l: (l, 0, 0, 0)),
         ],
         out_specs=(
-            pl.BlockSpec((1, SENT, lanes), lambda l: (l, 0, 0)),
-            pl.BlockSpec((1, 2, lanes), lambda l: (l, 0, 0)),
+            pl.BlockSpec((per_dev, SENT, lanes), lambda l: (0, 0, 0)),
+            pl.BlockSpec((per_dev, 2, lanes), lambda l: (0, 0, 0)),
         ),
         out_shape=(shape((per_dev, SENT, lanes), f32), shape((per_dev, 2, lanes), f32)),
         scratch_shapes=[pltpu.VMEM((per_dev, FIELDS, lanes), f32)],
         compiler_params=params(32),
         name="predict",
-    )(recv, model_grid)
+    )(recv, pltpu.with_memory_space_constraint(model_grid, pltpu.HBM))
     tiles = exchange(jnp.broadcast_to(sent[None], (devices,) + sent.shape))
     tiles = tiles.reshape(ntiles, SENT, lanes)
-    counts = jnp.sum((tiles[:, 0, :] > 0.5).astype(i32), axis=1)
-    back, counts = lax.optimization_barrier((back, counts))
+    back, tiles = lax.optimization_barrier((back, tiles))
     returned = back.reshape(per_dev, 2, MOST, devices).transpose(3, 1, 2, 0)
     returned = exchange(returned.reshape(devices, 2 * MOST * per_dev))
 
@@ -367,7 +376,8 @@
     cells = jnp.arange(side, dtype=i32)
     small = jnp.arange(NT, dtype=i32)
     turn_u = jnp.concatenate(cos_sin(image_rows[:, None] * cells[None, :], NPIX)).astype(bf16)
-    rot = jnp.stack(split3(jnp.concatenate(cos_sin(small[:, None] * small[None, :], NT))))
+    rot = cos_sin(small[:, None] * small[None, :], NT)
+    rot = jnp.concatenate(split3(jnp.concatenate(rot)), axis=1)
     cos_v, sin_v = cos_sin(cells[:, None] * cells[None, :], side)
     turn_v = jnp.concatenate([cos_v, -sin_v], axis=1).astype(bf16)
     twist = jnp.stack(cos_sin(cells[:, None] * small[None, :], NPIX))
@@ -375,7 +385,7 @@
     vmem = pl.BlockSpec(memory_space=pltpu.VMEM)
     gradient = call(
         image_body,
-        in_specs=[pl.BlockSpec(memory_space=pltpu.SMEM)] + [vmem] * 5,
+        in_specs=[vmem] * 5,
         out_specs=pl.BlockSpec(memory_space=pl.ANY),
         out_shape=shape((rows, NPIX), f32),
         scratch_shapes=[
@@ -386,11 +396,13 @@
             pltpu.VMEM((NT, 2 * side, rows), bf16),
             pltpu.VMEM((rows, NPIX), f32),
             pltpu.SemaphoreType.DMA((8,)),
+            pltpu.VMEM((8, ntiles), i32),
+            pltpu.SMEM((8, ntiles), i32),
         ]
         + [pltpu.VMEM((NPIX, thin), f32)] * (rows // thin),
         compiler_params=params(56),
         name="image",
-    )(counts, tiles, turn_u, rot, turn_v, twist)
+    )(tiles, turn_u, rot, turn_v, twist)
     weighted_residual = call(
         lambda *refs: own_body(*refs, per_dev=per_dev),
         out_shape=shape((2, n), f32),

time: 136 us -> 111 us (0.82)
  Pallas kernels: 79.3 us -> 62.5 us
  other arithmetic: 14.9 us -> 9.67 us
  local copies, waits for them, and re-layouts: 7.74 us -> 5.28 us
    pallas_call x1, Pallas kernels: 69.6 us -> 50.8 us  [on_device(): call(image_body, in_specs=[vmem] * 5, out_specs=pl.BlockSpec(memory_space...]
    reduce_sum x1 -> x0, other arithmetic: 5.24 us -> none  [on_device(): counts = jnp.sum((tiles[:, 0, :] > 0.5).astype(i32), axis=1)]
    unnamed x7 -> x3, local copies, waits for them, and re-layouts: 3.98 us -> 0.6 us
    pallas_call x1, Pallas kernels: 6.18 us -> 8.12 us  [on_device(): call(lambda *refs: predict_body(*refs, per_dev=per_dev), grid=(per_dev,),...]
    another operation x3 -> x2, other arithmetic: 7.41 us -> 6.8 us
  transfers between devices with their start and end apart: 2 -> 2, of which waited for: 1 -> 1; matrix products, arithmetic and copies ran while one was open for 8% -> 10% of each run, Pallas kernels for 52% -> 46%
where the time goes in v4:
time: 111 us; the launch traced here: 110 us
  Pallas kernels  62.5 us (56%)
  blocking collectives  14.4 us (13%)
  waiting for transfers between devices  11.5 us (10%)
  other arithmetic  9.67 us (9%)
  starting transfers between devices  6.35 us (6%)
  local copies, waits for them, and re-layouts  5.28 us (5%)
    pallas_call x1, Pallas kernels, on_device(): call(image_body, in_specs=[vmem] * 5, out_specs=pl.BlockSpec(memory_space...  50.8 us
    all_to_all x1, blocking collectives, exchange(): return lax.all_to_all(x, AXES, split_axis=0, concat_axis=0, tiled=True)  14.4 us
    all_to_all x2, waiting for transfers between devices, exchange(): return lax.all_to_all(x, AXES, split_axis=0, concat_axis=0, tiled=True)  11.5 us
    pallas_call x1, Pallas kernels, on_device(): call(lambda *refs: predict_body(*refs, per_dev=per_dev), grid=(per_dev,),...  8.12 us
    another operation x2, other arithmetic  6.8 us
    all_to_all x2, starting transfers between devices, exchange(): return lax.all_to_all(x, AXES, split_axis=0, concat_axis=0, tiled=True)  6.35 us
    all_to_all x3, local copies, waits for them, and re-layouts, exchange(): return lax.all_to_all(x, AXES, split_axis=0, concat_axis=0, tiled=True)  2.64 us
  transfers between devices with their start and end apart: 2, of which 1 were waited for; matrix products, arithmetic and copies ran while one was open for 10% of the time, Pallas kernels for 46%

profile of v4, /device:TPU:0, one launch (start us, length us, event | category | flops | bytes accessed | tf_op | source)
XLA Modules:
  0.0 110.4 jit_solution(572867968501191305)
XLA Ops:
  0.6 2.0 %pack.1 = (f32[32,256]{1,0:T(8,128)}, s32[1,512]{1,0:T(1,128)}) custom-call(s32[1,512]{1,0:T(1,128)} %bitcast.17, s32[2,512]{1,0:T(2,128)} %refs_1_.2, f32[2,512]{1,0:T(2,128)} %refs_2_.1, f32[2,512]{1,0:T(2,128)} %refs_3_.1, f32[1,512]{1,0:T(1,128)} %bitcast.19, s32[1,512]{1,0:T(1,128)} %bitcast.20), custom_call_target="tpu_custom_call" | custom-call | tf_op jit(solution)/shard_map/pack/pallas_call | solution.py:347
  2.6 0.8 copy.18
  3.4 14.4 %all_to_all.27 = f32[32,1,256]{2,1,0:T(1,128)S(1)} all-to-all(f32[32,1,256]{2,1,0:T(1,128)S(1)} %copy.18), channel_id=1, replica_groups=mesh['blen'=4,'tm'=8] {'blen','tm'}, dimensions={0} | all-to-all | bytes 65536 | tf_op jit(solution)/shard_map/all_to_all | solution.py:330
  17.8 8.1 %predict.1 = (f32[8,6,128]{2,1,0:T(8,128)S(1)}, f32[8,2,128]{2,1,0:T(2,128)S(1)}) custom-call(f32[32,256]{1,0:T(8,128)S(1)} %bitcast.12, bf16[8,2,512,512]{3,2,1,0:T(8,128)(2,1)} %refs_1_.3), custom_call_target="tpu_custom_call" | custom-call | tf_op jit(solution)/shard_map/predict/pallas_call | solution.py:353
  25.9 0.9 broadcast_in_dim.2
  26.8 2.6 %all-to-all-start.1 = ((f32[32,8,6,128]{3,1,2,0:T(8,128)}), f32[32,8,6,128]{3,1,2,0:T(8,128)S(1)}, u32[]{:S(2)}, u32[]{:S(2)}) async-start(f32[32,8,6,128]{3,1,2,0:T(8,128)} %broadcast_in_dim.2), calls=%async_computation.1 | async-start | bytes 1572864 | tf_op jit(solution)/shard_map/all_to_all | solution.py:330
  29.5 0.1 fusion.28
  29.6 0.1 fusion.18
  29.7 2.5 %cosine_convert_fusion.1 = (bf16[256,512]{1,0:T(8,128)(2,1)S(1)}, bf16[256,512]{1,0:T(8,128)(2,1)S(1)}) fusion(s32[256]{0:T(256)S(1)} %iota_add_fusion), kind=kLoop, calls=%fused_computation.20 | loop fusion | flops 2097152 | bytes 525312 | tf_op jit(solution)/shard_map/convert.2
  32.2 0.8 pad_maximum_fusion.1.turn_u
  33.0 4.3 %negate_convert_fusion = (bf16[512,512]{1,0:T(8,128)(2,1)S(1)}, bf16[512,512]{1,0:T(8,128)(2,1)S(1)}) fusion(), kind=kLoop, calls=%fused_computation.7 | loop fusion | flops 4456448 | bytes 1048576 | tf_op jit(solution)/shard_map/convert.1
  37.4 1.1 %pad_maximum_fusion.turn_v = bf16[512,1024]{1,0:T(8,128)(2,1)} fusion(bf16[512,512]{1,0:T(8,128)(2,1)S(1)} %get-tuple-element.20, bf16[512,512]{1,0:T(8,128)(2,1)S(1)} %get-tuple-element.21), kind=kLoop, calls=%fused_computation.6 | loop fusion | flops 2097152 | bytes 2097152 | tf_op jit(solution)/shard_map/concatenate | solution.py:382
  38.5 11.5 %all-to-all-done.1 = f32[32,8,6,128]{3,1,2,0:T(8,128)S(1)} async-done(((f32[32,8,6,128]{3,1,2,0:T(8,128)}), f32[32,8,6,128]{3,1,2,0:T(8,128)S(1)}, u32[]{:S(2)}, u32[]{:S(2)}) %all-to-all-start.1) | async-done | bytes 786464 | tf_op jit(solution)/shard_map/all_to_all | solution.py:330
  50.1 1.2 %copy.20 = f32[32,8,6,128]{3,2,1,0:T(8,128)} copy(f32[32,8,6,128]{3,1,2,0:T(8,128)S(1)} %all-to-all-done.1) | data formatting | bytes 1572864 | tf_op jit(solution)/shard_map/all_to_all | solution.py:330
  51.2 0.1 reshape.102
  51.3 0.7 copy.23
  52.0 3.7 %all-to-all-start.2 = ((f32[32,1,64]{2,1,0:T(1,128)}), f32[32,1,64]{2,1,0:T(1,128)S(1)}, u32[]{:S(2)}, u32[]{:S(2)}) async-start(f32[32,1,64]{2,1,0:T(1,128)} %copy.23), calls=%async_computation.2 | async-start | bytes 32768 | tf_op jit(solution)/shard_map/all_to_all | solution.py:330
  55.7 0.7 pad_maximum_fusion.4.rot
  56.4 1.0 copy.21.twist
  57.4 50.8 %image.1 = f32[256,8192]{1,0:T(8,128)} custom-call(f32[256,6,128]{2,1,0:T(8,128)} %bitcast.13, bf16[512,512]{1,0:T(8,128)(2,1)} %pad_maximum_fusion.1.turn_u, bf16[32,48]{1,0:T(8,128)(2,1)} %pad_maximum_fusion.4.rot, bf16[512,1024]{1,0:T(8,128)(2,1)} %pad_maximum_fusion.turn_v, f32[2,512,16]{2,1,0:T(8,128)} %copy.21.twist), custom_call_target="tpu_custom_call" | custom-call | tf_op jit(solution)/shard_map/image/pallas_call | solution.py:386
  108.2 0.0 all-to-all-done.2
  108.2 0.0 copy-start
  108.2 0.6 copy-done
  108.8 1.6 %own.1 = f32[2,512]{1,0:T(2,128)} custom-call(f32[32,64]{1,0:T(8,128)} %bitcast.15, s32[1,512]{1,0:T(1,128)} %bitcast.18, s32[1,512]{1,0:T(1,128)} %get-tuple-element.13.refs_2_), custom_call_target="tpu_custom_call" | custom-call | tf_op jit(solution)/shard_map/own/pallas_call | solution.py:406
  (7 shorter events, 0.0 us)
Async XLA Ops:
  26.8 23.2 %all-to-all-start.1 = ((f32[32,8,6,128]{3,1,2,0:T(8,128)}), f32[32,8,6,128]{3,1,2,0:T(8,128)S(1)}, u32[]{:S(2)}, u32[]{:S(2)}) async-start(f32[32,8,6,128]{3,1,2,0:T(8,128)} %broadcast_in_dim.2), calls=%async_computation.1 | async-start | bytes 1572864 | tf_op jit(solution)/shard_map/all_to_all | solution.py:330
  52.0 56.2 %all-to-all-start.2 = ((f32[32,1,64]{2,1,0:T(1,128)}), f32[32,1,64]{2,1,0:T(1,128)S(1)}, u32[]{:S(2)}, u32[]{:S(2)}) async-start(f32[32,1,64]{2,1,0:T(1,128)} %copy.23), calls=%async_computation.2 | async-start | bytes 32768 | tf_op jit(solution)/shard_map/all_to_all | solution.py:330
  108.2 0.6 copy-start

commit v5 on v4

--- a/solution.py
+++ b/solution.py
@@ -93,34 +93,35 @@
 
 
 def predict_body(recv, model, sent, back, fields, *, per_dev):
+    group = model.shape[0]
     side = model.shape[2]
-    lanes = back.shape[2]
-    l = pl.program_id(0)
-
-    @pl.when(l == 0)
+    lanes = sent.shape[1]
+    devices = recv.shape[0]
+    step = pl.program_id(0)
+
+    @pl.when(step == 0)
     def _():
         turned = recv[...].T
         span = FIELDS * per_dev
         for k in range(MOST):
             some = turned[k * span : (k + 1) * span, :]
-            width = some.shape[1]
             for t in range(per_dev):
                 for f in range(FIELDS):
                     at = f * per_dev + t
-                    fields[t, f : f + 1, k * width : (k + 1) * width] = some[at : at + 1, :]
-
-    rows = fields[l]
-    first = rows[0:2].astype(i32) - (KSUP // 2 - 1)
-    ku = dense(*pattern(first[0:1], rows[2:3]), side)
-    kv = dense(*pattern(first[1:2], rows[3:4]), side).astype(f32)
-    for c in range(2):
-        product = lax.dot_general(model[0, c], ku, NN_DIMS, preferred_element_type=f32)
-        predicted = jnp.sum(product * kv, axis=0, keepdims=True)
-        residual = rows[6:7] * (predicted - rows[4 + c : 5 + c])
-        fields[l, 4 + c : 5 + c, :] = residual
-        back[l, c : c + 1, :] = residual
-
-    @pl.when(l == per_dev - 1)
+                    fields[t, f : f + 1, k * devices : (k + 1) * devices] = some[at : at + 1, :]
+
+    for i in range(group):
+        l = step * group + i
+        rows = fields[l]
+        first = rows[0:2].astype(i32) - (KSUP // 2 - 1)
+        ku = dense(*pattern(first[0:1], rows[2:3]), side)
+        kv = dense(*pattern(first[1:2], rows[3:4]), side).astype(f32)
+        for c in range(2):
+            product = lax.dot_general(model[i, c], ku, NN_DIMS, preferred_element_type=f32)
+            predicted = jnp.sum(product * kv, axis=0, keepdims=True)
+            fields[l, 4 + c : 5 + c, :] = rows[6:7] * (predicted - rows[4 + c : 5 + c])
+
+    @pl.when(step == per_dev // group - 1)
     def _():
         above = lax.broadcasted_iota(i32, (lanes, lanes), 0)
         above = above < lax.broadcasted_iota(i32, (lanes, lanes), 1)
@@ -136,7 +137,13 @@
             parts = jnp.concatenate(split3(fields[t]), axis=0)
             total = lax.dot_general(parts, move, NT_DIMS, preferred_element_type=f32)
             total = total[0:8] + total[8:16] + total[16:24]
-            sent[t] = total[0:SENT]
+            sent[t * SENT : (t + 1) * SENT, :] = total[0:SENT]
+        mine = [fields[t, 4 + c : 5 + c, :] for c in range(2) for t in range(per_dev)]
+        turned = jnp.concatenate(mine, axis=0).T
+        back[...] = jnp.zeros(back.shape, f32)
+        wide = 2 * per_dev
+        for k in range(MOST):
+            back[:, k * wide : (k + 1) * wide] = turned[k * devices : (k + 1) * devices, :]
 
 
 def fft_pos(z):
@@ -163,23 +170,49 @@
 
 
 def image_body(
-    tiles, turn_u, rot, turn_v, twist, out,
-    merged, kv_all, up_all, grid, turned, stage, sems, tally, counts, *flips,
+    recv, tile_row, rank, turn_u, rot, turn_v, twist, out, own,
+    tiles, merged, kv_all, up_all, grid, turned, stage, sems, tally, counts, *flips,
 ):
     side = turn_u.shape[1]
     rows2 = turn_u.shape[0]
     rows = rows2 // 2
-    lanes = tiles.shape[2]
+    devices = recv.shape[0]
+    lanes = recv.shape[2]
+    per_dev = recv.shape[1] // SENT
     width = flips[0].shape[1]
     most = NT * lanes // CHUNK
 
-    there = jnp.where(tiles[:, 0, :] > 0.5, 1.0, 0.0).astype(bf16)
+    there = []
+    for l in range(per_dev):
+        some = recv[:, l * SENT : (l + 1) * SENT, :]
+        filled = some[:, 0:1, :] > 0.5
+        tile = lax.broadcasted_iota(i32, filled.shape, 0) * per_dev + l
+        mark = jnp.where(filled, (tile // TVG % NT).astype(f32), 0.0)
+        tiles[:, l] = jnp.concatenate([some, mark, jnp.zeros_like(mark)], axis=1)
+        there.append(jnp.where(filled[:, 0], 1.0, 0.0).astype(bf16))
     total = lax.dot_general(
-        jnp.ones((8, lanes), bf16), there, NT_DIMS, preferred_element_type=f32
+        jnp.ones((8, lanes), bf16),
+        jnp.concatenate(there, axis=0),
+        NT_DIMS,
+        preferred_element_type=f32,
     )
     tally[...] = total.astype(i32)
     count_copy = pltpu.make_async_copy(tally, counts, sems.at[0])
     count_copy.start()
+
+    n = tile_row.shape[1]
+    t_row = tile_row[...]
+    owner = t_row // per_dev
+    local = t_row - owner * per_dev
+    hot = lax.broadcasted_iota(i32, (devices, n), 0) == owner
+    hot = hot.astype(f32).astype(bf16)
+    mine = jnp.concatenate(split3(recv[:, per_dev * SENT, :].T), axis=0)
+    total = lax.dot_general(mine, hot, NN_DIMS, preferred_element_type=f32)
+    total = total[0:lanes] + total[lanes : 2 * lanes] + total[2 * lanes : 3 * lanes]
+    places = lax.broadcasted_iota(i32, (lanes, n), 0)
+    for c in range(2):
+        picked = places == (rank[...] * 2 + c) * per_dev + local
+        own[c : c + 1, :] = jnp.sum(jnp.where(picked, total, 0.0), axis=0, keepdims=True)
     count_copy.wait()
 
     def chunk(at):
@@ -197,8 +230,8 @@
         cos_t, sin_t = turn[:NT], turn[NT:]
         c_re = (r_re * cos_t - r_im * sin_t)[None]
         c_im = (r_re * sin_t + r_im * cos_t)[None]
-        v_re = v[:rows].reshape(rows // NT, NT, CHUNK)
-        v_im = v[rows:].reshape(rows // NT, NT, CHUNK)
+        v = v.reshape(rows // NT, 2, NT, CHUNK)
+        v_re, v_im = v[:, 0], v[:, 1]
         u_re = (c_re * v_re - c_im * v_im).reshape(rows, CHUNK)
         u_im = (c_re * v_im + c_im * v_re).reshape(rows, CHUNK)
         up_all[0:rows, pl.ds(at, CHUNK)] = u_re.astype(bf16)
@@ -218,13 +251,12 @@
         used = jnp.int32(0)
         for tu in range(NT):
             tile = group + tu * TVG
-            cell = tiles[tile]
-            mark = jnp.where(cell[0:1] > 0.5, float(tu), 0.0)
-            cell = jnp.concatenate([cell, mark, jnp.zeros((1, lanes), f32)], axis=0)
-            cell = jnp.concatenate([cell, jnp.zeros((8, 128), f32)], axis=1)
+            holder = tile // per_dev
+            local = tile % per_dev
+            cell = jnp.concatenate([tiles[holder, local], jnp.zeros((8, 128), f32)], axis=1)
             at = pl.ds(pl.multiple_of(used // 128 * 128, 128), lanes + 128)
             merged[:, at] = merged[:, at] + pltpu.roll(cell, used % 128, axis=1)
-            used = used + counts[0, tile]
+            used = used + counts[0, local * devices + holder]
         chunks = (used + CHUNK - 1) // CHUNK
 
         if most == 8:
@@ -302,25 +334,6 @@
         copy.wait()
 
 
-def own_body(res, tile_row, rank, out, *, per_dev):
-    devices = res.shape[0]
-    n = tile_row.shape[1]
-    t_row = tile_row[...]
-    owner = t_row // per_dev
-    local = t_row - owner * per_dev
-    hot = lax.broadcasted_iota(i32, (devices, n), 0) == owner
-    hot = hot.astype(f32).astype(bf16)
-    places = MOST * per_dev
-    mine = lax.broadcasted_iota(i32, (places, n), 0) == rank[...] * per_dev + local
-    turned = res[...].T
-    total = jnp.zeros((2 * places, n), f32)
-    for part in split3(turned):
-        total = total + lax.dot_general(part, hot, NN_DIMS, preferred_element_type=f32)
-    for c in range(2):
-        some = total[c * places : (c + 1) * places]
-        out[c : c + 1, :] = jnp.sum(jnp.where(mine, some, 0.0), axis=0, keepdims=True)
-
-
 def cos_sin(product, period):
     angle = (2.0 * math.pi / period) * (product % period).astype(f32)
     return jnp.cos(angle), jnp.sin(angle)
@@ -350,45 +363,48 @@
         name="pack",
     )(tile_row, cell_offset, uv_frac, vis_values, weights.reshape(1, n), flags.reshape(1, n))
     recv = exchange(packed)
-    sent, back = call(
-        lambda *refs: predict_body(*refs, per_dev=per_dev),
-        grid=(per_dev,),
-        in_specs=[
-            pl.BlockSpec((devices, width), lambda l: (0, 0)),
-            pl.BlockSpec((1, 2, side, side), lambda l: (l, 0, 0, 0)),
-        ],
-        out_specs=(
-            pl.BlockSpec((per_dev, SENT, lanes), lambda l: (0, 0, 0)),
-            pl.BlockSpec((per_dev, 2, lanes), lambda l: (0, 0, 0)),
-        ),
-        out_shape=(shape((per_dev, SENT, lanes), f32), shape((per_dev, 2, lanes), f32)),
-        scratch_shapes=[pltpu.VMEM((per_dev, FIELDS, lanes), f32)],
-        compiler_params=params(32),
-        name="predict",
-    )(recv, pltpu.with_memory_space_constraint(model_grid, pltpu.HBM))
-    tiles = exchange(jnp.broadcast_to(sent[None], (devices,) + sent.shape))
-    tiles = tiles.reshape(ntiles, SENT, lanes)
-    back, tiles = lax.optimization_barrier((back, tiles))
-    returned = back.reshape(per_dev, 2, MOST, devices).transpose(3, 1, 2, 0)
-    returned = exchange(returned.reshape(devices, 2 * MOST * per_dev))
-
     image_rows = me * rows + jnp.arange(rows, dtype=i32)
     cells = jnp.arange(side, dtype=i32)
     small = jnp.arange(NT, dtype=i32)
-    turn_u = jnp.concatenate(cos_sin(image_rows[:, None] * cells[None, :], NPIX)).astype(bf16)
+    turn_u = cos_sin((image_rows[:, None] * cells[None, :]).reshape(rows // NT, NT, side), NPIX)
+    turn_u = jnp.stack(turn_u, axis=1).reshape(2 * rows, side).astype(bf16)
     rot = cos_sin(small[:, None] * small[None, :], NT)
     rot = jnp.concatenate(split3(jnp.concatenate(rot)), axis=1)
     cos_v, sin_v = cos_sin(cells[:, None] * cells[None, :], side)
     turn_v = jnp.concatenate([cos_v, -sin_v], axis=1).astype(bf16)
     twist = jnp.stack(cos_sin(cells[:, None] * small[None, :], NPIX))
+    recv, turn_u, rot, turn_v, twist = lax.optimization_barrier((recv, turn_u, rot, turn_v, twist))
+
+    group = min(2, per_dev)
+    sent, back = call(
+        lambda *refs: predict_body(*refs, per_dev=per_dev),
+        grid=(per_dev // group,),
+        in_specs=[
+            pl.BlockSpec((devices, width), lambda l: (0, 0)),
+            pl.BlockSpec((group, 2, side, side), lambda l: (l, 0, 0, 0)),
+        ],
+        out_specs=(
+            pl.BlockSpec((per_dev * SENT, lanes), lambda l: (0, 0)),
+            pl.BlockSpec((devices, lanes), lambda l: (0, 0)),
+        ),
+        out_shape=(shape((per_dev * SENT, lanes), f32), shape((devices, lanes), f32)),
+        scratch_shapes=[pltpu.VMEM((per_dev, FIELDS, lanes), f32)],
+        compiler_params=params(32),
+        name="predict",
+    )(recv, pltpu.with_memory_space_constraint(model_grid, pltpu.HBM))
+    sent = jnp.broadcast_to(sent[None], (devices,) + sent.shape)
+    tiles = exchange(jnp.concatenate([sent, back[:, None, :]], axis=1))
+    tiles = pltpu.with_memory_space_constraint(tiles, pltpu.HBM)
+
     thin = min(128, rows)
     vmem = pl.BlockSpec(memory_space=pltpu.VMEM)
-    gradient = call(
+    gradient, weighted_residual = call(
         image_body,
-        in_specs=[vmem] * 5,
-        out_specs=pl.BlockSpec(memory_space=pl.ANY),
-        out_shape=shape((rows, NPIX), f32),
+        in_specs=[vmem] * 7,
+        out_specs=(pl.BlockSpec(memory_space=pl.ANY), vmem),
+        out_shape=(shape((rows, NPIX), f32), shape((2, n), f32)),
         scratch_shapes=[
+            pltpu.VMEM((devices, per_dev, 8, lanes), f32),
             pltpu.VMEM((8, NT * lanes + 128), f32),
             pltpu.VMEM((side, NT * lanes), bf16),
             pltpu.VMEM((2 * rows, NT * lanes), bf16),
@@ -402,12 +418,7 @@
         + [pltpu.VMEM((NPIX, thin), f32)] * (rows // thin),
         compiler_params=params(56),
         name="image",
-    )(tiles, turn_u, rot, turn_v, twist)
-    weighted_residual = call(
-        lambda *refs: own_body(*refs, per_dev=per_dev),
-        out_shape=shape((2, n), f32),
-        name="own",
-    )(returned, tile_row, rank)
+    )(tiles, tile_row, rank, turn_u, rot, turn_v, twist)
     return (gradient, weighted_residual)
 
 

time: 111 us -> 112 us (level)
  blocking collectives: 14.4 us -> 0 us
  waiting for transfers between devices: 11.5 us -> 22.2 us
  starting transfers between devices: 6.35 us -> 13.3 us
  Pallas kernels: 62.5 us -> 60.1 us
  local copies, waits for them, and re-layouts: 5.28 us -> 3.43 us
    all_to_all x1 -> x0, blocking collectives: 14.4 us -> none  [exchange(): return lax.all_to_all(x, AXES, split_axis=0, concat_axis=0, tiled=True)]
    all_to_all x2, waiting for transfers between devices: 11.5 us -> 22.2 us  [exchange(): return lax.all_to_all(x, AXES, split_axis=0, concat_axis=0, tiled=True)]
    all_to_all x2, starting transfers between devices: 6.35 us -> 13.3 us  [exchange(): return lax.all_to_all(x, AXES, split_axis=0, concat_axis=0, tiled=True)]
    pallas_call x3 -> x2, Pallas kernels: 60.5 us -> 58.1 us  [the longest x1 51.9 us: on_device(): call(image_body, in_specs=[vmem] * 7, out_specs=(pl.BlockSpec(memory_spac...]
    all_to_all x3 -> x1, local copies, waits for them, and re-layouts: 2.64 us -> 1.39 us  [exchange(): return lax.all_to_all(x, AXES, split_axis=0, concat_axis=0, tiled=True)]
    another operation x2 -> x3, other arithmetic: 6.8 us -> 7.64 us
  transfers between devices with their start and end apart: 2 -> 2, of which waited for: 1 -> 1; matrix products, arithmetic and copies ran while one was open for 10% -> 10% of each run, Pallas kernels for 46% -> 0%
where the time goes in v5:
time: 112 us; the launch traced here: 111 us
  Pallas kernels  60.1 us (54%)
  waiting for transfers between devices  22.2 us (20%)
  starting transfers between devices  13.3 us (12%)
  other arithmetic  10.7 us (10%)
  local copies, waits for them, and re-layouts  3.43 us (3%)
    pallas_call x1, Pallas kernels, on_device(): call(image_body, in_specs=[vmem] * 7, out_specs=(pl.BlockSpec(memory_spac...  51.9 us
    all_to_all x2, waiting for transfers between devices, exchange(): return lax.all_to_all(x, AXES, split_axis=0, concat_axis=0, tiled=True)  22.2 us
    all_to_all x2, starting transfers between devices, exchange(): return lax.all_to_all(x, AXES, split_axis=0, concat_axis=0, tiled=True)  13.3 us
    another operation x2, other arithmetic  6.79 us
    pallas_call x1, Pallas kernels, on_device(): call(lambda *refs: predict_body(*refs, per_dev=per_dev), grid=(per_dev //...  6.21 us
  transfers between devices with their start and end apart: 2, of which 1 were waited for; matrix products, arithmetic and copies ran while one was open for 10% of the time, Pallas kernels for 0%

profile of v5, /device:TPU:0, one launch (start us, length us, event | category | flops | bytes accessed | tf_op | source)
XLA Modules:
  0.0 110.6 jit_solution(10211070725698633181)
XLA Ops:
  0.6 2.0 %pack.1 = (f32[32,256]{1,0:T(8,128)}, s32[1,512]{1,0:T(1,128)}) custom-call(s32[1,512]{1,0:T(1,128)} %bitcast.13, s32[2,512]{1,0:T(2,128)} %refs_1_.2, f32[2,512]{1,0:T(2,128)} %refs_2_.1, f32[2,512]{1,0:T(2,128)} %refs_3_.1, f32[1,512]{1,0:T(1,128)} %bitcast.15, s32[1,512]{1,0:T(1,128)} %bitcast.16), custom_call_target="tpu_custom_call" | custom-call | tf_op jit(solution)/shard_map/pack/pallas_call | solution.py:360
  2.6 1.4 %copy.11 = f32[32,1,256]{2,1,0:T(1,128)} copy(f32[32,1,256]{2,0,1:T(8,128)} %bitcast.12) | data formatting | bytes 65536 | tf_op jit(solution)/shard_map/all_to_all | solution.py:343
  4.0 7.3 %all-to-all-start = ((f32[32,1,256]{2,1,0:T(1,128)}), f32[32,1,256]{2,1,0:T(1,128)S(1)}, u32[]{:S(2)}, u32[]{:S(2)}) async-start(f32[32,1,256]{2,1,0:T(1,128)} %copy.11), calls=%async_computation | async-start | bytes 65536 | tf_op jit(solution)/shard_map/all_to_all | solution.py:343
  11.3 0.1 fusion.28
  11.4 0.1 fusion.18
  11.5 4.3 %negate_convert_fusion = (bf16[512,512]{1,0:T(8,128)(2,1)S(1)}, bf16[512,512]{1,0:T(8,128)(2,1)S(1)}) fusion(), kind=kLoop, calls=%fused_computation.7 | loop fusion | flops 4456448 | bytes 1048576 | tf_op jit(solution)/shard_map/convert.1
  15.9 2.4 %cosine_convert_fusion.1 = (bf16[16,1,16,512]{3,2,1,0:T(8,128)(2,1)S(1)}, bf16[16,1,16,512]{3,2,1,0:T(8,128)(2,1)S(1)}) fusion(s32[16,16]{1,0:T(8,128)S(1)} %add_add_fusion), kind=kLoop, calls=%fused_computation.21 | loop fusion | flops 2097152 | bytes 525312 | tf_op jit(solution)/shard_map/convert.2
  18.4 0.8 pad_maximum_fusion.2
  19.2 1.1 %pad_maximum_fusion.turn_v = bf16[512,1024]{1,0:T(8,128)(2,1)} fusion(bf16[512,512]{1,0:T(8,128)(2,1)S(1)} %get-tuple-element.26, bf16[512,512]{1,0:T(8,128)(2,1)S(1)} %get-tuple-element.27), kind=kLoop, calls=%fused_computation.6 | loop fusion | flops 2097152 | bytes 2097152 | tf_op jit(solution)/shard_map/concatenate | solution.py:374
  20.4 0.7 pad_maximum_fusion.5.rot
  21.0 0.0 all-to-all-done
  21.0 6.2 %predict.1 = (f32[48,128]{1,0:T(8,128)S(1)}, f32[32,128]{1,0:T(8,128)S(1)}) custom-call(f32[32,256]{1,0:T(8,128)S(1)} %bitcast.9, bf16[8,2,512,512]{3,2,1,0:T(8,128)(2,1)} %refs_1_.3), custom_call_target="tpu_custom_call" | custom-call | tf_op jit(solution)/shard_map/predict/pallas_call | solution.py:379
  27.3 0.1 broadcast_in_dim.4
  27.3 1.0 pad_maximum_fusion.1
  28.3 6.0 %all-to-all-start.1 = ((f32[32,49,128]{2,1,0:T(8,128)}), f32[32,49,128]{2,1,0:T(8,128)S(1)}, u32[]{:S(2)}, u32[]{:S(2)}) async-start(f32[32,49,128]{2,1,0:T(8,128)} %pad_maximum_fusion.1), calls=%async_computation.1 | async-start | bytes 1835008 | tf_op jit(solution)/shard_map/all_to_all | solution.py:343
  34.3 1.0 copy.12.twist
  35.3 22.2 %all-to-all-done.1.recv = f32[32,49,128]{2,1,0:T(8,128)S(1)} async-done(((f32[32,49,128]{2,1,0:T(8,128)}), f32[32,49,128]{2,1,0:T(8,128)S(1)}, u32[]{:S(2)}, u32[]{:S(2)}) %all-to-all-start.1) | async-done | bytes 802848 | tf_op jit(solution)/shard_map/all_to_all | solution.py:343
  57.6 0.0 copy-start
  57.6 1.0 copy-done
  58.5 51.9 %image.1 = (f32[256,8192]{1,0:T(8,128)}, f32[2,512]{1,0:T(2,128)}) custom-call(f32[32,49,128]{2,1,0:T(8,128)} %copy-done, s32[1,512]{1,0:T(1,128)} %bitcast.14, s32[1,512]{1,0:T(1,128)} %get-tuple-element.15.rank, bf16[512,512]{1,0:T(8,128)(2,1)} %bitcast.11, bf16[32,48]{1,0:T(8,128)(2,1)} %pad_maximum_fusion.5.rot, ...), custom_call_target="tpu_custom_call" | custom-call | tf_op jit(solution)/shard_map/image/pallas_call | solution.py:401
  (5 shorter events, 0.0 us)
Async XLA Ops:
  4.0 17.0 %all-to-all-start = ((f32[32,1,256]{2,1,0:T(1,128)}), f32[32,1,256]{2,1,0:T(1,128)S(1)}, u32[]{:S(2)}, u32[]{:S(2)}) async-start(f32[32,1,256]{2,1,0:T(1,128)} %copy.11), calls=%async_computation | async-start | bytes 65536 | tf_op jit(solution)/shard_map/all_to_all | solution.py:343
  28.3 29.3 %all-to-all-start.1 = ((f32[32,49,128]{2,1,0:T(8,128)}), f32[32,49,128]{2,1,0:T(8,128)S(1)}, u32[]{:S(2)}, u32[]{:S(2)}) async-start(f32[32,49,128]{2,1,0:T(8,128)} %pad_maximum_fusion.1), calls=%async_computation.1 | async-start | bytes 1835008 | tf_op jit(solution)/shard_map/all_to_all | solution.py:343
  57.6 1.0 copy-start

commit v6 on v5

--- a/solution.py
+++ b/solution.py
@@ -5,6 +5,7 @@
 from jax import lax
 from jax.experimental import pallas as pl
 from jax.experimental.pallas import tpu as pltpu
+from jax.sharding import Mesh
 from jax.sharding import PartitionSpec as P
 
 NPIX = 8192
@@ -18,7 +19,8 @@
 CELLS = 16
 CHUNK = 256
 
-AXES = ("blen", "tm")
+AXES = ("blen", "chip", "core")
+CORES = 2
 f32 = jnp.float32
 bf16 = jnp.bfloat16
 i32 = jnp.int32
@@ -89,10 +91,10 @@
             total = total + lax.dot_general(part, hot, NT_DIMS, preferred_element_type=f32)
         for k in range(MOST):
             at = (k * FIELDS + f) * per_dev
-            packed[:, at : at + per_dev] = total[:, k * per_dev : (k + 1) * per_dev]
-
-
-def predict_body(recv, model, sent, back, fields, *, per_dev):
+            packed[:, 0, at : at + per_dev] = total[:, k * per_dev : (k + 1) * per_dev]
+
+
+def predict_body(recv, model, sent, back, fields, flip, *, per_dev):
     group = model.shape[0]
     side = model.shape[2]
     lanes = sent.shape[1]
@@ -139,11 +141,14 @@
             total = total[0:8] + total[8:16] + total[16:24]
             sent[t * SENT : (t + 1) * SENT, :] = total[0:SENT]
         mine = [fields[t, 4 + c : 5 + c, :] for c in range(2) for t in range(per_dev)]
-        turned = jnp.concatenate(mine, axis=0).T
+        wide = 2 * per_dev
+        flip[:, 0:wide] = jnp.concatenate(mine, axis=0).T
         back[...] = jnp.zeros(back.shape, f32)
-        wide = 2 * per_dev
-        for k in range(MOST):
-            back[:, k * wide : (k + 1) * wide] = turned[k * devices : (k + 1) * devices, :]
+        for core in range(CORES):
+            for k in range(MOST):
+                some = flip[pl.ds(k * devices + core, devices // CORES, stride=CORES), :]
+                at = (core * MOST + k) * wide
+                back[:, at : at + wide] = some[:, 0:wide]
 
 
 def fft_pos(z):
@@ -170,26 +175,29 @@
 
 
 def image_body(
-    recv, tile_row, rank, turn_u, rot, turn_v, twist, out, own,
+    core, near, far, tile_row, rank, turn_u, rot, turn_v, twist, out, own,
     tiles, merged, kv_all, up_all, grid, turned, stage, sems, tally, counts, *flips,
 ):
     side = turn_u.shape[1]
     rows2 = turn_u.shape[0]
     rows = rows2 // 2
-    devices = recv.shape[0]
-    lanes = recv.shape[2]
-    per_dev = recv.shape[1] // SENT
+    chips = near.shape[0]
+    lanes = near.shape[2]
+    per_dev = near.shape[1] // SENT
     width = flips[0].shape[1]
     most = NT * lanes // CHUNK
 
     there = []
-    for l in range(per_dev):
-        some = recv[:, l * SENT : (l + 1) * SENT, :]
-        filled = some[:, 0:1, :] > 0.5
-        tile = lax.broadcasted_iota(i32, filled.shape, 0) * per_dev + l
-        mark = jnp.where(filled, (tile // TVG % NT).astype(f32), 0.0)
-        tiles[:, l] = jnp.concatenate([some, mark, jnp.zeros_like(mark)], axis=1)
-        there.append(jnp.where(filled[:, 0], 1.0, 0.0).astype(bf16))
+    for far_off, recv in enumerate((near, far)):
+        from_core = core[0] if far_off == 0 else 1 - core[0]
+        for l in range(per_dev):
+            some = recv[:, l * SENT : (l + 1) * SENT, :]
+            filled = some[:, 0:1, :] > 0.5
+            owner = lax.broadcasted_iota(i32, filled.shape, 0) * CORES + from_core
+            tile = owner * per_dev + l
+            mark = jnp.where(filled, (tile // TVG % NT).astype(f32), 0.0)
+            tiles[far_off, l] = jnp.concatenate([some, mark, jnp.zeros_like(mark)], axis=1)
+            there.append(jnp.where(filled[:, 0], 1.0, 0.0).astype(bf16))
     total = lax.dot_general(
         jnp.ones((8, lanes), bf16),
         jnp.concatenate(there, axis=0),
@@ -204,14 +212,18 @@
     t_row = tile_row[...]
     owner = t_row // per_dev
     local = t_row - owner * per_dev
-    hot = lax.broadcasted_iota(i32, (devices, n), 0) == owner
-    hot = hot.astype(f32).astype(bf16)
-    mine = jnp.concatenate(split3(recv[:, per_dev * SENT, :].T), axis=0)
-    total = lax.dot_general(mine, hot, NN_DIMS, preferred_element_type=f32)
+    span = MOST * 2 * per_dev
+    total = jnp.zeros((3 * lanes, n), f32)
+    for far_off, recv in enumerate((near, far)):
+        from_core = core[0] if far_off == 0 else 1 - core[0]
+        hot = lax.broadcasted_iota(i32, (chips, n), 0) * CORES + from_core == owner
+        hot = hot.astype(f32).astype(bf16)
+        mine = jnp.concatenate(split3(recv[:, per_dev * SENT, :].T), axis=0)
+        total = total + lax.dot_general(mine, hot, NN_DIMS, preferred_element_type=f32)
     total = total[0:lanes] + total[lanes : 2 * lanes] + total[2 * lanes : 3 * lanes]
     places = lax.broadcasted_iota(i32, (lanes, n), 0)
     for c in range(2):
-        picked = places == (rank[...] * 2 + c) * per_dev + local
+        picked = places == core[0] * span + (rank[...] * 2 + c) * per_dev + local
         own[c : c + 1, :] = jnp.sum(jnp.where(picked, total, 0.0), axis=0, keepdims=True)
     count_copy.wait()
 
@@ -251,12 +263,15 @@
         used = jnp.int32(0)
         for tu in range(NT):
             tile = group + tu * TVG
-            holder = tile // per_dev
+            owner = tile // per_dev
             local = tile % per_dev
-            cell = jnp.concatenate([tiles[holder, local], jnp.zeros((8, 128), f32)], axis=1)
+            far_off = (owner + core[0]) % CORES
+            chip = owner // CORES
+            cell = tiles[far_off, local, chip]
+            cell = jnp.concatenate([cell, jnp.zeros((8, 128), f32)], axis=1)
             at = pl.ds(pl.multiple_of(used // 128 * 128, 128), lanes + 128)
             merged[:, at] = merged[:, at] + pltpu.roll(cell, used % 128, axis=1)
-            used = used + counts[0, local * devices + holder]
+            used = used + counts[0, (far_off * per_dev + local) * chips + chip]
         chunks = (used + CHUNK - 1) // CHUNK
 
         if most == 8:
@@ -339,13 +354,11 @@
     return jnp.cos(angle), jnp.sin(angle)
 
 
-def exchange(x):
-    return lax.all_to_all(x, AXES, split_axis=0, concat_axis=0, tiled=True)
-
-
 def on_device(model_grid, vis_values, weights, flags, uv_frac, cell_offset, tile_index):
-    devices = lax.axis_size("blen") * lax.axis_size("tm")
-    me = lax.axis_index("blen") * lax.axis_size("tm") + lax.axis_index("tm")
+    chips = lax.axis_size("blen") * lax.axis_size("chip")
+    devices = chips * CORES
+    core = lax.axis_index("core")
+    me = (lax.axis_index("blen") * lax.axis_size("chip") + lax.axis_index("chip")) * CORES + core
     per_dev = model_grid.shape[0]
     side = model_grid.shape[2]
     n = weights.shape[0]
@@ -359,10 +372,11 @@
     width = MOST * FIELDS * per_dev
     packed, rank = call(
         lambda *refs: pack_body(*refs, devices=devices, per_dev=per_dev),
-        out_shape=(shape((devices, width), f32), shape((1, n), i32)),
+        out_shape=(shape((devices, 1, width), f32), shape((1, n), i32)),
         name="pack",
     )(tile_row, cell_offset, uv_frac, vis_values, weights.reshape(1, n), flags.reshape(1, n))
-    recv = exchange(packed)
+    recv = lax.all_to_all(packed, AXES, split_axis=0, concat_axis=0, tiled=True)
+    recv = recv.reshape(devices, width)
     image_rows = me * rows + jnp.arange(rows, dtype=i32)
     cells = jnp.arange(side, dtype=i32)
     small = jnp.arange(NT, dtype=i32)
@@ -373,7 +387,7 @@
     cos_v, sin_v = cos_sin(cells[:, None] * cells[None, :], side)
     turn_v = jnp.concatenate([cos_v, -sin_v], axis=1).astype(bf16)
     twist = jnp.stack(cos_sin(cells[:, None] * small[None, :], NPIX))
-    recv, turn_u, rot, turn_v, twist = lax.optimization_barrier((recv, turn_u, rot, turn_v, twist))
+    recv, turn_u, rot, twist = lax.optimization_barrier((recv, turn_u, rot, twist))
 
     group = min(2, per_dev)
     sent, back = call(
@@ -385,26 +399,33 @@
         ],
         out_specs=(
             pl.BlockSpec((per_dev * SENT, lanes), lambda l: (0, 0)),
-            pl.BlockSpec((devices, lanes), lambda l: (0, 0)),
+            pl.BlockSpec((chips, lanes), lambda l: (0, 0)),
         ),
-        out_shape=(shape((per_dev * SENT, lanes), f32), shape((devices, lanes), f32)),
-        scratch_shapes=[pltpu.VMEM((per_dev, FIELDS, lanes), f32)],
+        out_shape=(shape((per_dev * SENT, lanes), f32), shape((chips, lanes), f32)),
+        scratch_shapes=[pltpu.VMEM((per_dev, FIELDS, lanes), f32), pltpu.VMEM((lanes, 128), f32)],
         compiler_params=params(32),
         name="predict",
     )(recv, pltpu.with_memory_space_constraint(model_grid, pltpu.HBM))
-    sent = jnp.broadcast_to(sent[None], (devices,) + sent.shape)
-    tiles = exchange(jnp.concatenate([sent, back[:, None, :]], axis=1))
-    tiles = pltpu.with_memory_space_constraint(tiles, pltpu.HBM)
+    sent = jnp.broadcast_to(sent[None], (chips,) + sent.shape)
+    near = lax.all_to_all(
+        jnp.concatenate([sent, back[:, None, :]], axis=1),
+        AXES[:2],
+        split_axis=0,
+        concat_axis=0,
+        tiled=True,
+    )
+    near, turn_v, twist = lax.optimization_barrier((near, turn_v, twist))
+    far = lax.ppermute(near, "core", [(0, 1), (1, 0)])
 
     thin = min(128, rows)
     vmem = pl.BlockSpec(memory_space=pltpu.VMEM)
     gradient, weighted_residual = call(
         image_body,
-        in_specs=[vmem] * 7,
+        in_specs=[pl.BlockSpec(memory_space=pltpu.SMEM)] + [vmem] * 8,
         out_specs=(pl.BlockSpec(memory_space=pl.ANY), vmem),
         out_shape=(shape((rows, NPIX), f32), shape((2, n), f32)),
         scratch_shapes=[
-            pltpu.VMEM((devices, per_dev, 8, lanes), f32),
+            pltpu.VMEM((CORES, per_dev, chips, 8, lanes), f32),
             pltpu.VMEM((8, NT * lanes + 128), f32),
             pltpu.VMEM((side, NT * lanes), bf16),
             pltpu.VMEM((2 * rows, NT * lanes), bf16),
@@ -416,23 +437,25 @@
             pltpu.SMEM((8, ntiles), i32),
         ]
         + [pltpu.VMEM((NPIX, thin), f32)] * (rows // thin),
-        compiler_params=params(56),
+        compiler_params=params(44),
         name="image",
-    )(tiles, tile_row, rank, turn_u, rot, turn_v, twist)
+    )(core.reshape(1), near, far, tile_row, rank, turn_u, rot, turn_v, twist)
     return (gradient, weighted_residual)
 
 
 def solution(mesh):
+    cut = mesh.devices.reshape(mesh.shape["blen"], mesh.shape["tm"] // CORES, CORES)
+    whole = P(AXES)
     in_specs = (
         P(AXES, None, None, None),
         P(None, AXES),
-        P(AXES),
-        P(AXES),
+        whole,
+        whole,
         P(None, AXES),
         P(None, AXES),
         P(AXES, None),
     )
     out_specs = (P(AXES, None), P(None, AXES))
     return jax.shard_map(
-        on_device, mesh=mesh, in_specs=in_specs, out_specs=out_specs, check_vma=False
+        on_device, mesh=Mesh(cut, AXES), in_specs=in_specs, out_specs=out_specs, check_vma=False
     )

time: 112 us -> 99.6 us (0.89); the launches traced: 111 us -> 99.7 us
  waiting for transfers between devices: 22.2 us -> 15.6 us
  Pallas kernels: 60.1 us -> 63.8 us
  local copies, waits for them, and re-layouts: 3.43 us -> 0.24 us
  other arithmetic: 10.7 us -> 8.08 us
  starting transfers between devices: 13.3 us -> 11 us
    all_to_all x2, waiting for transfers between devices: 22.2 us -> 14 us  [the longest x1 9.59 us: on_device(): lax.all_to_all(jnp.concatenate([sent, back[:, None, :]], axis=1), AXES[:2...]
    pallas_call x1, Pallas kernels: 51.9 us -> 54.9 us  [on_device(): call(image_body, in_specs=[pl.BlockSpec(memory_space=pltpu.SMEM)] + [vmem...]
    all_to_all x2, starting transfers between devices: 13.3 us -> 11 us  [the longest x1 7.3 us: on_device(): recv = lax.all_to_all(packed, AXES, split_axis=0, concat_axis=0, tiled=True)]
    ppermute x0 -> x1, waiting for transfers between devices: none -> 1.61 us  [on_device(): far = lax.ppermute(near, 'core', [(0, 1), (1, 0)])]
    all_to_all x1 -> x0, local copies, waits for them, and re-layouts: 1.39 us -> none  [exchange(): return lax.all_to_all(x, AXES, split_axis=0, concat_axis=0, tiled=True)]
  transfers between devices with their start and end apart: 2 -> 3, of which waited for: 1 -> 3; matrix products, arithmetic and copies ran while one was open for 10% -> 7% of each run, Pallas kernels for 0% -> 0%
where the time goes in v6:
time: 99.6 us; the launch traced here: 99.7 us
  Pallas kernels  63.8 us (64%)
  waiting for transfers between devices  15.6 us (16%)
  starting transfers between devices  11 us (11%)
  other arithmetic  8.08 us (8%)
    pallas_call x1, Pallas kernels, on_device(): call(image_body, in_specs=[pl.BlockSpec(memory_space=pltpu.SMEM)] + [vmem...  54.9 us
    all_to_all x1, waiting for transfers between devices, on_device(): lax.all_to_all(jnp.concatenate([sent, back[:, None, :]], axis=1), AXES[:2...  9.59 us
    all_to_all x1, starting transfers between devices, on_device(): recv = lax.all_to_all(packed, AXES, split_axis=0, concat_axis=0, tiled=True)  7.3 us
    another operation x2, other arithmetic  6.79 us
    pallas_call x1, Pallas kernels, on_device(): call(lambda *refs: predict_body(*refs, per_dev=per_dev), grid=(per_dev //...  6.21 us
    all_to_all x1, waiting for transfers between devices, on_device(): recv = lax.all_to_all(packed, AXES, split_axis=0, concat_axis=0, tiled=True)  4.37 us
    all_to_all x1, starting transfers between devices, on_device(): lax.all_to_all(jnp.concatenate([sent, back[:, None, :]], axis=1), AXES[:2...  3.74 us
    pallas_call x1, Pallas kernels, on_device(): call(lambda *refs: pack_body(*refs, devices=devices, per_dev=per_dev), ou...  2.68 us
  transfers between devices with their start and end apart: 3, of which 3 were waited for; matrix products, arithmetic and copies ran while one was open for 7% of the time, Pallas kernels for 0%

profile of v6, /device:TPU:0, one launch (start us, length us, event | category | flops | bytes accessed | tf_op | source)
XLA Modules:
  0.0 99.7 jit_solution(7580913457962934442)
XLA Ops:
  0.6 2.7 %pack.1 = (f32[32,1,256]{2,1,0:T(1,128)}, s32[1,512]{1,0:T(1,128)}) custom-call(s32[1,512]{1,0:T(1,128)} %bitcast.12, s32[2,512]{1,0:T(2,128)} %refs_1_.2, f32[2,512]{1,0:T(2,128)} %refs_2_.1, f32[2,512]{1,0:T(2,128)} %refs_3_.1, f32[1,512]{1,0:T(1,128)} %bitcast.14, s32[1,512]{1,0:T(1,128)} %bitcast.15), custom_call_target="tpu_custom_call" | custom-call | tf_op jit(solution)/shard_map/pack/pallas_call | solution.py:373
  3.3 7.3 %all-to-all-start = ((f32[32,1,256]{2,1,0:T(1,128)}), f32[32,1,256]{2,1,0:T(1,128)S(1)}, u32[]{:S(2)}, u32[]{:S(2)}) async-start(f32[32,1,256]{2,1,0:T(1,128)} %get-tuple-element.13), calls=%async_computation | async-start | bytes 65536 | tf_op jit(solution)/shard_map/all_to_all | solution.py:378
  10.6 0.1 fusion.28
  10.7 0.1 fusion.18
  10.9 2.4 %cosine_convert_fusion.1 = (bf16[16,1,16,512]{3,2,1,0:T(8,128)(2,1)S(1)}, bf16[16,1,16,512]{3,2,1,0:T(8,128)(2,1)S(1)}) fusion(s32[16,16]{1,0:T(8,128)S(1)} %add_add_fusion), kind=kLoop, calls=%fused_computation.20 | loop fusion | flops 2097152 | bytes 525312 | tf_op jit(solution)/shard_map/convert.2
  13.3 0.1 pad_maximum_fusion.1
  13.4 0.1 pad_maximum_fusion.5.rot
  13.5 4.4 %all-to-all-done = f32[32,1,256]{2,1,0:T(1,128)S(1)} async-done(((f32[32,1,256]{2,1,0:T(1,128)}), f32[32,1,256]{2,1,0:T(1,128)S(1)}, u32[]{:S(2)}, u32[]{:S(2)}) %all-to-all-start) | async-done | bytes 32800 | tf_op jit(solution)/shard_map/all_to_all | solution.py:378
  17.9 6.2 %predict.1 = (f32[48,128]{1,0:T(8,128)S(1)}, f32[16,128]{1,0:T(8,128)S(1)}) custom-call(f32[32,256]{1,0:T(8,128)S(1)} %bitcast.10, bf16[8,2,512,512]{3,2,1,0:T(8,128)(2,1)} %refs_1_.3), custom_call_target="tpu_custom_call" | custom-call | tf_op jit(solution)/shard_map/predict/pallas_call | solution.py:393
  24.1 0.8 pad_maximum_fusion.2
  24.9 3.7 %all-to-all-start.1 = ((f32[16,49,128]{2,1,0:T(8,128)}), f32[16,49,128]{2,1,0:T(8,128)S(1)}, u32[]{:S(2)}, u32[]{:S(2)}) async-start(f32[16,49,128]{2,1,0:T(8,128)} %pad_maximum_fusion.2), calls=%async_computation.1 | async-start | bytes 917504 | tf_op jit(solution)/shard_map/all_to_all | solution.py:410
  28.7 0.0 copy-start
  28.7 0.0 copy-start.1
  28.7 4.3 %negate_convert_fusion = (bf16[512,512]{1,0:T(8,128)(2,1)S(1)}, bf16[512,512]{1,0:T(8,128)(2,1)S(1)}) fusion(), kind=kLoop, calls=%fused_computation.7 | loop fusion | flops 4456448 | bytes 1048576 | tf_op jit(solution)/shard_map/convert.1
  33.1 0.1 pad_maximum_fusion.turn_v
  33.2 9.6 %all-to-all-done.1.near = f32[16,49,128]{2,1,0:T(8,128)S(1)} async-done(((f32[16,49,128]{2,1,0:T(8,128)}), f32[16,49,128]{2,1,0:T(8,128)S(1)}, u32[]{:S(2)}, u32[]{:S(2)}) %all-to-all-start.1) | async-done | bytes 401440 | tf_op jit(solution)/shard_map/all_to_all | solution.py:410
  42.8 0.0 collective-permute-start
  42.8 0.2 copy.11.twist
  43.0 1.6 %collective-permute-done.far = f32[16,49,128]{2,1,0:T(8,128)S(1)} collective-permute-done((f32[16,49,128]{2,1,0:T(8,128)S(1)}, f32[16,49,128]{2,1,0:T(8,128)S(1)}, u32[]{:S(2)}, u32[]{:S(2)}) %collective-permute-start) | collective-permute-done | bytes 401440 | tf_op jit(solution)/shard_map/ppermute | solution.py:418
  44.6 0.0 copy-done
  44.6 0.0 copy-done.1
  44.6 54.9 %image.1 = (f32[256,8192]{1,0:T(8,128)}, f32[2,512]{1,0:T(2,128)}) custom-call(s32[1]{0:T(128)} %bitcast.core, f32[16,49,128]{2,1,0:T(8,128)S(1)} %all-to-all-done.1.near, f32[16,49,128]{2,1,0:T(8,128)S(1)} %collective-permute-done.far, s32[1,512]{1,0:T(1,128)S(1)} %bitcast.13, s32[1,512]{1,0:T(1,128)S(1)} %copy-done.1, bf16[512,512]{1,0:T(8,128)(2,1)S(1)} %bitcast.9, ...), custom_call_target="tpu_custom_call" | custom-call | tf_op jit(solution)/shard_map/image/pallas_call | solution.py:422
  (6 shorter events, 0.1 us)
Async XLA Ops:
  3.3 14.6 %all-to-all-start = ((f32[32,1,256]{2,1,0:T(1,128)}), f32[32,1,256]{2,1,0:T(1,128)S(1)}, u32[]{:S(2)}, u32[]{:S(2)}) async-start(f32[32,1,256]{2,1,0:T(1,128)} %get-tuple-element.13), calls=%async_computation | async-start | bytes 65536 | tf_op jit(solution)/shard_map/all_to_all | solution.py:378
  24.9 17.8 %all-to-all-start.1 = ((f32[16,49,128]{2,1,0:T(8,128)}), f32[16,49,128]{2,1,0:T(8,128)S(1)}, u32[]{:S(2)}, u32[]{:S(2)}) async-start(f32[16,49,128]{2,1,0:T(8,128)} %pad_maximum_fusion.2), calls=%async_computation.1 | async-start | bytes 917504 | tf_op jit(solution)/shard_map/all_to_all | solution.py:410
  28.7 15.9 %copy-start = (s32[512,1]{0,1:T(1,128)S(1)}, s32[512,1]{0,1:T(1,128)}, u32[]{:S(2)}) copy-start(s32[512,1]{0,1:T(1,128)} %param.13) | copy-start | bytes 6148
  28.7 15.9 %copy-start.1 = (s32[1,512]{1,0:T(1,128)S(1)}, s32[1,512]{1,0:T(1,128)}, u32[]{:S(2)}) copy-start(s32[1,512]{1,0:T(1,128)} %get-tuple-element.19.rank) | copy-start | bytes 6148
  42.8 1.8 %collective-permute-start = (f32[16,49,128]{2,1,0:T(8,128)S(1)}, f32[16,49,128]{2,1,0:T(8,128)S(1)}, u32[]{:S(2)}, u32[]{:S(2)}) collective-permute-start(f32[16,49,128]{2,1,0:T(8,128)S(1)} %all-to-all-done.1.near), channel_id=1, source_target_pairs={{0,1},{1,0},{2,3},{3,2},{4,5},{5,4},{6,7},{7,6},{8,9},{9,8},{10,11... | collective-permute-start | bytes 1204232 | tf_op jit(solution)/shard_map/ppermute | solution.py:418

commit v7 on v6

--- a/solution.py
+++ b/solution.py
@@ -187,20 +187,20 @@
     width = flips[0].shape[1]
     most = NT * lanes // CHUNK
 
-    there = []
     for far_off, recv in enumerate((near, far)):
         from_core = core[0] if far_off == 0 else 1 - core[0]
         for l in range(per_dev):
             some = recv[:, l * SENT : (l + 1) * SENT, :]
-            filled = some[:, 0:1, :] > 0.5
-            owner = lax.broadcasted_iota(i32, filled.shape, 0) * CORES + from_core
-            tile = owner * per_dev + l
-            mark = jnp.where(filled, (tile // TVG % NT).astype(f32), 0.0)
-            tiles[far_off, l] = jnp.concatenate([some, mark, jnp.zeros_like(mark)], axis=1)
-            there.append(jnp.where(filled[:, 0], 1.0, 0.0).astype(bf16))
+            owner = lax.broadcasted_iota(i32, (chips, 1, lanes), 0) * CORES + from_core
+            mark = ((owner * per_dev + l) // TVG % NT).astype(f32)
+            mark = jnp.where(some[:, 0:1, :] > 0.5, mark, 0.0)
+            cells = jnp.concatenate([some, mark, jnp.zeros_like(mark)], axis=1)
+            for chip in range(chips):
+                tiles[(chip * CORES + from_core) * per_dev + l] = cells[chip]
+    there = jnp.where(tiles[:, 0, :] > 0.5, 1.0, 0.0).astype(bf16)
     total = lax.dot_general(
         jnp.ones((8, lanes), bf16),
-        jnp.concatenate(there, axis=0),
+        there,
         NT_DIMS,
         preferred_element_type=f32,
     )
@@ -258,20 +258,15 @@
         )
 
     def tile_column(tv, carry):
-        group = tv // TVG * (NT * TVG) + tv % TVG
+        group = (tv >> 2) * (NT * TVG) + (tv & 3)
         merged[...] = jnp.zeros(merged.shape, f32)
         used = jnp.int32(0)
         for tu in range(NT):
             tile = group + tu * TVG
-            owner = tile // per_dev
-            local = tile % per_dev
-            far_off = (owner + core[0]) % CORES
-            chip = owner // CORES
-            cell = tiles[far_off, local, chip]
-            cell = jnp.concatenate([cell, jnp.zeros((8, 128), f32)], axis=1)
-            at = pl.ds(pl.multiple_of(used // 128 * 128, 128), lanes + 128)
-            merged[:, at] = merged[:, at] + pltpu.roll(cell, used % 128, axis=1)
-            used = used + counts[0, (far_off * per_dev + local) * chips + chip]
+            cell = jnp.concatenate([tiles[tile], jnp.zeros((8, 128), f32)], axis=1)
+            at = pl.ds(pl.multiple_of((used >> 7) << 7, 128), lanes + 128)
+            merged[:, at] = merged[:, at] + pltpu.roll(cell, used & 127, axis=1)
+            used = used + counts[0, tile]
         chunks = (used + CHUNK - 1) // CHUNK
 
         if most == 8:
@@ -425,7 +420,7 @@
         out_specs=(pl.BlockSpec(memory_space=pl.ANY), vmem),
         out_shape=(shape((rows, NPIX), f32), shape((2, n), f32)),
         scratch_shapes=[
-            pltpu.VMEM((CORES, per_dev, chips, 8, lanes), f32),
+            pltpu.VMEM((ntiles, 8, lanes), f32),
             pltpu.VMEM((8, NT * lanes + 128), f32),
             pltpu.VMEM((side, NT * lanes), bf16),
             pltpu.VMEM((2 * rows, NT * lanes), bf16),

time: 99.6 us -> 94.7 us (0.951)
  Pallas kernels: 63.8 us -> 58.9 us
    pallas_call x1, Pallas kernels: 54.9 us -> 50 us  [on_device(): call(image_body, in_specs=[pl.BlockSpec(memory_space=pltpu.SMEM)] + [vmem...]
  transfers between devices with their start and end apart: 3 -> 3, of which waited for: 3 -> 3; matrix products, arithmetic and copies ran while one was open for 7% -> 8% of each run, Pallas kernels for 0% -> 0%
where the time goes in v7:
time: 94.7 us; the launch traced here: 94.8 us
  Pallas kernels  58.9 us (62%)
  waiting for transfers between devices  15.6 us (16%)
  starting transfers between devices  11 us (12%)
  other arithmetic  8.08 us (9%)
  between operations  0.95 us (1%)
    pallas_call x1, Pallas kernels, on_device(): call(image_body, in_specs=[pl.BlockSpec(memory_space=pltpu.SMEM)] + [vmem...  50 us
    all_to_all x1, waiting for transfers between devices, on_device(): lax.all_to_all(jnp.concatenate([sent, back[:, None, :]], axis=1), AXES[:2...  9.59 us
    all_to_all x1, starting transfers between devices, on_device(): recv = lax.all_to_all(packed, AXES, split_axis=0, concat_axis=0, tiled=True)  7.3 us
    another operation x2, other arithmetic  6.79 us
    pallas_call x1, Pallas kernels, on_device(): call(lambda *refs: predict_body(*refs, per_dev=per_dev), grid=(per_dev //...  6.21 us
    all_to_all x1, waiting for transfers between devices, on_device(): recv = lax.all_to_all(packed, AXES, split_axis=0, concat_axis=0, tiled=True)  4.37 us
    all_to_all x1, starting transfers between devices, on_device(): lax.all_to_all(jnp.concatenate([sent, back[:, None, :]], axis=1), AXES[:2...  3.74 us
    pallas_call x1, Pallas kernels, on_device(): call(lambda *refs: pack_body(*refs, devices=devices, per_dev=per_dev), ou...  2.68 us
  transfers between devices with their start and end apart: 3, of which 3 were waited for; matrix products, arithmetic and copies ran while one was open for 8% of the time, Pallas kernels for 0%

profile of v7, /device:TPU:0, one launch (start us, length us, event | category | flops | bytes accessed | tf_op | source)
XLA Modules:
  0.0 94.8 jit_solution(13922375858214073606)
XLA Ops:
  0.6 2.7 %pack.1 = (f32[32,1,256]{2,1,0:T(1,128)}, s32[1,512]{1,0:T(1,128)}) custom-call(s32[1,512]{1,0:T(1,128)} %bitcast.12, s32[2,512]{1,0:T(2,128)} %refs_1_.2, f32[2,512]{1,0:T(2,128)} %refs_2_.1, f32[2,512]{1,0:T(2,128)} %refs_3_.1, f32[1,512]{1,0:T(1,128)} %bitcast.14, s32[1,512]{1,0:T(1,128)} %bitcast.15), custom_call_target="tpu_custom_call" | custom-call | tf_op jit(solution)/shard_map/pack/pallas_call | solution.py:368
  3.3 7.3 %all-to-all-start = ((f32[32,1,256]{2,1,0:T(1,128)}), f32[32,1,256]{2,1,0:T(1,128)S(1)}, u32[]{:S(2)}, u32[]{:S(2)}) async-start(f32[32,1,256]{2,1,0:T(1,128)} %get-tuple-element.13), calls=%async_computation | async-start | bytes 65536 | tf_op jit(solution)/shard_map/all_to_all | solution.py:373
  10.6 0.1 fusion.28
  10.7 0.1 fusion.18
  10.9 2.4 %cosine_convert_fusion.1 = (bf16[16,1,16,512]{3,2,1,0:T(8,128)(2,1)S(1)}, bf16[16,1,16,512]{3,2,1,0:T(8,128)(2,1)S(1)}) fusion(s32[16,16]{1,0:T(8,128)S(1)} %add_add_fusion), kind=kLoop, calls=%fused_computation.20 | loop fusion | flops 2097152 | bytes 525312 | tf_op jit(solution)/shard_map/convert.2
  13.3 0.1 pad_maximum_fusion.1
  13.4 0.1 pad_maximum_fusion.5.rot
  13.5 4.4 %all-to-all-done = f32[32,1,256]{2,1,0:T(1,128)S(1)} async-done(((f32[32,1,256]{2,1,0:T(1,128)}), f32[32,1,256]{2,1,0:T(1,128)S(1)}, u32[]{:S(2)}, u32[]{:S(2)}) %all-to-all-start) | async-done | bytes 32800 | tf_op jit(solution)/shard_map/all_to_all | solution.py:373
  17.9 6.2 %predict.1 = (f32[48,128]{1,0:T(8,128)S(1)}, f32[16,128]{1,0:T(8,128)S(1)}) custom-call(f32[32,256]{1,0:T(8,128)S(1)} %bitcast.10, bf16[8,2,512,512]{3,2,1,0:T(8,128)(2,1)} %refs_1_.3), custom_call_target="tpu_custom_call" | custom-call | tf_op jit(solution)/shard_map/predict/pallas_call | solution.py:388
  24.1 0.8 pad_maximum_fusion.2
  24.9 3.7 %all-to-all-start.1 = ((f32[16,49,128]{2,1,0:T(8,128)}), f32[16,49,128]{2,1,0:T(8,128)S(1)}, u32[]{:S(2)}, u32[]{:S(2)}) async-start(f32[16,49,128]{2,1,0:T(8,128)} %pad_maximum_fusion.2), calls=%async_computation.1 | async-start | bytes 917504 | tf_op jit(solution)/shard_map/all_to_all | solution.py:405
  28.7 0.0 copy-start
  28.7 0.0 copy-start.1
  28.7 4.3 %negate_convert_fusion = (bf16[512,512]{1,0:T(8,128)(2,1)S(1)}, bf16[512,512]{1,0:T(8,128)(2,1)S(1)}) fusion(), kind=kLoop, calls=%fused_computation.7 | loop fusion | flops 4456448 | bytes 1048576 | tf_op jit(solution)/shard_map/convert.1
  33.1 0.1 pad_maximum_fusion.turn_v
  33.2 9.6 %all-to-all-done.1.near = f32[16,49,128]{2,1,0:T(8,128)S(1)} async-done(((f32[16,49,128]{2,1,0:T(8,128)}), f32[16,49,128]{2,1,0:T(8,128)S(1)}, u32[]{:S(2)}, u32[]{:S(2)}) %all-to-all-start.1) | async-done | bytes 401440 | tf_op jit(solution)/shard_map/all_to_all | solution.py:405
  42.8 0.0 collective-permute-start
  42.8 0.2 copy.11.twist
  43.0 1.6 %collective-permute-done.far = f32[16,49,128]{2,1,0:T(8,128)S(1)} collective-permute-done((f32[16,49,128]{2,1,0:T(8,128)S(1)}, f32[16,49,128]{2,1,0:T(8,128)S(1)}, u32[]{:S(2)}, u32[]{:S(2)}) %collective-permute-start) | collective-permute-done | bytes 401440 | tf_op jit(solution)/shard_map/ppermute | solution.py:413
  44.6 0.0 copy-done
  44.6 0.0 copy-done.1
  44.6 50.0 %image.1 = (f32[256,8192]{1,0:T(8,128)}, f32[2,512]{1,0:T(2,128)}) custom-call(s32[1]{0:T(128)} %bitcast.core, f32[16,49,128]{2,1,0:T(8,128)S(1)} %all-to-all-done.1.near, f32[16,49,128]{2,1,0:T(8,128)S(1)} %collective-permute-done.far, s32[1,512]{1,0:T(1,128)S(1)} %bitcast.13, s32[1,512]{1,0:T(1,128)S(1)} %copy-done.1, bf16[512,512]{1,0:T(8,128)(2,1)S(1)} %bitcast.9, ...), custom_call_target="tpu_custom_call" | custom-call | tf_op jit(solution)/shard_map/image/pallas_call | solution.py:417
  (6 shorter events, 0.1 us)
Async XLA Ops:
  3.3 14.6 %all-to-all-start = ((f32[32,1,256]{2,1,0:T(1,128)}), f32[32,1,256]{2,1,0:T(1,128)S(1)}, u32[]{:S(2)}, u32[]{:S(2)}) async-start(f32[32,1,256]{2,1,0:T(1,128)} %get-tuple-element.13), calls=%async_computation | async-start | bytes 65536 | tf_op jit(solution)/shard_map/all_to_all | solution.py:373
  24.9 17.8 %all-to-all-start.1 = ((f32[16,49,128]{2,1,0:T(8,128)}), f32[16,49,128]{2,1,0:T(8,128)S(1)}, u32[]{:S(2)}, u32[]{:S(2)}) async-start(f32[16,49,128]{2,1,0:T(8,128)} %pad_maximum_fusion.2), calls=%async_computation.1 | async-start | bytes 917504 | tf_op jit(solution)/shard_map/all_to_all | solution.py:405
  28.7 15.9 %copy-start = (s32[512,1]{0,1:T(1,128)S(1)}, s32[512,1]{0,1:T(1,128)}, u32[]{:S(2)}) copy-start(s32[512,1]{0,1:T(1,128)} %param.13) | copy-start | bytes 6148
  28.7 15.9 %copy-start.1 = (s32[1,512]{1,0:T(1,128)S(1)}, s32[1,512]{1,0:T(1,128)}, u32[]{:S(2)}) copy-start(s32[1,512]{1,0:T(1,128)} %get-tuple-element.19.rank) | copy-start | bytes 6148
  42.8 1.8 %collective-permute-start = (f32[16,49,128]{2,1,0:T(8,128)S(1)}, f32[16,49,128]{2,1,0:T(8,128)S(1)}, u32[]{:S(2)}, u32[]{:S(2)}) collective-permute-start(f32[16,49,128]{2,1,0:T(8,128)S(1)} %all-to-all-done.1.near), channel_id=1, source_target_pairs={{0,1},{1,0},{2,3},{3,2},{4,5},{5,4},{6,7},{7,6},{8,9},{9,8},{10,11... | collective-permute-start | bytes 1204232 | tf_op jit(solution)/shard_map/ppermute | solution.py:413

commit v8 on v7

--- a/solution.py
+++ b/solution.py
@@ -176,7 +176,7 @@
 
 def image_body(
     core, near, far, tile_row, rank, turn_u, rot, turn_v, twist, out, own,
-    tiles, merged, kv_all, up_all, grid, turned, stage, sems, tally, counts, *flips,
+    tiles, merged, kv_all, up_all, grid, turned, stage, sems, tally, counts, fill, *flips,
 ):
     side = turn_u.shape[1]
     rows2 = turn_u.shape[0]
@@ -187,17 +187,18 @@
     width = flips[0].shape[1]
     most = NT * lanes // CHUNK
 
+    there = []
     for far_off, recv in enumerate((near, far)):
         from_core = core[0] if far_off == 0 else 1 - core[0]
         for l in range(per_dev):
             some = recv[:, l * SENT : (l + 1) * SENT, :]
-            owner = lax.broadcasted_iota(i32, (chips, 1, lanes), 0) * CORES + from_core
-            mark = ((owner * per_dev + l) // TVG % NT).astype(f32)
-            mark = jnp.where(some[:, 0:1, :] > 0.5, mark, 0.0)
+            filled = some[:, 0:1, :] > 0.5
+            owner = lax.broadcasted_iota(i32, filled.shape, 0) * CORES + from_core
+            mark = jnp.where(filled, ((owner * per_dev + l) // TVG % NT).astype(f32), 0.0)
             cells = jnp.concatenate([some, mark, jnp.zeros_like(mark)], axis=1)
-            for chip in range(chips):
-                tiles[(chip * CORES + from_core) * per_dev + l] = cells[chip]
-    there = jnp.where(tiles[:, 0, :] > 0.5, 1.0, 0.0).astype(bf16)
+            tiles[(far_off * per_dev + l) * chips : (far_off * per_dev + l + 1) * chips] = cells
+            there.append(jnp.where(filled[:, 0], 1.0, 0.0).astype(bf16))
+    there = jnp.concatenate(there, axis=0)
     total = lax.dot_general(
         jnp.ones((8, lanes), bf16),
         there,
@@ -227,8 +228,8 @@
         own[c : c + 1, :] = jnp.sum(jnp.where(picked, total, 0.0), axis=0, keepdims=True)
     count_copy.wait()
 
-    def chunk(at):
-        m = merged[:, pl.ds(at, CHUNK)]
+    def chunk(slot, at):
+        m = merged[slot, :, pl.ds(at, CHUNK)]
         first = m[0:2].astype(i32) - (KSUP // 2 - 1)
         ku = dense(*pattern(first[0:1], m[2:3]), side)
         kv_all[:, pl.ds(at, CHUNK)] = dense(*pattern(first[1:2], m[3:4]), side)
@@ -257,17 +258,26 @@
             preferred_element_type=f32,
         )
 
-    def tile_column(tv, carry):
+    def merge(tv, slot):
         group = (tv >> 2) * (NT * TVG) + (tv & 3)
-        merged[...] = jnp.zeros(merged.shape, f32)
+        merged[slot] = jnp.zeros(merged.shape[1:], f32)
         used = jnp.int32(0)
         for tu in range(NT):
             tile = group + tu * TVG
-            cell = jnp.concatenate([tiles[tile], jnp.zeros((8, 128), f32)], axis=1)
+            owner = tile >> (per_dev.bit_length() - 1)
+            local = tile & (per_dev - 1)
+            far_off = (owner ^ core[0]) & 1
+            index = (far_off * per_dev + local) * chips + (owner >> 1)
+            cell = jnp.concatenate([tiles[index], jnp.zeros((8, 128), f32)], axis=1)
             at = pl.ds(pl.multiple_of((used >> 7) << 7, 128), lanes + 128)
-            merged[:, at] = merged[:, at] + pltpu.roll(cell, used & 127, axis=1)
-            used = used + counts[0, tile]
-        chunks = (used + CHUNK - 1) // CHUNK
+            merged[slot, :, at] = merged[slot, :, at] + pltpu.roll(cell, used & 127, axis=1)
+            used = used + counts[0, index]
+        fill[slot] = used
+
+    def tile_column(tv, carry):
+        slot = tv & 1
+        following = jnp.minimum(tv + 1, NT - 1)
+        chunks = (fill[slot] + CHUNK - 1) // CHUNK
 
         if most == 8:
             low = -1
@@ -276,24 +286,27 @@
                 @pl.when((chunks > low) & (chunks <= n))
                 def _():
                     for i in range(n):
-                        chunk(i * CHUNK)
+                        chunk(slot, i * CHUNK)
+                    merge(following, 1 - slot)
                     grid[tv] = product(0, n * CHUNK).astype(bf16)
 
                 low = n
         else:
 
             def make(i, c):
-                chunk(pl.multiple_of(i * CHUNK, CHUNK))
+                chunk(slot, pl.multiple_of(i * CHUNK, CHUNK))
                 return c
 
             def add(i, ft):
                 return ft + product(pl.multiple_of(i * CHUNK, CHUNK), CHUNK)
 
             lax.fori_loop(0, chunks, make, 0)
+            merge(following, 1 - slot)
             ft = lax.fori_loop(0, chunks, add, jnp.zeros((side, rows2), f32))
             grid[tv] = ft.astype(bf16)
         return carry
 
+    merge(jnp.int32(0), 0)
     lax.fori_loop(0, NT, tile_column, 0)
 
     def stripe(j, carry):
@@ -421,7 +434,7 @@
         out_shape=(shape((rows, NPIX), f32), shape((2, n), f32)),
         scratch_shapes=[
             pltpu.VMEM((ntiles, 8, lanes), f32),
-            pltpu.VMEM((8, NT * lanes + 128), f32),
+            pltpu.VMEM((2, 8, NT * lanes + 128), f32),
             pltpu.VMEM((side, NT * lanes), bf16),
             pltpu.VMEM((2 * rows, NT * lanes), bf16),
             pltpu.VMEM((NT, side, 2 * rows), bf16),
@@ -430,6 +443,7 @@
             pltpu.SemaphoreType.DMA((8,)),
             pltpu.VMEM((8, ntiles), i32),
             pltpu.SMEM((8, ntiles), i32),
+            pltpu.SMEM((2,), i32),
         ]
         + [pltpu.VMEM((NPIX, thin), f32)] * (rows // thin),
         compiler_params=params(44),

time: 94.7 us -> 93.4 us (0.986)
  Pallas kernels: 58.9 us -> 57.9 us
    pallas_call x1, Pallas kernels: 50 us -> 49 us  [on_device(): call(image_body, in_specs=[pl.BlockSpec(memory_space=pltpu.SMEM)] + [vmem...]
where the time goes in v8:
time: 93.4 us; the launch traced here: 93.8 us
  Pallas kernels  57.9 us (62%)
  waiting for transfers between devices  15.6 us (17%)
  starting transfers between devices  11 us (12%)
  other arithmetic  8.08 us (9%)
  between operations  0.95 us (1%)
    pallas_call x1, Pallas kernels, on_device(): call(image_body, in_specs=[pl.BlockSpec(memory_space=pltpu.SMEM)] + [vmem...  49 us
    all_to_all x1, waiting for transfers between devices, on_device(): lax.all_to_all(jnp.concatenate([sent, back[:, None, :]], axis=1), AXES[:2...  9.59 us
    all_to_all x1, starting transfers between devices, on_device(): recv = lax.all_to_all(packed, AXES, split_axis=0, concat_axis=0, tiled=True)  7.3 us
    another operation x2, other arithmetic  6.79 us
    pallas_call x1, Pallas kernels, on_device(): call(lambda *refs: predict_body(*refs, per_dev=per_dev), grid=(per_dev //...  6.21 us
    all_to_all x1, waiting for transfers between devices, on_device(): recv = lax.all_to_all(packed, AXES, split_axis=0, concat_axis=0, tiled=True)  4.37 us
    all_to_all x1, starting transfers between devices, on_device(): lax.all_to_all(jnp.concatenate([sent, back[:, None, :]], axis=1), AXES[:2...  3.74 us
    pallas_call x1, Pallas kernels, on_device(): call(lambda *refs: pack_body(*refs, devices=devices, per_dev=per_dev), ou...  2.68 us
  transfers between devices with their start and end apart: 3, of which 3 were waited for; matrix products, arithmetic and copies ran while one was open for 8% of the time, Pallas kernels for 0%

profile of v8, /device:TPU:0, one launch (start us, length us, event | category | flops | bytes accessed | tf_op | source)
XLA Modules:
  0.0 93.8 jit_solution(985110344929137867)
XLA Ops:
  0.6 2.7 %pack.1 = (f32[32,1,256]{2,1,0:T(1,128)}, s32[1,512]{1,0:T(1,128)}) custom-call(s32[1,512]{1,0:T(1,128)} %bitcast.12, s32[2,512]{1,0:T(2,128)} %refs_1_.2, f32[2,512]{1,0:T(2,128)} %refs_2_.1, f32[2,512]{1,0:T(2,128)} %refs_3_.1, f32[1,512]{1,0:T(1,128)} %bitcast.14, s32[1,512]{1,0:T(1,128)} %bitcast.15), custom_call_target="tpu_custom_call" | custom-call | tf_op jit(solution)/shard_map/pack/pallas_call | solution.py:381
  3.3 7.3 %all-to-all-start = ((f32[32,1,256]{2,1,0:T(1,128)}), f32[32,1,256]{2,1,0:T(1,128)S(1)}, u32[]{:S(2)}, u32[]{:S(2)}) async-start(f32[32,1,256]{2,1,0:T(1,128)} %get-tuple-element.13), calls=%async_computation | async-start | bytes 65536 | tf_op jit(solution)/shard_map/all_to_all | solution.py:386
  10.6 0.1 fusion.28
  10.7 0.1 fusion.18
  10.9 2.4 %cosine_convert_fusion.1 = (bf16[16,1,16,512]{3,2,1,0:T(8,128)(2,1)S(1)}, bf16[16,1,16,512]{3,2,1,0:T(8,128)(2,1)S(1)}) fusion(s32[16,16]{1,0:T(8,128)S(1)} %add_add_fusion), kind=kLoop, calls=%fused_computation.20 | loop fusion | flops 2097152 | bytes 525312 | tf_op jit(solution)/shard_map/convert.2
  13.3 0.1 pad_maximum_fusion.1
  13.4 0.1 pad_maximum_fusion.5.rot
  13.5 4.4 %all-to-all-done = f32[32,1,256]{2,1,0:T(1,128)S(1)} async-done(((f32[32,1,256]{2,1,0:T(1,128)}), f32[32,1,256]{2,1,0:T(1,128)S(1)}, u32[]{:S(2)}, u32[]{:S(2)}) %all-to-all-start) | async-done | bytes 32800 | tf_op jit(solution)/shard_map/all_to_all | solution.py:386
  17.9 6.2 %predict.1 = (f32[48,128]{1,0:T(8,128)S(1)}, f32[16,128]{1,0:T(8,128)S(1)}) custom-call(f32[32,256]{1,0:T(8,128)S(1)} %bitcast.10, bf16[8,2,512,512]{3,2,1,0:T(8,128)(2,1)} %refs_1_.3), custom_call_target="tpu_custom_call" | custom-call | tf_op jit(solution)/shard_map/predict/pallas_call | solution.py:401
  24.1 0.8 pad_maximum_fusion.2
  24.9 3.7 %all-to-all-start.1 = ((f32[16,49,128]{2,1,0:T(8,128)}), f32[16,49,128]{2,1,0:T(8,128)S(1)}, u32[]{:S(2)}, u32[]{:S(2)}) async-start(f32[16,49,128]{2,1,0:T(8,128)} %pad_maximum_fusion.2), calls=%async_computation.1 | async-start | bytes 917504 | tf_op jit(solution)/shard_map/all_to_all | solution.py:418
  28.7 0.0 copy-start
  28.7 0.0 copy-start.1
  28.7 4.3 %negate_convert_fusion = (bf16[512,512]{1,0:T(8,128)(2,1)S(1)}, bf16[512,512]{1,0:T(8,128)(2,1)S(1)}) fusion(), kind=kLoop, calls=%fused_computation.7 | loop fusion | flops 4456448 | bytes 1048576 | tf_op jit(solution)/shard_map/convert.1
  33.1 0.1 pad_maximum_fusion.turn_v
  33.2 9.6 %all-to-all-done.1.near = f32[16,49,128]{2,1,0:T(8,128)S(1)} async-done(((f32[16,49,128]{2,1,0:T(8,128)}), f32[16,49,128]{2,1,0:T(8,128)S(1)}, u32[]{:S(2)}, u32[]{:S(2)}) %all-to-all-start.1) | async-done | bytes 401440 | tf_op jit(solution)/shard_map/all_to_all | solution.py:418
  42.8 0.0 collective-permute-start
  42.8 0.2 copy.11.twist
  43.0 1.6 %collective-permute-done.far = f32[16,49,128]{2,1,0:T(8,128)S(1)} collective-permute-done((f32[16,49,128]{2,1,0:T(8,128)S(1)}, f32[16,49,128]{2,1,0:T(8,128)S(1)}, u32[]{:S(2)}, u32[]{:S(2)}) %collective-permute-start) | collective-permute-done | bytes 401440 | tf_op jit(solution)/shard_map/ppermute | solution.py:426
  44.6 0.0 copy-done
  44.6 0.0 copy-done.1
  44.6 49.0 %image.1 = (f32[256,8192]{1,0:T(8,128)}, f32[2,512]{1,0:T(2,128)}) custom-call(s32[1]{0:T(128)} %bitcast.core, f32[16,49,128]{2,1,0:T(8,128)S(1)} %all-to-all-done.1.near, f32[16,49,128]{2,1,0:T(8,128)S(1)} %collective-permute-done.far, s32[1,512]{1,0:T(1,128)S(1)} %bitcast.13, s32[1,512]{1,0:T(1,128)S(1)} %copy-done.1, bf16[512,512]{1,0:T(8,128)(2,1)S(1)} %bitcast.9, ...), custom_call_target="tpu_custom_call" | custom-call | tf_op jit(solution)/shard_map/image/pallas_call | solution.py:430
  (6 shorter events, 0.1 us)
Async XLA Ops:
  3.3 14.6 %all-to-all-start = ((f32[32,1,256]{2,1,0:T(1,128)}), f32[32,1,256]{2,1,0:T(1,128)S(1)}, u32[]{:S(2)}, u32[]{:S(2)}) async-start(f32[32,1,256]{2,1,0:T(1,128)} %get-tuple-element.13), calls=%async_computation | async-start | bytes 65536 | tf_op jit(solution)/shard_map/all_to_all | solution.py:386
  24.9 17.8 %all-to-all-start.1 = ((f32[16,49,128]{2,1,0:T(8,128)}), f32[16,49,128]{2,1,0:T(8,128)S(1)}, u32[]{:S(2)}, u32[]{:S(2)}) async-start(f32[16,49,128]{2,1,0:T(8,128)} %pad_maximum_fusion.2), calls=%async_computation.1 | async-start | bytes 917504 | tf_op jit(solution)/shard_map/all_to_all | solution.py:418
  28.7 15.9 %copy-start = (s32[512,1]{0,1:T(1,128)S(1)}, s32[512,1]{0,1:T(1,128)}, u32[]{:S(2)}) copy-start(s32[512,1]{0,1:T(1,128)} %param.13) | copy-start | bytes 6148
  28.7 15.9 %copy-start.1 = (s32[1,512]{1,0:T(1,128)S(1)}, s32[1,512]{1,0:T(1,128)}, u32[]{:S(2)}) copy-start(s32[1,512]{1,0:T(1,128)} %get-tuple-element.19.rank) | copy-start | bytes 6148
  42.8 1.8 %collective-permute-start = (f32[16,49,128]{2,1,0:T(8,128)S(1)}, f32[16,49,128]{2,1,0:T(8,128)S(1)}, u32[]{:S(2)}, u32[]{:S(2)}) collective-permute-start(f32[16,49,128]{2,1,0:T(8,128)S(1)} %all-to-all-done.1.near), channel_id=1, source_target_pairs={{0,1},{1,0},{2,3},{3,2},{4,5},{5,4},{6,7},{7,6},{8,9},{9,8},{10,11... | collective-permute-start | bytes 1204232 | tf_op jit(solution)/shard_map/ppermute | solution.py:426

commit v9 on v8

--- a/solution.py
+++ b/solution.py
@@ -18,6 +18,7 @@
 SENT = 6
 CELLS = 16
 CHUNK = 256
+PARTS = 4
 
 AXES = ("blen", "chip", "core")
 CORES = 2
@@ -105,12 +106,10 @@
     def _():
         turned = recv[...].T
         span = FIELDS * per_dev
-        for k in range(MOST):
-            some = turned[k * span : (k + 1) * span, :]
-            for t in range(per_dev):
-                for f in range(FIELDS):
-                    at = f * per_dev + t
-                    fields[t, f : f + 1, k * devices : (k + 1) * devices] = some[at : at + 1, :]
+        lined = [turned[k * span : (k + 1) * span, :] for k in range(MOST)]
+        lined = jnp.concatenate(lined, axis=1)
+        for f in range(FIELDS):
+            fields[:, f, :] = lined[f * per_dev : (f + 1) * per_dev, :]
 
     for i in range(group):
         l = step * group + i
@@ -335,24 +334,32 @@
 
     lax.fori_loop(0, side // 16, stripe, 0)
 
-    for n0 in range(NT):
-        x = lax.dot_general(turn_v[...], turned[n0], NN_DIMS, preferred_element_type=f32)
-        for h in range(rows // width):
-            flips[h][pl.ds(n0, side, stride=NT), :] = x[:, h * width : (h + 1) * width]
-
     pieces = sems.shape[0]
     wide = NPIX // pieces
     copies = []
-    for i in range(pieces):
-        for h in range(rows // width):
-            stage[h * width : (h + 1) * width, i * wide : (i + 1) * wide] = (
-                flips[h][i * wide : (i + 1) * wide, :].T
+    part = side // PARTS
+    for b in range(PARTS):
+        for n0 in range(NT):
+            x = lax.dot_general(
+                turn_v[b * part : (b + 1) * part, :],
+                turned[n0],
+                NN_DIMS,
+                preferred_element_type=f32,
             )
-        copy = pltpu.make_async_copy(
-            stage.at[:, pl.ds(i * wide, wide)], out.at[:, pl.ds(i * wide, wide)], sems.at[i]
-        )
-        copy.start()
-        copies.append(copy)
+            for h in range(rows // width):
+                flips[h][pl.ds(b * part * NT + n0, part, stride=NT), :] = (
+                    x[:, h * width : (h + 1) * width]
+                )
+        for i in range(b * pieces // PARTS, (b + 1) * pieces // PARTS):
+            for h in range(rows // width):
+                stage[h * width : (h + 1) * width, i * wide : (i + 1) * wide] = (
+                    flips[h][i * wide : (i + 1) * wide, :].T
+                )
+            copy = pltpu.make_async_copy(
+                stage.at[:, pl.ds(i * wide, wide)], out.at[:, pl.ds(i * wide, wide)], sems.at[i]
+            )
+            copy.start()
+            copies.append(copy)
     for copy in copies:
         copy.wait()
 
@@ -397,7 +404,7 @@
     twist = jnp.stack(cos_sin(cells[:, None] * small[None, :], NPIX))
     recv, turn_u, rot, twist = lax.optimization_barrier((recv, turn_u, rot, twist))
 
-    group = min(2, per_dev)
+    group = min(4, per_dev)
     sent, back = call(
         lambda *refs: predict_body(*refs, per_dev=per_dev),
         grid=(per_dev // group,),

time: 93.4 us -> 91.8 us (0.983)
  Pallas kernels: 57.9 us -> 55.4 us
    pallas_call x1, Pallas kernels: 49 us -> 47.4 us  [on_device(): call(image_body, in_specs=[pl.BlockSpec(memory_space=pltpu.SMEM)] + [vmem...]
where the time goes in v9:
time: 91.8 us; the launch traced here: 91.3 us
  Pallas kernels  55.4 us (60%)
  waiting for transfers between devices  15.6 us (17%)
  starting transfers between devices  11 us (12%)
  other arithmetic  8.08 us (9%)
  between operations  0.95 us (1%)
    pallas_call x1, Pallas kernels, on_device(): call(image_body, in_specs=[pl.BlockSpec(memory_space=pltpu.SMEM)] + [vmem...  47.4 us
    all_to_all x1, waiting for transfers between devices, on_device(): lax.all_to_all(jnp.concatenate([sent, back[:, None, :]], axis=1), AXES[:2...  9.59 us
    all_to_all x1, starting transfers between devices, on_device(): recv = lax.all_to_all(packed, AXES, split_axis=0, concat_axis=0, tiled=True)  7.3 us
    another operation x2, other arithmetic  6.79 us
    pallas_call x1, Pallas kernels, on_device(): call(lambda *refs: predict_body(*refs, per_dev=per_dev), grid=(per_dev //...  5.33 us
    all_to_all x1, waiting for transfers between devices, on_device(): recv = lax.all_to_all(packed, AXES, split_axis=0, concat_axis=0, tiled=True)  4.37 us
    all_to_all x1, starting transfers between devices, on_device(): lax.all_to_all(jnp.concatenate([sent, back[:, None, :]], axis=1), AXES[:2...  3.74 us
    pallas_call x1, Pallas kernels, on_device(): call(lambda *refs: pack_body(*refs, devices=devices, per_dev=per_dev), ou...  2.68 us
  transfers between devices with their start and end apart: 3, of which 3 were waited for; matrix products, arithmetic and copies ran while one was open for 8% of the time, Pallas kernels for 0%

profile of v9, /device:TPU:0, one launch (start us, length us, event | category | flops | bytes accessed | tf_op | source)
XLA Modules:
  0.0 91.3 jit_solution(16743940822267902567)
XLA Ops:
  0.6 2.7 %pack.1 = (f32[32,1,256]{2,1,0:T(1,128)}, s32[1,512]{1,0:T(1,128)}) custom-call(s32[1,512]{1,0:T(1,128)} %bitcast.12, s32[2,512]{1,0:T(2,128)} %refs_1_.2, f32[2,512]{1,0:T(2,128)} %refs_2_.1, f32[2,512]{1,0:T(2,128)} %refs_3_.1, f32[1,512]{1,0:T(1,128)} %bitcast.14, s32[1,512]{1,0:T(1,128)} %bitcast.15), custom_call_target="tpu_custom_call" | custom-call | tf_op jit(solution)/shard_map/pack/pallas_call | solution.py:388
  3.3 7.3 %all-to-all-start = ((f32[32,1,256]{2,1,0:T(1,128)}), f32[32,1,256]{2,1,0:T(1,128)S(1)}, u32[]{:S(2)}, u32[]{:S(2)}) async-start(f32[32,1,256]{2,1,0:T(1,128)} %get-tuple-element.13), calls=%async_computation | async-start | bytes 65536 | tf_op jit(solution)/shard_map/all_to_all | solution.py:393
  10.6 0.1 fusion.28
  10.7 0.1 fusion.18
  10.9 2.4 %cosine_convert_fusion.1 = (bf16[16,1,16,512]{3,2,1,0:T(8,128)(2,1)S(1)}, bf16[16,1,16,512]{3,2,1,0:T(8,128)(2,1)S(1)}) fusion(s32[16,16]{1,0:T(8,128)S(1)} %add_add_fusion), kind=kLoop, calls=%fused_computation.20 | loop fusion | flops 2097152 | bytes 525312 | tf_op jit(solution)/shard_map/convert.2
  13.3 0.1 pad_maximum_fusion.1
  13.4 0.1 pad_maximum_fusion.5.rot
  13.5 4.4 %all-to-all-done = f32[32,1,256]{2,1,0:T(1,128)S(1)} async-done(((f32[32,1,256]{2,1,0:T(1,128)}), f32[32,1,256]{2,1,0:T(1,128)S(1)}, u32[]{:S(2)}, u32[]{:S(2)}) %all-to-all-start) | async-done | bytes 32800 | tf_op jit(solution)/shard_map/all_to_all | solution.py:393
  17.9 5.3 %predict.1 = (f32[48,128]{1,0:T(8,128)S(1)}, f32[16,128]{1,0:T(8,128)S(1)}) custom-call(f32[32,256]{1,0:T(8,128)S(1)} %bitcast.10, bf16[8,2,512,512]{3,2,1,0:T(8,128)(2,1)} %refs_1_.3), custom_call_target="tpu_custom_call" | custom-call | tf_op jit(solution)/shard_map/predict/pallas_call | solution.py:408
  23.2 0.8 pad_maximum_fusion.2
  24.0 3.7 %all-to-all-start.1 = ((f32[16,49,128]{2,1,0:T(8,128)}), f32[16,49,128]{2,1,0:T(8,128)S(1)}, u32[]{:S(2)}, u32[]{:S(2)}) async-start(f32[16,49,128]{2,1,0:T(8,128)} %pad_maximum_fusion.2), calls=%async_computation.1 | async-start | bytes 917504 | tf_op jit(solution)/shard_map/all_to_all | solution.py:425
  27.8 0.0 copy-start
  27.8 0.0 copy-start.1
  27.8 4.3 %negate_convert_fusion = (bf16[512,512]{1,0:T(8,128)(2,1)S(1)}, bf16[512,512]{1,0:T(8,128)(2,1)S(1)}) fusion(), kind=kLoop, calls=%fused_computation.7 | loop fusion | flops 4456448 | bytes 1048576 | tf_op jit(solution)/shard_map/convert.1
  32.2 0.1 pad_maximum_fusion.turn_v
  32.3 9.6 %all-to-all-done.1.near = f32[16,49,128]{2,1,0:T(8,128)S(1)} async-done(((f32[16,49,128]{2,1,0:T(8,128)}), f32[16,49,128]{2,1,0:T(8,128)S(1)}, u32[]{:S(2)}, u32[]{:S(2)}) %all-to-all-start.1) | async-done | bytes 401440 | tf_op jit(solution)/shard_map/all_to_all | solution.py:425
  41.9 0.0 collective-permute-start
  41.9 0.2 copy.11.twist
  42.1 1.6 %collective-permute-done.far = f32[16,49,128]{2,1,0:T(8,128)S(1)} collective-permute-done((f32[16,49,128]{2,1,0:T(8,128)S(1)}, f32[16,49,128]{2,1,0:T(8,128)S(1)}, u32[]{:S(2)}, u32[]{:S(2)}) %collective-permute-start) | collective-permute-done | bytes 401440 | tf_op jit(solution)/shard_map/ppermute | solution.py:433
  43.7 0.0 copy-done
  43.7 0.0 copy-done.1
  43.7 47.4 %image.1 = (f32[256,8192]{1,0:T(8,128)}, f32[2,512]{1,0:T(2,128)}) custom-call(s32[1]{0:T(128)} %bitcast.core, f32[16,49,128]{2,1,0:T(8,128)S(1)} %all-to-all-done.1.near, f32[16,49,128]{2,1,0:T(8,128)S(1)} %collective-permute-done.far, s32[1,512]{1,0:T(1,128)S(1)} %bitcast.13, s32[1,512]{1,0:T(1,128)S(1)} %copy-done.1, bf16[512,512]{1,0:T(8,128)(2,1)S(1)} %bitcast.9, ...), custom_call_target="tpu_custom_call" | custom-call | tf_op jit(solution)/shard_map/image/pallas_call | solution.py:437
  (6 shorter events, 0.1 us)
Async XLA Ops:
  3.3 14.6 %all-to-all-start = ((f32[32,1,256]{2,1,0:T(1,128)}), f32[32,1,256]{2,1,0:T(1,128)S(1)}, u32[]{:S(2)}, u32[]{:S(2)}) async-start(f32[32,1,256]{2,1,0:T(1,128)} %get-tuple-element.13), calls=%async_computation | async-start | bytes 65536 | tf_op jit(solution)/shard_map/all_to_all | solution.py:393
  24.0 17.8 %all-to-all-start.1 = ((f32[16,49,128]{2,1,0:T(8,128)}), f32[16,49,128]{2,1,0:T(8,128)S(1)}, u32[]{:S(2)}, u32[]{:S(2)}) async-start(f32[16,49,128]{2,1,0:T(8,128)} %pad_maximum_fusion.2), calls=%async_computation.1 | async-start | bytes 917504 | tf_op jit(solution)/shard_map/all_to_all | solution.py:425
  27.8 15.9 %copy-start = (s32[512,1]{0,1:T(1,128)S(1)}, s32[512,1]{0,1:T(1,128)}, u32[]{:S(2)}) copy-start(s32[512,1]{0,1:T(1,128)} %param.13) | copy-start | bytes 6148
  27.8 15.9 %copy-start.1 = (s32[1,512]{1,0:T(1,128)S(1)}, s32[1,512]{1,0:T(1,128)}, u32[]{:S(2)}) copy-start(s32[1,512]{1,0:T(1,128)} %get-tuple-element.19.rank) | copy-start | bytes 6148
  41.9 1.8 %collective-permute-start = (f32[16,49,128]{2,1,0:T(8,128)S(1)}, f32[16,49,128]{2,1,0:T(8,128)S(1)}, u32[]{:S(2)}, u32[]{:S(2)}) collective-permute-start(f32[16,49,128]{2,1,0:T(8,128)S(1)} %all-to-all-done.1.near), channel_id=1, source_target_pairs={{0,1},{1,0},{2,3},{3,2},{4,5},{5,4},{6,7},{7,6},{8,9},{9,8},{10,11... | collective-permute-start | bytes 1204232 | tf_op jit(solution)/shard_map/ppermute | solution.py:433

commit v10 on v9

--- a/solution.py
+++ b/solution.py
@@ -18,7 +18,7 @@
 SENT = 6
 CELLS = 16
 CHUNK = 256
-PARTS = 4
+PARTS = 8
 
 AXES = ("blen", "chip", "core")
 CORES = 2

time: 91.8 us -> 97.7 us (1.064)
  Pallas kernels: 55.4 us -> 61.5 us
    pallas_call x1, Pallas kernels: 47.4 us -> 53.5 us  [on_device(): call(image_body, in_specs=[pl.BlockSpec(memory_space=pltpu.SMEM)] + [vmem...]
where the time goes in v10:
time: 97.7 us; the launch traced here: 97.4 us
  Pallas kernels  61.5 us (63%)
  waiting for transfers between devices  15.6 us (16%)
  starting transfers between devices  11 us (11%)
  other arithmetic  8.08 us (8%)
    pallas_call x1, Pallas kernels, on_device(): call(image_body, in_specs=[pl.BlockSpec(memory_space=pltpu.SMEM)] + [vmem...  53.5 us
    all_to_all x1, waiting for transfers between devices, on_device(): lax.all_to_all(jnp.concatenate([sent, back[:, None, :]], axis=1), AXES[:2...  9.59 us
    all_to_all x1, starting transfers between devices, on_device(): recv = lax.all_to_all(packed, AXES, split_axis=0, concat_axis=0, tiled=True)  7.3 us
    another operation x2, other arithmetic  6.79 us
    pallas_call x1, Pallas kernels, on_device(): call(lambda *refs: predict_body(*refs, per_dev=per_dev), grid=(per_dev //...  5.33 us
    all_to_all x1, waiting for transfers between devices, on_device(): recv = lax.all_to_all(packed, AXES, split_axis=0, concat_axis=0, tiled=True)  4.37 us
    all_to_all x1, starting transfers between devices, on_device(): lax.all_to_all(jnp.concatenate([sent, back[:, None, :]], axis=1), AXES[:2...  3.74 us
    pallas_call x1, Pallas kernels, on_device(): call(lambda *refs: pack_body(*refs, devices=devices, per_dev=per_dev), ou...  2.68 us
  transfers between devices with their start and end apart: 3, of which 3 were waited for; matrix products, arithmetic and copies ran while one was open for 8% of the time, Pallas kernels for 0%

profile of v10, /device:TPU:0, one launch (start us, length us, event | category | flops | bytes accessed | tf_op | source)
XLA Modules:
  0.0 97.4 jit_solution(6695484052746707267)
XLA Ops:
  0.6 2.7 %pack.1 = (f32[32,1,256]{2,1,0:T(1,128)}, s32[1,512]{1,0:T(1,128)}) custom-call(s32[1,512]{1,0:T(1,128)} %bitcast.12, s32[2,512]{1,0:T(2,128)} %refs_1_.2, f32[2,512]{1,0:T(2,128)} %refs_2_.1, f32[2,512]{1,0:T(2,128)} %refs_3_.1, f32[1,512]{1,0:T(1,128)} %bitcast.14, s32[1,512]{1,0:T(1,128)} %bitcast.15), custom_call_target="tpu_custom_call" | custom-call | tf_op jit(solution)/shard_map/pack/pallas_call | solution.py:388
  3.3 7.3 %all-to-all-start = ((f32[32,1,256]{2,1,0:T(1,128)}), f32[32,1,256]{2,1,0:T(1,128)S(1)}, u32[]{:S(2)}, u32[]{:S(2)}) async-start(f32[32,1,256]{2,1,0:T(1,128)} %get-tuple-element.13), calls=%async_computation | async-start | bytes 65536 | tf_op jit(solution)/shard_map/all_to_all | solution.py:393
  10.6 0.1 fusion.28
  10.7 0.1 fusion.18
  10.9 2.4 %cosine_convert_fusion.1 = (bf16[16,1,16,512]{3,2,1,0:T(8,128)(2,1)S(1)}, bf16[16,1,16,512]{3,2,1,0:T(8,128)(2,1)S(1)}) fusion(s32[16,16]{1,0:T(8,128)S(1)} %add_add_fusion), kind=kLoop, calls=%fused_computation.20 | loop fusion | flops 2097152 | bytes 525312 | tf_op jit(solution)/shard_map/convert.2
  13.3 0.1 pad_maximum_fusion.1
  13.4 0.1 pad_maximum_fusion.5.rot
  13.5 4.4 %all-to-all-done = f32[32,1,256]{2,1,0:T(1,128)S(1)} async-done(((f32[32,1,256]{2,1,0:T(1,128)}), f32[32,1,256]{2,1,0:T(1,128)S(1)}, u32[]{:S(2)}, u32[]{:S(2)}) %all-to-all-start) | async-done | bytes 32800 | tf_op jit(solution)/shard_map/all_to_all | solution.py:393
  17.9 5.3 %predict.1 = (f32[48,128]{1,0:T(8,128)S(1)}, f32[16,128]{1,0:T(8,128)S(1)}) custom-call(f32[32,256]{1,0:T(8,128)S(1)} %bitcast.10, bf16[8,2,512,512]{3,2,1,0:T(8,128)(2,1)} %refs_1_.3), custom_call_target="tpu_custom_call" | custom-call | tf_op jit(solution)/shard_map/predict/pallas_call | solution.py:408
  23.2 0.8 pad_maximum_fusion.2
  24.0 3.7 %all-to-all-start.1 = ((f32[16,49,128]{2,1,0:T(8,128)}), f32[16,49,128]{2,1,0:T(8,128)S(1)}, u32[]{:S(2)}, u32[]{:S(2)}) async-start(f32[16,49,128]{2,1,0:T(8,128)} %pad_maximum_fusion.2), calls=%async_computation.1 | async-start | bytes 917504 | tf_op jit(solution)/shard_map/all_to_all | solution.py:425
  27.8 0.0 copy-start
  27.8 0.0 copy-start.1
  27.8 4.3 %negate_convert_fusion = (bf16[512,512]{1,0:T(8,128)(2,1)S(1)}, bf16[512,512]{1,0:T(8,128)(2,1)S(1)}) fusion(), kind=kLoop, calls=%fused_computation.7 | loop fusion | flops 4456448 | bytes 1048576 | tf_op jit(solution)/shard_map/convert.1
  32.2 0.1 pad_maximum_fusion.turn_v
  32.3 9.6 %all-to-all-done.1.near = f32[16,49,128]{2,1,0:T(8,128)S(1)} async-done(((f32[16,49,128]{2,1,0:T(8,128)}), f32[16,49,128]{2,1,0:T(8,128)S(1)}, u32[]{:S(2)}, u32[]{:S(2)}) %all-to-all-start.1) | async-done | bytes 401440 | tf_op jit(solution)/shard_map/all_to_all | solution.py:425
  41.9 0.0 collective-permute-start
  41.9 0.2 copy.11.twist
  42.1 1.6 %collective-permute-done.far = f32[16,49,128]{2,1,0:T(8,128)S(1)} collective-permute-done((f32[16,49,128]{2,1,0:T(8,128)S(1)}, f32[16,49,128]{2,1,0:T(8,128)S(1)}, u32[]{:S(2)}, u32[]{:S(2)}) %collective-permute-start) | collective-permute-done | bytes 401440 | tf_op jit(solution)/shard_map/ppermute | solution.py:433
  43.7 0.0 copy-done
  43.7 0.0 copy-done.1
  43.7 53.5 %image.1 = (f32[256,8192]{1,0:T(8,128)}, f32[2,512]{1,0:T(2,128)}) custom-call(s32[1]{0:T(128)} %bitcast.core, f32[16,49,128]{2,1,0:T(8,128)S(1)} %all-to-all-done.1.near, f32[16,49,128]{2,1,0:T(8,128)S(1)} %collective-permute-done.far, s32[1,512]{1,0:T(1,128)S(1)} %bitcast.13, s32[1,512]{1,0:T(1,128)S(1)} %copy-done.1, bf16[512,512]{1,0:T(8,128)(2,1)S(1)} %bitcast.9, ...), custom_call_target="tpu_custom_call" | custom-call | tf_op jit(solution)/shard_map/image/pallas_call | solution.py:437
  (6 shorter events, 0.1 us)
Async XLA Ops:
  3.3 14.6 %all-to-all-start = ((f32[32,1,256]{2,1,0:T(1,128)}), f32[32,1,256]{2,1,0:T(1,128)S(1)}, u32[]{:S(2)}, u32[]{:S(2)}) async-start(f32[32,1,256]{2,1,0:T(1,128)} %get-tuple-element.13), calls=%async_computation | async-start | bytes 65536 | tf_op jit(solution)/shard_map/all_to_all | solution.py:393
  24.0 17.8 %all-to-all-start.1 = ((f32[16,49,128]{2,1,0:T(8,128)}), f32[16,49,128]{2,1,0:T(8,128)S(1)}, u32[]{:S(2)}, u32[]{:S(2)}) async-start(f32[16,49,128]{2,1,0:T(8,128)} %pad_maximum_fusion.2), calls=%async_computation.1 | async-start | bytes 917504 | tf_op jit(solution)/shard_map/all_to_all | solution.py:425
  27.8 15.9 %copy-start = (s32[512,1]{0,1:T(1,128)S(1)}, s32[512,1]{0,1:T(1,128)}, u32[]{:S(2)}) copy-start(s32[512,1]{0,1:T(1,128)} %param.13) | copy-start | bytes 6148
  27.8 15.9 %copy-start.1 = (s32[1,512]{1,0:T(1,128)S(1)}, s32[1,512]{1,0:T(1,128)}, u32[]{:S(2)}) copy-start(s32[1,512]{1,0:T(1,128)} %get-tuple-element.19.rank) | copy-start | bytes 6148
  41.9 1.8 %collective-permute-start = (f32[16,49,128]{2,1,0:T(8,128)S(1)}, f32[16,49,128]{2,1,0:T(8,128)S(1)}, u32[]{:S(2)}, u32[]{:S(2)}) collective-permute-start(f32[16,49,128]{2,1,0:T(8,128)S(1)} %all-to-all-done.1.near), channel_id=1, source_target_pairs={{0,1},{1,0},{2,3},{3,2},{4,5},{5,4},{6,7},{7,6},{8,9},{9,8},{10,11... | collective-permute-start | bytes 1204232 | tf_op jit(solution)/shard_map/ppermute | solution.py:433
